TPU v7x, 128 devices: a whole 4x4x4 slice. The times are simulated.
128 devices in a mesh: row: 8 (over z, core), col: 16 (over x, y).
Axes of the slice: x: 4, y: 4, z: 4, core: 2. Of those that a mesh axis runs over, the one named last changes fastest.
Arguments:
- left_edge: bfloat16 [16, 3072, 3072], P('row', 'col'), may hold values from -6 to 6
- right_edge: bfloat16 [16, 3072, 3072], P('row', 'col'), may hold values from -0.109375 to 0.109375
- projector: bfloat16 [16, 3072, 64], P('row'), may hold values from -0.109375 to 0.109375
- sector_size: int32 [16], P('row'), may hold values from 1 to 3072, 30720 in all
Outputs:
- enlarged: float32 [16, 3072, 3072], P('row', 'col')
- new_corner: float32 [16, 64, 64], P('row')
All inputs are finite; a program needn't handle non-finite values. No bound on the sum of `sector_size` on one device may be relied on, other than what follows from the above.
Results may differ from a plain program's by a relative error of at most 0.0003.
Values may be sent and summed in bfloat16 or wider, within the bound.
No kernel may reach another device: no remote copies, remote signals or barrier semaphores. Data moves between devices by JAX's collectives and lax.ppermute only.
A program may use at most 128 MiB of HBM per device.

v0:
```python
import jax
import jax.numpy as jnp
from jax import lax
from jax.sharding import PartitionSpec as P


def body(left_edge, right_edge, projector, sector_size):
    count = left_edge.shape[0]
    rows = left_edge.shape[1]
    width = projector.shape[1]
    kept = projector.shape[2]
    first_row = lax.axis_index("col") * rows
    states = jnp.arange(width, dtype=jnp.int32)
    live = (states[None, :] < sector_size[:, None]).astype(jnp.bfloat16)
    masked = projector * live[:, :, None]
    own_masked = lax.dynamic_slice_in_dim(masked, first_row, rows, 1).astype(jnp.float32)
    enlarged = jnp.einsum(
        "sik,skj->sij",
        left_edge,
        lax.all_gather(right_edge, "col", axis=1, tiled=True),
        preferred_element_type=jnp.float32,
    )
    inner = jnp.einsum(
        "sij,sjq->siq", enlarged, masked.astype(jnp.float32), precision=lax.Precision.HIGHEST
    )
    parts = jnp.einsum("sip,siq->spq", own_masked, inner, precision=lax.Precision.HIGHEST)
    entries = lax.axis_size("row") * count * kept * kept
    corner = lax.psum(parts, "col")
    total = lax.psum(jnp.sum(corner * corner), "row")
    return (enlarged, corner * lax.rsqrt(total / entries + 1e-06))


def solution(mesh):
    placed = (P("row", "col", None), P("row", "col", None), P("row", None, None), P("row"))
    return jax.shard_map(
        body,
        mesh=mesh,
        in_specs=placed,
        out_specs=(P("row", "col", None), P("row", None, None)),
        check_vma=False,
    )
```

profile of v0, /device:TPU:0, one launch (start us, length us, event | category | flops | bytes accessed | tf_op | source)
XLA Modules:
  0.0 347.5 jit_solution(8765672397625688852)
XLA Ops:
  7.2 0.0 copy-start
  7.2 0.0 all-gather.2.cloned.1.call-start
  7.2 0.7 all-gather.2.cloned.1.call-update
  7.9 0.7 compare_convert_fusion
  8.7 1.2 broadcast_multiply_fusion
  9.9 221.2 %all-gather.2.cloned.1.call-done = bf16[2,3072,3072]{2,1,0:T(8,128)(2,1)} async-done(((bf16[2,192,3072]{2,1,0:T(8,128)(2,1)}), bf16[2,3072,3072]{2,1,0:T(8,128)(2,1)}) %all-gather.2.cloned.1.call-update) | async-done | bytes 37748752 | tf_op jit(solution)/shard_map/all_gather | solution.py:20
  231.0 0.0 copy-done
  231.0 16.9 %fusion.3 = f32[2,192,3072]{2,1,0:T(8,128)} fusion(bf16[2,192,3072]{2,1,0:T(8,128)(2,1)S(1)} %copy-done, bf16[2,3072,3072]{2,1,0:T(8,128)(2,1)} %all-gather.2.cloned.1.call-done), kind=kOutput, calls=%fused_computation.7 | convolution fusion | flops 7247757312 | bytes 44826624 | tf_op jit(solution)/shard_map/sik,skj->sij/dot_general | solution.py:17
  247.9 5.0 %fusion.4 = f32[2,192,64]{1,2,0:T(8,128)S(1)} fusion(f32[2,192,3072]{2,1,0:T(8,128)} %fusion.3, bf16[2,3072,64]{1,2,0:T(8,128)(2,1)S(1)} %broadcast_multiply_fusion), kind=kOutput, calls=%fused_computation.8 | convolution fusion | flops 905969664 | bytes 5603328 | tf_op jit(solution)/shard_map/sij,sjq->siq/dot_general | solution.py:23
  252.9 0.3 fusion
  253.2 72.5 %psum.14 = f32[2,64,64]{2,1,0:T(8,128)S(1)} all-reduce(f32[2,64,64]{2,1,0:T(8,128)S(1)} %fusion), channel_id=1, replica_groups=mesh['row'=8,'col'=16] {'col'}, use_global_device_ids=true, to_apply=%region_0.0 | all-reduce | flops 8192 | bytes 65536 | tf_op jit(solution)/shard_map/psum | solution.py:28
  325.6 0.6 multiply_reduce_fusion
  326.3 13.0 %psum.15 = f32[]{:T(128)} all-reduce(f32[]{:T(128)} %multiply_reduce_fusion), channel_id=1, replica_groups=mesh['row'=8,'col'=16] {'row'}, use_global_device_ids=true, to_apply=%region_2.0 | all-reduce | flops 1 | bytes 8 | tf_op jit(solution)/shard_map/psum | solution.py:29
  340.0 0.6 broadcast_multiply_fusion.1
Async XLA Ops:
  7.2 223.9 %copy-start = (bf16[2,192,3072]{2,1,0:T(8,128)(2,1)S(1)}, bf16[2,192,3072]{2,1,0:T(8,128)(2,1)}, u32[]{:S(2)}) copy-start(bf16[2,192,3072]{2,1,0:T(8,128)(2,1)} %param.4) | copy-start | bytes 7077892
  7.2 223.8 %all-gather.2.cloned.1.call-start = ((), (), s32[]{:S(2)}) async-start(), calls=%async_computation | async-start | bytes 40108032 | tf_op jit(solution)/shard_map/all_gather | solution.py:20
Sparse Core Ops, SparseCore 0:
  10.2 220.8 all-gather.1
where the time goes:
time: 349 us; the launch traced here: 347 us
  waiting for transfers between devices  222 us (64%)
  blocking collectives  85.5 us (24%)
  matrix products  22.1 us (6%)
  between operations  14.7 us (4%)
    all_gather x1, waiting for transfers between devices, body(): lax.all_gather(right_edge, 'col', axis=1, tiled=True)  221 us
    psum x1, blocking collectives, body(): corner = lax.psum(parts, 'col')  72.5 us
    dot_general x1, matrix products, body(): jnp.einsum('sik,skj->sij', left_edge, lax.all_gather(right_edge, 'col', a...  16.9 us
    psum x1, blocking collectives, body(): total = lax.psum(jnp.sum(corner * corner), 'row')  13 us
  transfers between devices with their start and end apart: 1, of which 1 were waited for; matrix products, arithmetic and copies ran while one was open for 1% of the time, Pallas kernels for 0%

commit v1 on v0

v1 whole, which is shorter than its diff:
```python
import jax
import jax.numpy as jnp
from jax import lax
from jax.experimental import pallas as pl
from jax.experimental.pallas import tpu as pltpu
from jax.sharding import PartitionSpec as P

SIDE = 4
CHUNKS = 3


def product(offsets, left, own, below, above, low, high, widths):
    rows, depth = left.shape[1:]
    full = own.shape[2]
    pieces = [(i, p) for i, ref in enumerate((own, below, above, low, high)) for p in range(ref.shape[0])]

    def kernel(off, l, r0, r1, r2, r3, r4, *rest):
        outs, (scratch, sems) = rest[:-2], rest[-2:]
        refs = (r0, r1, r2, r3, r4)
        copies = []
        for n, (i, p) in enumerate(pieces):
            at = pl.multiple_of(off[n], 64)
            copies.append(pltpu.make_async_copy(refs[i].at[p], scratch.at[pl.ds(at, rows)], sems.at[n]))
        for copy in copies:
            copy.start()
        for copy in copies:
            copy.wait()
        lhs = l[...].reshape(SIDE * rows, depth)
        start = 0
        for out, width in zip(outs, widths):
            got = jnp.dot(lhs, scratch[:, start:start + width], preferred_element_type=jnp.float32)
            out[...] = got.reshape(SIDE, rows, width)
            start += width

    anywhere = pl.BlockSpec(memory_space=pl.ANY)
    inside = pl.BlockSpec(memory_space=pltpu.VMEM)
    return pl.pallas_call(
        kernel,
        in_specs=[pl.BlockSpec(memory_space=pltpu.SMEM), inside] + [anywhere] * 5,
        out_specs=[inside] * len(widths),
        out_shape=[jax.ShapeDtypeStruct((SIDE, rows, width), jnp.float32) for width in widths],
        scratch_shapes=[pltpu.VMEM((depth, full), jnp.bfloat16), pltpu.SemaphoreType.DMA((len(pieces),))],
        compiler_params=pltpu.CompilerParams(vmem_limit_bytes=40 << 20),
    )(offsets, left, own, below, above, low, high)


def solution(mesh):
    n_row, n_col = mesh.shape["row"], mesh.shape["col"]

    def pairs(move):
        found = []
        for row in range(n_row):
            for col in range(n_col):
                cx, cy = col // SIDE, col % SIDE
                g, h = (cy, cx) if row % 2 else (cx, cy)
                to, g, h = move(row, g, h)
                cx, cy = (h, g) if row % 2 else (g, h)
                if to != row:
                    cx, cy = col // SIDE, col % SIDE
                found.append((row * n_col + col, to * n_col + cx * SIDE + cy))
        return found

    along_g = {p: pairs(lambda row, g, h, p=p: (row, g ^ p, h)) for p in (1, 2, 3)}
    along_h = {p: pairs(lambda row, g, h, p=p: (row, g, h ^ p)) for p in (1, 2)}
    up = pairs(lambda row, g, h: (row, g, (h + 1) % SIDE))
    down = pairs(lambda row, g, h: (row, g, (h - 1) % SIDE))
    across = {p: pairs(lambda row, g, h, p=p: (row ^ p, g, h)) for p in (1, 2, 4)}

    def send(value, table):
        return lax.ppermute(value, ("row", "col"), table)

    def body(left_edge, right_edge, projector, sector_size):
        count, rows, depth = left_edge.shape
        kept = projector.shape[2]
        half = depth // 2
        width = half // CHUNKS
        odd = lax.axis_index("row") % 2
        col = lax.axis_index("col")
        cx, cy = col // SIDE, col % SIDE
        g = jnp.where(odd == 1, cy, cx)
        h = jnp.where(odd == 1, cx, cy)
        owner = lambda gg, hh: jnp.where(odd == 1, hh * SIDE + gg, gg * SIDE + hh)

        states = jnp.arange(depth, dtype=jnp.int32)
        live = (states[None, :] < sector_size[:, None]).astype(jnp.bfloat16)
        masked = projector * live[:, :, None]

        seen = jnp.einsum("skj,sjq->skq", right_edge, masked, preferred_element_type=jnp.float32)
        top = lax.reduce_precision(seen, exponent_bits=8, mantissa_bits=7)
        shadow = jnp.concatenate([top, seen - top], axis=2).astype(jnp.bfloat16)

        sector = g // 2
        mine = lax.dynamic_index_in_dim(left_edge, sector, 0, keepdims=False)
        other = lax.dynamic_index_in_dim(left_edge, 1 - sector, 0, keepdims=False)

        def part(p, c):
            to = g ^ p
            start = (to % 2) * half + c * width
            got = lax.dynamic_slice(right_edge, (to // 2, 0, start), (1, rows, width))[0]
            if c == 0:
                got = jnp.concatenate([got, lax.dynamic_index_in_dim(shadow, to // 2, 0, keepdims=False)], axis=1)
            return got

        near = send(other, along_g[3])
        paired = send(mine, along_g[1])
        far = send(near, along_g[1])
        left = jnp.stack([mine, paired, far, near])

        hs = [h, (h - 1) % SIDE, (h + 1) % SIDE, (h + 2) % SIDE]
        offsets = jnp.stack([owner(g ^ p, hh) * rows for hh in hs for p in range(SIDE)]).astype(jnp.int32)

        enlarged = jnp.zeros((count, rows, depth), jnp.float32)
        inner = None
        for c in range(CHUNKS):
            own = jnp.stack([part(0, c)] + [send(part(p, c), along_g[p]) for p in (1, 2, 3)])
            below = send(own, up)
            above = send(own, down)
            low = send(below[:2], up)
            high = send(above[2:], down)
            widths = (width,) if c else (width, 2 * kept)
            out = product(offsets, left, own, below, above, low, high, widths)
            if c == 0:
                inner = out[1]
            for p in range(SIDE):
                block = out[0][p]
                if p:
                    block = send(block, along_g[p])
                start = ((g ^ p) % 2) * half + c * width
                enlarged = lax.dynamic_update_slice(enlarged, block[None], ((g ^ p) // 2, 0, start))

        inner = inner[:, :, :kept] + inner[:, :, kept:]
        ours = lax.dynamic_index_in_dim(masked, sector, 0, keepdims=False)
        terms = []
        for p in range(SIDE):
            chosen = lax.dynamic_slice_in_dim(ours, owner(g ^ p, h) * rows, rows, 0).astype(jnp.float32)
            terms.append(jnp.einsum("ip,iq->pq", chosen, inner[p], precision=lax.Precision.HIGHEST))
        corner = (terms[0] + terms[1]) + (terms[2] + terms[3])
        for p in (1, 2):
            corner = corner + send(corner, along_h[p])
        beside = send(corner, along_g[2])
        corner = jnp.where(sector == 0, jnp.stack([corner, beside]), jnp.stack([beside, corner]))
        total = jnp.broadcast_to(jnp.sum(corner * corner), (8, 128))
        for p in (1, 2, 4):
            total = total + send(total, across[p])
        entries = n_row * count * kept * kept
        return enlarged, corner * lax.rsqrt(total[0, 0] / entries + 1e-06)

    placed = (P("row", "col", None), P("row", "col", None), P("row", None, None), P("row"))
    return jax.shard_map(
        body,
        mesh=mesh,
        in_specs=placed,
        out_specs=(P("row", "col", None), P("row", None, None)),
        check_vma=False,
    )
```

time: 349 us -> 211 us (0.60)
  waiting for transfers between devices: 222 us -> 73.5 us
  blocking collectives: 85.5 us -> 0 us
  starting transfers between devices: 0.04 us -> 66.6 us
  local copies, waits for them, and re-layouts: 0.01 us -> 28.8 us
  Pallas kernels: 0 us -> 23.6 us
  matrix products: 22.1 us -> 5.15 us
  between operations: 14.7 us -> 1.91 us
  other arithmetic: 3.19 us -> 10.2 us
    all_gather x1 -> x0, waiting for transfers between devices: 221 us -> none  [body(): lax.all_gather(right_edge, 'col', axis=1, tiled=True)]
    psum x2 -> x0, blocking collectives: 85.5 us -> none  [the longest x1 72.5 us: body(): corner = lax.psum(parts, 'col')]
    ppermute x0 -> x39, waiting for transfers between devices: none -> 73.5 us  [send(): return lax.ppermute(value, ('row', 'col'), table)]
    ppermute x0 -> x39, starting transfers between devices: none -> 66.6 us  [send(): return lax.ppermute(value, ('row', 'col'), table)]
    pallas_call x0 -> x3, Pallas kernels: none -> 23.6 us  [product(): pl.pallas_call(kernel, in_specs=[pl.BlockSpec(memory_space=pltpu.SMEM), i...]
    dot_general x3 -> x5, matrix products: 22.1 us -> 5.15 us  [the longest x4 4.27 us: body(): jnp.einsum('ip,iq->pq', chosen, inner[p], precision=lax.Precision.HIGHEST)]
    slice x0 -> x7, local copies, waits for them, and re-layouts: none -> 7.87 us  [the longest x3 3.68 us: body(): high = send(above[2:], down)]
    unnamed x2 -> x36, local copies, waits for them, and re-layouts: 0.01 us -> 6.33 us
  transfers between devices with their start and end apart: 1 -> 39, of which waited for: 1 -> 15; matrix products, arithmetic and copies ran while one was open for 1% -> 16% of each run, Pallas kernels for 0% -> 11%
where the time goes in v1:
time: 211 us; the launch traced here: 210 us
  waiting for transfers between devices  73.5 us (35%)
  starting transfers between devices  66.6 us (32%)
  local copies, waits for them, and re-layouts  28.8 us (14%)
  Pallas kernels  23.6 us (11%)
  other arithmetic  10.2 us (5%)
  matrix products  5.15 us (2%)
    ppermute x39, waiting for transfers between devices, send(): return lax.ppermute(value, ('row', 'col'), table)  73.5 us
    ppermute x39, starting transfers between devices, send(): return lax.ppermute(value, ('row', 'col'), table)  66.6 us
    pallas_call x3, Pallas kernels, product(): pl.pallas_call(kernel, in_specs=[pl.BlockSpec(memory_space=pltpu.SMEM), i...  23.6 us
    unnamed x36, local copies, waits for them, and re-layouts  6.33 us
    dynamic_update_slice x9, local copies, waits for them, and re-layouts, body(): lax.dynamic_update_slice(enlarged, block[None], ((g ^ p) // 2, 0, start))  5.74 us
    dot_general x4, matrix products, body(): jnp.einsum('ip,iq->pq', chosen, inner[p], precision=lax.Precision.HIGHEST)  4.27 us
  transfers between devices with their start and end apart: 39, of which 15 were waited for; matrix products, arithmetic and copies ran while one was open for 16% of the time, Pallas kernels for 11%

profile of v1, /device:TPU:0, one launch (start us, length us, event | category | flops | bytes accessed | tf_op | source)
XLA Modules:
  0.0 209.8 jit_solution(205670825895935751)
XLA Ops:
  0.7 3.3 %constant_dynamic-slice_fusion.2 = (bf16[1,192,3072]{2,1,0:T(8,128)(2,1)}, bf16[192,3072]{1,0:T(8,128)(2,1)}) fusion(bf16[2,192,3072]{2,1,0:T(8,128)(2,1)} %param.4, s32[]{:T(128)S(6)} %select_n.325, s32[]{:T(128)S(6)} %select_n.326), kind=kLoop, calls=%fused_computation.85 | loop fusion | bytes 4718600 | tf_op jit(solution)/shard_map/jit(dynamic_index_in_dim)/dynamic_slice | solution.py:93
  4.1 2.8 %collective-permute-start.1 = (bf16[192,3072]{1,0:T(8,128)(2,1)}, bf16[192,3072]{1,0:T(8,128)(2,1)}, u32[]{:S(2)}, u32[]{:S(2)}) collective-permute-start(bf16[192,3072]{1,0:T(8,128)(2,1)} %get-tuple-element.19), channel_id=1, source_target_pairs={{0,12},{1,13},{2,14},{3,15},{4,8},{5,9},{6,10},{7,11},{8,4},{9,5},... | collective-permute-start | bytes 3538952 | tf_op jit(solution)/shard_map/ppermute | solution.py:70
  7.1 0.9 copy-done.12
  8.0 0.9 fusion.1
  9.7 1.1 constant_dynamic-slice_fusion
  11.3 1.7 collective-permute-start.4
  13.2 2.9 %collective-permute-start.5 = (bf16[192,640]{1,0:T(8,128)(2,1)S(1)}, bf16[192,640]{1,0:T(8,128)(2,1)S(1)}, u32[]{:S(2)}, u32[]{:S(2)}) collective-permute-start(bf16[192,640]{1,0:T(8,128)(2,1)S(1)} %pad_maximum_fusion.6), channel_id=1, source_target_pairs={{0,12},{1,13},{2,14},{3,15},{4,8},{5,9},{6,10},{7,11},{8,4},{9,5},... | collective-permute-start | bytes 737288 | tf_op jit(solution)/shard_map/ppermute | solution.py:70
  16.2 0.9 collective-permute-done.3
  17.5 2.1 %collective-permute-done.4 = bf16[192,640]{1,0:T(8,128)(2,1)S(1)} collective-permute-done((bf16[192,640]{1,0:T(8,128)(2,1)S(1)}, bf16[192,640]{1,0:T(8,128)(2,1)S(1)}, u32[]{:S(2)}, u32[]{:S(2)}) %collective-permute-start.4) | collective-permute-done | bytes 245792 | tf_op jit(solution)/shard_map/ppermute | solution.py:70
  19.7 1.9 collective-permute-start.24
  21.6 7.5 %collective-permute-done.5 = bf16[192,640]{1,0:T(8,128)(2,1)S(1)} collective-permute-done((bf16[192,640]{1,0:T(8,128)(2,1)S(1)}, bf16[192,640]{1,0:T(8,128)(2,1)S(1)}, u32[]{:S(2)}, u32[]{:S(2)}) %collective-permute-start.5) | collective-permute-done | bytes 245792 | tf_op jit(solution)/shard_map/ppermute | solution.py:70
  29.2 3.2 %collective-permute-start.7 = (bf16[4,192,640]{2,1,0:T(8,128)(2,1)S(1)}, bf16[4,192,640]{2,1,0:T(8,128)(2,1)S(1)}, u32[]{:S(2)}, u32[]{:S(2)}) collective-permute-start(bf16[4,192,640]{2,1,0:T(8,128)(2,1)S(1)} %pad_maximum_fusion.1.r0), channel_id=1, source_target_pairs={{0,3},{1,0},{2,1},{3,2},{4,7},{5,4},{6,5},{7,6},{8,11},{9,8},{10,9... | collective-permute-start | bytes 2949128 | tf_op jit(solution)/shard_map/ppermute | solution.py:70
  32.4 2.8 %collective-permute-start.15 = (bf16[192,512]{1,0:T(8,128)(2,1)}, bf16[192,512]{1,0:T(8,128)(2,1)S(1)}, u32[]{:S(2)}, u32[]{:S(2)}) collective-permute-start(bf16[192,512]{1,0:T(8,128)(2,1)} %get-tuple-element.8), channel_id=1, source_target_pairs={{0,12},{1,13},{2,14},{3,15},{4,8},{5,9},{6,10},{7,11},{8,4},{9,5},... | collective-permute-start | bytes 589832 | tf_op jit(solution)/shard_map/ppermute | solution.py:70
  35.2 1.0 pad_maximum_fusion.3.r0
  36.2 3.3 %collective-permute-start.27 = (bf16[4,192,512]{2,1,0:T(8,128)(2,1)S(1)}, bf16[4,192,512]{2,1,0:T(8,128)(2,1)S(1)}, u32[]{:S(2)}, u32[]{:S(2)}) collective-permute-start(bf16[4,192,512]{2,1,0:T(8,128)(2,1)S(1)} %pad_maximum_fusion.3.r0), channel_id=1, source_target_pairs={{0,3},{1,0},{2,1},{3,2},{4,7},{5,4},{6,5},{7,6},{8,11},{9,8},{10,9... | collective-permute-start | bytes 2359304 | tf_op jit(solution)/shard_map/ppermute | solution.py:70
  39.5 2.1 collective-permute-done.15
  42.2 6.7 %collective-permute-done.14 = bf16[192,512]{1,0:T(8,128)(2,1)S(1)} collective-permute-done((bf16[192,512]{1,0:T(8,128)(2,1)S(1)}, bf16[192,512]{1,0:T(8,128)(2,1)S(1)}, u32[]{:S(2)}, u32[]{:S(2)}) %collective-permute-start.14) | collective-permute-done | bytes 196640 | tf_op jit(solution)/shard_map/ppermute | solution.py:70
  48.9 2.2 %collective-permute-start.13 = (bf16[192,512]{1,0:T(8,128)(2,1)S(1)}, bf16[192,512]{1,0:T(8,128)(2,1)S(1)}, u32[]{:S(2)}, u32[]{:S(2)}) collective-permute-start(bf16[192,512]{1,0:T(8,128)(2,1)S(1)} %get-tuple-element.10), channel_id=1, source_target_pairs={{0,4},{1,5},{2,6},{3,7},{4,0},{5,1},{6,2},{7,3},{8,12},{9,13},{10,... | collective-permute-start | bytes 589832 | tf_op jit(solution)/shard_map/ppermute | solution.py:70
  51.1 3.6 %collective-permute-done.13 = bf16[192,512]{1,0:T(8,128)(2,1)S(1)} collective-permute-done((bf16[192,512]{1,0:T(8,128)(2,1)S(1)}, bf16[192,512]{1,0:T(8,128)(2,1)S(1)}, u32[]{:S(2)}, u32[]{:S(2)}) %collective-permute-start.13) | collective-permute-done | bytes 196640 | tf_op jit(solution)/shard_map/ppermute | solution.py:70
  54.7 2.0 collective-permute-start
  56.8 1.0 pad_maximum_fusion.2.r0
  57.9 3.2 %collective-permute-start.17 = (bf16[4,192,512]{2,1,0:T(8,128)(2,1)S(1)}, bf16[4,192,512]{2,1,0:T(8,128)(2,1)S(1)}, u32[]{:S(2)}, u32[]{:S(2)}) collective-permute-start(bf16[4,192,512]{2,1,0:T(8,128)(2,1)S(1)} %pad_maximum_fusion.2.r0), channel_id=1, source_target_pairs={{0,3},{1,0},{2,1},{3,2},{4,7},{5,4},{6,5},{7,6},{8,11},{9,8},{10,9... | collective-permute-start | bytes 2359304 | tf_op jit(solution)/shard_map/ppermute | solution.py:70
  61.2 0.9 slice.101
  62.9 13.0 %collective-permute-done.26.r1 = bf16[4,192,512]{2,1,0:T(8,128)(2,1)S(1)} collective-permute-done((bf16[4,192,512]{2,1,0:T(8,128)(2,1)S(1)}, bf16[4,192,512]{2,1,0:T(8,128)(2,1)S(1)}, u32[]{:S(2)}, u32[]{:S(2)}) %collective-permute-start.26) | collective-permute-done | bytes 786464 | tf_op jit(solution)/shard_map/ppermute | solution.py:70
  75.9 4.9 %collective-permute-start.9 = (bf16[2,192,640]{2,1,0:T(8,128)(2,1)}, bf16[2,192,640]{2,1,0:T(8,128)(2,1)}, u32[]{:S(2)}, u32[]{:S(2)}) collective-permute-start(bf16[2,192,640]{2,1,0:T(8,128)(2,1)} %slice.101), channel_id=1, source_target_pairs={{0,3},{1,0},{2,1},{3,2},{4,7},{5,4},{6,5},{7,6},{8,11},{9,8},{10,9... | collective-permute-start | bytes 1474568 | tf_op jit(solution)/shard_map/ppermute | solution.py:70
  80.9 0.9 copy-done.8
  81.8 1.8 slice.109
  83.6 1.8 slice.108
  85.4 1.0 slice.103
  86.4 6.4 %collective-permute-done.16.r1 = bf16[4,192,512]{2,1,0:T(8,128)(2,1)} collective-permute-done((bf16[4,192,512]{2,1,0:T(8,128)(2,1)S(1)}, bf16[4,192,512]{2,1,0:T(8,128)(2,1)}, u32[]{:S(2)}, u32[]{:S(2)}) %collective-permute-start.16) | collective-permute-done | bytes 786464 | tf_op jit(solution)/shard_map/ppermute | solution.py:70
  92.8 5.0 %collective-permute-start.29 = (bf16[2,192,512]{2,1,0:T(8,128)(2,1)}, bf16[2,192,512]{2,1,0:T(8,128)(2,1)}, u32[]{:S(2)}, u32[]{:S(2)}) collective-permute-start(bf16[2,192,512]{2,1,0:T(8,128)(2,1)} %slice.109), channel_id=1, source_target_pairs={{0,3},{1,0},{2,1},{3,2},{4,7},{5,4},{6,5},{7,6},{8,11},{9,8},{10,9... | collective-permute-start | bytes 1179656 | tf_op jit(solution)/shard_map/ppermute | solution.py:70
  97.8 1.0 slice.102
  98.9 9.8 %collective-permute-done.2 = bf16[192,3072]{1,0:T(8,128)(2,1)} collective-permute-done((bf16[192,3072]{1,0:T(8,128)(2,1)}, bf16[192,3072]{1,0:T(8,128)(2,1)}, u32[]{:S(2)}, u32[]{:S(2)}) %collective-permute-start.2) | collective-permute-done | bytes 1179680 | tf_op jit(solution)/shard_map/ppermute | solution.py:70
  109.2 2.7 %pad_maximum_fusion.l = bf16[4,192,3072]{2,1,0:T(8,128)(2,1)S(1)} fusion(bf16[1,192,3072]{2,1,0:T(8,128)(2,1)} %bitcast.20, bf16[1,192,3072]{2,1,0:T(8,128)(2,1)} %bitcast.19, bf16[1,192,3072]{2,1,0:T(8,128)(2,1)} %bitcast.17, bf16[1,192,3072]{2,1,0:T(8,128)(2,1)} %get-tuple-element.18), kind=kLoop, calls=%fused_computation | loop fusion | flops 7077888 | bytes 9437184 | tf_op jit(solution)/shard_map/stack | solution.py:107
  111.9 1.8 collective-permute-start.18
  113.7 9.6 %shard_map.59 = (f32[4,192,512]{2,1,0:T(8,128)S(1)}, f32[4,192,128]{2,1,0:T(8,128)S(1)}) custom-call(s32[16]{0:T(128)S(1)} %stack.133.off, bf16[4,192,3072]{2,1,0:T(8,128)(2,1)S(1)} %pad_maximum_fusion.l, bf16[4,192,640]{2,1,0:T(8,128)(2,1)S(1)} %pad_maximum_fusion.1.r0, bf16[4,192,640]{2,1,0:T(8,128)(2,1)S(1)} %copy-done.3, ...), custom_call_target="tpu_custom_call" | custom-call | tf_op jit(solution)/shard_map/pallas_call | solution.py:37
  124.1 5.3 %collective-permute-start.12 = (f32[192,512]{1,0:T(8,128)S(1)}, f32[192,512]{1,0:T(8,128)S(1)}, u32[]{:S(2)}, u32[]{:S(2)}) collective-permute-start(f32[192,512]{1,0:T(8,128)S(1)} %get-tuple-element.28), channel_id=1, source_target_pairs={{0,12},{1,13},{2,14},{3,15},{4,8},{5,9},{6,10},{7,11},{8,4},{9,5},... | collective-permute-start | bytes 1179656 | tf_op jit(solution)/shard_map/ppermute | solution.py:70
  129.6 1.0 collective-permute-start.10
  130.6 6.5 %shard_map.60 = f32[4,192,512]{2,1,0:T(8,128)S(1)} custom-call(s32[16]{0:T(128)S(1)} %stack.133.off, bf16[4,192,3072]{2,1,0:T(8,128)(2,1)S(1)} %pad_maximum_fusion.l, bf16[4,192,512]{2,1,0:T(8,128)(2,1)S(1)} %pad_maximum_fusion.2.r0, bf16[4,192,512]{2,1,0:T(8,128)(2,1)} %collective-permute-done.16.r1, bf16[4,192,512]{2,1,0:T(8,128)(2,1)S(1)} %copy-done.9, ...), custom_call_target="tpu_custom_call" | custom-call | tf_op jit(solution)/shard_map/pallas_call | solution.py:37
  137.1 1.2 fusion.3
  138.3 1.0 convolution_add_fusion.1
  139.4 1.1 collective-permute-done.10
  140.7 1.1 slice_bitcast_fusion.3
  141.7 2.2 %copy-done.11 = f32[2,192,3072]{2,1,0:T(8,128)} copy-done((f32[2,192,3072]{2,1,0:T(8,128)}, f32[2,192,3072]{2,1,0:T(8,128)S(1)}, u32[]{:S(2)}) %copy-start.11) | copy-done | bytes 4718616
  143.9 1.2 collective-permute-start.20
  145.1 1.0 fusion.2
  146.1 4.0 %collective-permute-start.21 = (f32[192,512]{1,0:T(8,128)}, f32[192,512]{1,0:T(8,128)S(1)}, u32[]{:S(2)}, u32[]{:S(2)}) collective-permute-start(f32[192,512]{1,0:T(8,128)} %get-tuple-element.25), channel_id=1, source_target_pairs={{0,8},{1,9},{2,10},{3,11},{4,12},{5,13},{6,14},{7,15},{8,0},{9,1},... | collective-permute-start | bytes 1179656 | tf_op jit(solution)/shard_map/ppermute | solution.py:70
  150.1 1.0 fusion
  151.2 3.9 %collective-permute-done.33 = f32[64,64]{1,0:T(8,128)S(1)} collective-permute-done((f32[64,64]{1,0:T(8,128)S(1)}, f32[64,64]{1,0:T(8,128)S(1)}, u32[]{:S(2)}, u32[]{:S(2)}) %collective-permute-start.33) | collective-permute-done | bytes 16416 | tf_op jit(solution)/shard_map/ppermute | solution.py:70
  155.1 0.9 collective-permute-start.34
  156.1 4.5 %collective-permute-done.34 = f32[64,64]{1,0:T(8,128)S(1)} collective-permute-done((f32[64,64]{1,0:T(8,128)S(1)}, f32[64,64]{1,0:T(8,128)S(1)}, u32[]{:S(2)}, u32[]{:S(2)}) %collective-permute-start.34) | collective-permute-done | bytes 16416 | tf_op jit(solution)/shard_map/ppermute | solution.py:70
  161.2 2.3 %copy-done.1 = bf16[4,192,3072]{2,1,0:T(8,128)(2,1)S(1)} copy-done((bf16[4,192,3072]{2,1,0:T(8,128)(2,1)S(1)}, bf16[4,192,3072]{2,1,0:T(8,128)(2,1)}, u32[]{:S(2)}) %copy-start.1) | copy-done | bytes 4718616
  163.6 7.5 %shard_map.61 = f32[4,192,512]{2,1,0:T(8,128)S(1)} custom-call(s32[16]{0:T(128)S(1)} %stack.133.off, bf16[4,192,3072]{2,1,0:T(8,128)(2,1)S(1)} %copy-done.1, bf16[4,192,512]{2,1,0:T(8,128)(2,1)S(1)} %pad_maximum_fusion.3.r0, bf16[4,192,512]{2,1,0:T(8,128)(2,1)S(1)} %copy-done.7, bf16[4,192,512]{2,1,0:T(8,128)(2,1)S(1)} %copy-done.5, ...), custom_call_target="tpu_custom_call" | custom-call | tf_op jit(solution)/shard_map/pallas_call | solution.py:37
  171.1 1.5 multiply_reduce_fusion
  173.3 3.4 %collective-permute-start.22 = (f32[192,512]{1,0:T(8,128)S(1)}, f32[192,512]{1,0:T(8,128)S(1)}, u32[]{:S(2)}, u32[]{:S(2)}) collective-permute-start(f32[192,512]{1,0:T(8,128)S(1)} %copy-done.14), channel_id=1, source_target_pairs={{0,12},{1,13},{2,14},{3,15},{4,8},{5,9},{6,10},{7,11},{8,4},{9,5},... | collective-permute-start | bytes 1179656 | tf_op jit(solution)/shard_map/ppermute | solution.py:70
  176.7 1.8 bitcast_dynamic-update-slice_fusion.5
  179.3 3.2 %collective-permute-done.22 = f32[192,512]{1,0:T(8,128)S(1)} collective-permute-done((f32[192,512]{1,0:T(8,128)S(1)}, f32[192,512]{1,0:T(8,128)S(1)}, u32[]{:S(2)}, u32[]{:S(2)}) %collective-permute-start.22) | collective-permute-done | bytes 393248 | tf_op jit(solution)/shard_map/ppermute | solution.py:70
  183.3 0.9 slice_bitcast_fusion
  184.9 2.0 collective-permute-start.37
  186.9 4.6 %collective-permute-start.31 = (f32[192,512]{1,0:T(8,128)S(1)}, f32[192,512]{1,0:T(8,128)S(1)}, u32[]{:S(2)}, u32[]{:S(2)}) collective-permute-start(f32[192,512]{1,0:T(8,128)S(1)} %get-tuple-element.21), channel_id=1, source_target_pairs={{0,8},{1,9},{2,10},{3,11},{4,12},{5,13},{6,14},{7,15},{8,0},{9,1},... | collective-permute-start | bytes 1179656 | tf_op jit(solution)/shard_map/ppermute | solution.py:70
  192.1 3.7 %collective-permute-start.38 = (f32[8,128]{1,0:T(8,128)S(1)}, f32[8,128]{1,0:T(8,128)S(1)}, u32[]{:S(2)}, u32[]{:S(2)}) collective-permute-start(f32[8,128]{1,0:T(8,128)S(1)} %fusion.23), channel_id=1, source_target_pairs={{0,64},{1,65},{2,66},{3,67},{4,68},{5,69},{6,70},{7,71},{8,72},{9,... | collective-permute-start | bytes 12296 | tf_op jit(solution)/shard_map/ppermute | solution.py:70
  195.8 1.6 collective-permute-done.38
  198.6 1.5 fusion.8
  202.2 6.9 %collective-permute-done.32 = f32[192,512]{1,0:T(8,128)S(1)} collective-permute-done((f32[192,512]{1,0:T(8,128)S(1)}, f32[192,512]{1,0:T(8,128)S(1)}, u32[]{:S(2)}, u32[]{:S(2)}) %collective-permute-start.32) | collective-permute-done | bytes 393248 | tf_op jit(solution)/shard_map/ppermute | solution.py:70
  (105 shorter events, 13.4 us)
Async XLA Ops:
  0.6 6.3 %copy-start.17 = (s32[2]{0:T(128)S(1)}, s32[2]{0:T(128)}, u32[]{:S(2)}) copy-start(s32[2]{0:T(128)} %param.7) | copy-start | bytes 28
  0.6 6.4 %copy-start.13 = (bf16[2,3072,64]{1,2,0:T(8,128)(2,1)S(1)}, bf16[2,3072,64]{1,2,0:T(8,128)(2,1)}, u32[]{:S(2)}) copy-start(bf16[2,3072,64]{1,2,0:T(8,128)(2,1)} %param.6) | copy-start | bytes 2359300
  0.7 7.3 %copy-start.10 = (bf16[2,192,3072]{2,1,0:T(8,128)(2,1)S(1)}, bf16[2,192,3072]{2,1,0:T(8,128)(2,1)}, u32[]{:S(2)}) copy-start(bf16[2,192,3072]{2,1,0:T(8,128)(2,1)} %param.5) | copy-start | bytes 7077892
  4.1 52.7 %collective-permute-start.1 = (bf16[192,3072]{1,0:T(8,128)(2,1)}, bf16[192,3072]{1,0:T(8,128)(2,1)}, u32[]{:S(2)}, u32[]{:S(2)}) collective-permute-start(bf16[192,3072]{1,0:T(8,128)(2,1)} %get-tuple-element.19), channel_id=1, source_target_pairs={{0,12},{1,13},{2,14},{3,15},{4,8},{5,9},{6,10},{7,11},{8,4},{9,5},... | collective-permute-start | bytes 3538952 | tf_op jit(solution)/shard_map/ppermute | solution.py:70
  7.1 0.9 copy-start.12
  9.7 1.2 copy-start.16
  10.8 6.3 %collective-permute-start.3 = (bf16[192,640]{1,0:T(8,128)(2,1)S(1)}, bf16[192,640]{1,0:T(8,128)(2,1)S(1)}, u32[]{:S(2)}, u32[]{:S(2)}) collective-permute-start(bf16[192,640]{1,0:T(8,128)(2,1)S(1)} %pad_maximum_fusion.4), channel_id=1, source_target_pairs={{0,4},{1,5},{2,6},{3,7},{4,0},{5,1},{6,2},{7,3},{8,12},{9,13},{10,... | collective-permute-start | bytes 737288 | tf_op jit(solution)/shard_map/ppermute | solution.py:70
  11.3 30.3 %copy-start.15 = (bf16[192,512]{1,0:T(8,128)(2,1)S(1)}, bf16[192,512]{1,0:T(8,128)(2,1)}, u32[]{:S(2)}) copy-start(bf16[192,512]{1,0:T(8,128)(2,1)} %get-tuple-element.9) | copy-start | bytes 589828
  11.3 8.4 %collective-permute-start.4 = (bf16[192,640]{1,0:T(8,128)(2,1)S(1)}, bf16[192,640]{1,0:T(8,128)(2,1)S(1)}, u32[]{:S(2)}, u32[]{:S(2)}) collective-permute-start(bf16[192,640]{1,0:T(8,128)(2,1)S(1)} %pad_maximum_fusion.5), channel_id=1, source_target_pairs={{0,8},{1,9},{2,10},{3,11},{4,12},{5,13},{6,14},{7,15},{8,0},{9,1},... | collective-permute-start | bytes 737288 | tf_op jit(solution)/shard_map/ppermute | solution.py:70
  13.2 15.9 %collective-permute-start.5 = (bf16[192,640]{1,0:T(8,128)(2,1)S(1)}, bf16[192,640]{1,0:T(8,128)(2,1)S(1)}, u32[]{:S(2)}, u32[]{:S(2)}) collective-permute-start(bf16[192,640]{1,0:T(8,128)(2,1)S(1)} %pad_maximum_fusion.6), channel_id=1, source_target_pairs={{0,12},{1,13},{2,14},{3,15},{4,8},{5,9},{6,10},{7,11},{8,4},{9,5},... | collective-permute-start | bytes 737288 | tf_op jit(solution)/shard_map/ppermute | solution.py:70
  16.1 16.3 %collective-permute-start.23 = (bf16[192,512]{1,0:T(8,128)(2,1)}, bf16[192,512]{1,0:T(8,128)(2,1)}, u32[]{:S(2)}, u32[]{:S(2)}) collective-permute-start(bf16[192,512]{1,0:T(8,128)(2,1)} %get-tuple-element.7), channel_id=1, source_target_pairs={{0,4},{1,5},{2,6},{3,7},{4,0},{5,1},{6,2},{7,3},{8,12},{9,13},{10,... | collective-permute-start | bytes 589832 | tf_op jit(solution)/shard_map/ppermute | solution.py:70
  17.1 18.0 %collective-permute-start.25 = (bf16[192,512]{1,0:T(8,128)(2,1)}, bf16[192,512]{1,0:T(8,128)(2,1)S(1)}, u32[]{:S(2)}, u32[]{:S(2)}) collective-permute-start(bf16[192,512]{1,0:T(8,128)(2,1)} %get-tuple-element.16), channel_id=1, source_target_pairs={{0,12},{1,13},{2,14},{3,15},{4,8},{5,9},{6,10},{7,11},{8,4},{9,5},... | collective-permute-start | bytes 589832 | tf_op jit(solution)/shard_map/ppermute | solution.py:70
  19.7 15.5 %collective-permute-start.24 = (bf16[192,512]{1,0:T(8,128)(2,1)}, bf16[192,512]{1,0:T(8,128)(2,1)S(1)}, u32[]{:S(2)}, u32[]{:S(2)}) collective-permute-start(bf16[192,512]{1,0:T(8,128)(2,1)} %get-tuple-element.17), channel_id=1, source_target_pairs={{0,8},{1,9},{2,10},{3,11},{4,12},{5,13},{6,14},{7,15},{8,0},{9,1},... | collective-permute-start | bytes 589832 | tf_op jit(solution)/shard_map/ppermute | solution.py:70
  29.2 28.7 %collective-permute-start.7 = (bf16[4,192,640]{2,1,0:T(8,128)(2,1)S(1)}, bf16[4,192,640]{2,1,0:T(8,128)(2,1)S(1)}, u32[]{:S(2)}, u32[]{:S(2)}) collective-permute-start(bf16[4,192,640]{2,1,0:T(8,128)(2,1)S(1)} %pad_maximum_fusion.1.r0), channel_id=1, source_target_pairs={{0,3},{1,0},{2,1},{3,2},{4,7},{5,4},{6,5},{7,6},{8,11},{9,8},{10,9... | collective-permute-start | bytes 2949128 | tf_op jit(solution)/shard_map/ppermute | solution.py:70
  32.4 9.2 %collective-permute-start.15 = (bf16[192,512]{1,0:T(8,128)(2,1)}, bf16[192,512]{1,0:T(8,128)(2,1)S(1)}, u32[]{:S(2)}, u32[]{:S(2)}) collective-permute-start(bf16[192,512]{1,0:T(8,128)(2,1)} %get-tuple-element.8), channel_id=1, source_target_pairs={{0,12},{1,13},{2,14},{3,15},{4,8},{5,9},{6,10},{7,11},{8,4},{9,5},... | collective-permute-start | bytes 589832 | tf_op jit(solution)/shard_map/ppermute | solution.py:70
  35.2 26.0 %collective-permute-start.6 = (bf16[4,192,640]{2,1,0:T(8,128)(2,1)S(1)}, bf16[4,192,640]{2,1,0:T(8,128)(2,1)S(1)}, u32[]{:S(2)}, u32[]{:S(2)}) collective-permute-start(bf16[4,192,640]{2,1,0:T(8,128)(2,1)S(1)} %pad_maximum_fusion.1.r0), channel_id=1, source_target_pairs={{0,1},{1,2},{2,3},{3,0},{4,5},{5,6},{6,7},{7,4},{8,9},{9,10},{10,1... | collective-permute-start | bytes 2949128 | tf_op jit(solution)/shard_map/ppermute | solution.py:70
  36.2 21.6 %collective-permute-start.27 = (bf16[4,192,512]{2,1,0:T(8,128)(2,1)S(1)}, bf16[4,192,512]{2,1,0:T(8,128)(2,1)S(1)}, u32[]{:S(2)}, u32[]{:S(2)}) collective-permute-start(bf16[4,192,512]{2,1,0:T(8,128)(2,1)S(1)} %pad_maximum_fusion.3.r0), channel_id=1, source_target_pairs={{0,3},{1,0},{2,1},{3,2},{4,7},{5,4},{6,5},{7,6},{8,11},{9,8},{10,9... | collective-permute-start | bytes 2359304 | tf_op jit(solution)/shard_map/ppermute | solution.py:70
  41.6 7.3 %collective-permute-start.14 = (bf16[192,512]{1,0:T(8,128)(2,1)S(1)}, bf16[192,512]{1,0:T(8,128)(2,1)S(1)}, u32[]{:S(2)}, u32[]{:S(2)}) collective-permute-start(bf16[192,512]{1,0:T(8,128)(2,1)S(1)} %copy-done.15), channel_id=1, source_target_pairs={{0,8},{1,9},{2,10},{3,11},{4,12},{5,13},{6,14},{7,15},{8,0},{9,1},... | collective-permute-start | bytes 589832 | tf_op jit(solution)/shard_map/ppermute | solution.py:70
  48.9 5.9 %collective-permute-start.13 = (bf16[192,512]{1,0:T(8,128)(2,1)S(1)}, bf16[192,512]{1,0:T(8,128)(2,1)S(1)}, u32[]{:S(2)}, u32[]{:S(2)}) collective-permute-start(bf16[192,512]{1,0:T(8,128)(2,1)S(1)} %get-tuple-element.10), channel_id=1, source_target_pairs={{0,4},{1,5},{2,6},{3,7},{4,0},{5,1},{6,2},{7,3},{8,12},{9,13},{10,... | collective-permute-start | bytes 589832 | tf_op jit(solution)/shard_map/ppermute | solution.py:70
  54.7 44.1 %collective-permute-start = (bf16[192,3072]{1,0:T(8,128)(2,1)}, bf16[192,3072]{1,0:T(8,128)(2,1)}, u32[]{:S(2)}, u32[]{:S(2)}) collective-permute-start(bf16[192,3072]{1,0:T(8,128)(2,1)} %bitcast.124), channel_id=1, source_target_pairs={{0,4},{1,5},{2,6},{3,7},{4,0},{5,1},{6,2},{7,3},{8,12},{9,13},{10,... | collective-permute-start | bytes 3538952 | tf_op jit(solution)/shard_map/ppermute | solution.py:70
  56.8 52.0 %collective-permute-start.2 = (bf16[192,3072]{1,0:T(8,128)(2,1)}, bf16[192,3072]{1,0:T(8,128)(2,1)}, u32[]{:S(2)}, u32[]{:S(2)}) collective-permute-start(bf16[192,3072]{1,0:T(8,128)(2,1)} %collective-permute-done.1), channel_id=1, source_target_pairs={{0,4},{1,5},{2,6},{3,7},{4,0},{5,1},{6,2},{7,3},{8,12},{9,13},{10,... | collective-permute-start | bytes 3538952 | tf_op jit(solution)/shard_map/ppermute | solution.py:70
  57.8 23.0 %copy-start.4 = (bf16[4,192,512]{2,1,0:T(8,128)(2,1)}, bf16[4,192,512]{2,1,0:T(8,128)(2,1)S(1)}, u32[]{:S(2)}) copy-start(bf16[4,192,512]{2,1,0:T(8,128)(2,1)S(1)} %collective-permute-done.27.r2) | copy-start | bytes 2359300
  57.9 18.1 %collective-permute-start.26 = (bf16[4,192,512]{2,1,0:T(8,128)(2,1)S(1)}, bf16[4,192,512]{2,1,0:T(8,128)(2,1)S(1)}, u32[]{:S(2)}, u32[]{:S(2)}) collective-permute-start(bf16[4,192,512]{2,1,0:T(8,128)(2,1)S(1)} %pad_maximum_fusion.3.r0), channel_id=1, source_target_pairs={{0,1},{1,2},{2,3},{3,0},{4,5},{5,6},{6,7},{7,4},{8,9},{9,10},{10,1... | collective-permute-start | bytes 2359304 | tf_op jit(solution)/shard_map/ppermute | solution.py:70
  57.9 22.9 %collective-permute-start.17 = (bf16[4,192,512]{2,1,0:T(8,128)(2,1)S(1)}, bf16[4,192,512]{2,1,0:T(8,128)(2,1)S(1)}, u32[]{:S(2)}, u32[]{:S(2)}) collective-permute-start(bf16[4,192,512]{2,1,0:T(8,128)(2,1)S(1)} %pad_maximum_fusion.2.r0), channel_id=1, source_target_pairs={{0,3},{1,0},{2,1},{3,2},{4,7},{5,4},{6,5},{7,6},{8,11},{9,8},{10,9... | collective-permute-start | bytes 2359304 | tf_op jit(solution)/shard_map/ppermute | solution.py:70
  61.2 19.7 %copy-start.2 = (bf16[4,192,640]{2,1,0:T(8,128)(2,1)}, bf16[4,192,640]{2,1,0:T(8,128)(2,1)S(1)}, u32[]{:S(2)}) copy-start(bf16[4,192,640]{2,1,0:T(8,128)(2,1)S(1)} %collective-permute-done.6.r1) | copy-start | bytes 2949124
  61.2 31.6 %collective-permute-start.16 = (bf16[4,192,512]{2,1,0:T(8,128)(2,1)S(1)}, bf16[4,192,512]{2,1,0:T(8,128)(2,1)}, u32[]{:S(2)}, u32[]{:S(2)}) collective-permute-start(bf16[4,192,512]{2,1,0:T(8,128)(2,1)S(1)} %pad_maximum_fusion.2.r0), channel_id=1, source_target_pairs={{0,1},{1,2},{2,3},{3,0},{4,5},{5,6},{6,7},{7,4},{8,9},{9,10},{10,1... | collective-permute-start | bytes 2359304 | tf_op jit(solution)/shard_map/ppermute | solution.py:70
  75.9 4.9 %copy-start.6 = (bf16[4,192,512]{2,1,0:T(8,128)(2,1)}, bf16[4,192,512]{2,1,0:T(8,128)(2,1)S(1)}, u32[]{:S(2)}) copy-start(bf16[4,192,512]{2,1,0:T(8,128)(2,1)S(1)} %collective-permute-done.26.r1) | copy-start | bytes 2359300
  75.9 36.0 %collective-permute-start.9 = (bf16[2,192,640]{2,1,0:T(8,128)(2,1)}, bf16[2,192,640]{2,1,0:T(8,128)(2,1)}, u32[]{:S(2)}, u32[]{:S(2)}) collective-permute-start(bf16[2,192,640]{2,1,0:T(8,128)(2,1)} %slice.101), channel_id=1, source_target_pairs={{0,3},{1,0},{2,1},{3,2},{4,7},{5,4},{6,5},{7,6},{8,11},{9,8},{10,9... | collective-permute-start | bytes 1474568 | tf_op jit(solution)/shard_map/ppermute | solution.py:70
  80.8 0.9 copy-start.8
  81.7 32.0 %collective-permute-start.8 = (bf16[2,192,640]{2,1,0:T(8,128)(2,1)}, bf16[2,192,640]{2,1,0:T(8,128)(2,1)}, u32[]{:S(2)}, u32[]{:S(2)}) collective-permute-start(bf16[2,192,640]{2,1,0:T(8,128)(2,1)} %slice.100), channel_id=1, source_target_pairs={{0,1},{1,2},{2,3},{3,0},{4,5},{5,6},{6,7},{7,4},{8,9},{9,10},{10,1... | collective-permute-start | bytes 1474568 | tf_op jit(solution)/shard_map/ppermute | solution.py:70
  92.8 68.4 %collective-permute-start.29 = (bf16[2,192,512]{2,1,0:T(8,128)(2,1)}, bf16[2,192,512]{2,1,0:T(8,128)(2,1)}, u32[]{:S(2)}, u32[]{:S(2)}) collective-permute-start(bf16[2,192,512]{2,1,0:T(8,128)(2,1)} %slice.109), channel_id=1, source_target_pairs={{0,3},{1,0},{2,1},{3,2},{4,7},{5,4},{6,5},{7,6},{8,11},{9,8},{10,9... | collective-permute-start | bytes 1179656 | tf_op jit(solution)/shard_map/ppermute | solution.py:70
  98.8 62.4 %collective-permute-start.28 = (bf16[2,192,512]{2,1,0:T(8,128)(2,1)}, bf16[2,192,512]{2,1,0:T(8,128)(2,1)}, u32[]{:S(2)}, u32[]{:S(2)}) collective-permute-start(bf16[2,192,512]{2,1,0:T(8,128)(2,1)} %slice.108), channel_id=1, source_target_pairs={{0,1},{1,2},{2,3},{3,0},{4,5},{5,6},{6,7},{7,4},{8,9},{9,10},{10,1... | collective-permute-start | bytes 1179656 | tf_op jit(solution)/shard_map/ppermute | solution.py:70
  108.7 20.8 %collective-permute-start.19 = (bf16[2,192,512]{2,1,0:T(8,128)(2,1)S(1)}, bf16[2,192,512]{2,1,0:T(8,128)(2,1)S(1)}, u32[]{:S(2)}, u32[]{:S(2)}) collective-permute-start(bf16[2,192,512]{2,1,0:T(8,128)(2,1)S(1)} %slice.103), channel_id=1, source_target_pairs={{0,3},{1,0},{2,1},{3,2},{4,7},{5,4},{6,5},{7,6},{8,11},{9,8},{10,9... | collective-permute-start | bytes 1179656 | tf_op jit(solution)/shard_map/ppermute | solution.py:70
  109.2 4.6 %copy-start.3 = (bf16[4,192,640]{2,1,0:T(8,128)(2,1)S(1)}, bf16[4,192,640]{2,1,0:T(8,128)(2,1)}, u32[]{:S(2)}) copy-start(bf16[4,192,640]{2,1,0:T(8,128)(2,1)} %copy-done.2) | copy-start | bytes 2949124
  111.9 18.7 %copy-start = (bf16[4,192,3072]{2,1,0:T(8,128)(2,1)}, bf16[4,192,3072]{2,1,0:T(8,128)(2,1)S(1)}, u32[]{:S(2)}) copy-start(bf16[4,192,3072]{2,1,0:T(8,128)(2,1)S(1)} %pad_maximum_fusion.l) | copy-start | bytes 14155780
  111.9 17.7 %collective-permute-start.18 = (bf16[2,192,512]{2,1,0:T(8,128)(2,1)S(1)}, bf16[2,192,512]{2,1,0:T(8,128)(2,1)S(1)}, u32[]{:S(2)}, u32[]{:S(2)}) collective-permute-start(bf16[2,192,512]{2,1,0:T(8,128)(2,1)S(1)} %slice.102), channel_id=1, source_target_pairs={{0,1},{1,2},{2,3},{3,0},{4,5},{5,6},{6,7},{7,4},{8,9},{9,10},{10,1... | collective-permute-start | bytes 1179656 | tf_op jit(solution)/shard_map/ppermute | solution.py:70
  123.4 7.3 %copy-start.9 = (bf16[4,192,512]{2,1,0:T(8,128)(2,1)S(1)}, bf16[4,192,512]{2,1,0:T(8,128)(2,1)}, u32[]{:S(2)}) copy-start(bf16[4,192,512]{2,1,0:T(8,128)(2,1)} %copy-done.8) | copy-start | bytes 2359300
  124.1 16.5 %collective-permute-start.12 = (f32[192,512]{1,0:T(8,128)S(1)}, f32[192,512]{1,0:T(8,128)S(1)}, u32[]{:S(2)}, u32[]{:S(2)}) collective-permute-start(f32[192,512]{1,0:T(8,128)S(1)} %get-tuple-element.28), channel_id=1, source_target_pairs={{0,12},{1,13},{2,14},{3,15},{4,8},{5,9},{6,10},{7,11},{8,4},{9,5},... | collective-permute-start | bytes 1179656 | tf_op jit(solution)/shard_map/ppermute | solution.py:70
  129.5 11.0 %collective-permute-start.11 = (f32[192,512]{1,0:T(8,128)S(1)}, f32[192,512]{1,0:T(8,128)S(1)}, u32[]{:S(2)}, u32[]{:S(2)}) collective-permute-start(f32[192,512]{1,0:T(8,128)S(1)} %get-tuple-element.29), channel_id=1, source_target_pairs={{0,8},{1,9},{2,10},{3,11},{4,12},{5,13},{6,14},{7,15},{8,0},{9,1},... | collective-permute-start | bytes 1179656 | tf_op jit(solution)/shard_map/ppermute | solution.py:70
  129.6 10.9 %collective-permute-start.10 = (f32[192,512]{1,0:T(8,128)S(1)}, f32[192,512]{1,0:T(8,128)S(1)}, u32[]{:S(2)}, u32[]{:S(2)}) collective-permute-start(f32[192,512]{1,0:T(8,128)S(1)} %get-tuple-element.30), channel_id=1, source_target_pairs={{0,4},{1,5},{2,6},{3,7},{4,0},{5,1},{6,2},{7,3},{8,12},{9,13},{10,... | collective-permute-start | bytes 1179656 | tf_op jit(solution)/shard_map/ppermute | solution.py:70
  137.1 24.1 %copy-start.5 = (bf16[4,192,512]{2,1,0:T(8,128)(2,1)S(1)}, bf16[4,192,512]{2,1,0:T(8,128)(2,1)}, u32[]{:S(2)}) copy-start(bf16[4,192,512]{2,1,0:T(8,128)(2,1)} %copy-done.4) | copy-start | bytes 2359300
  137.1 24.1 %copy-start.7 = (bf16[4,192,512]{2,1,0:T(8,128)(2,1)S(1)}, bf16[4,192,512]{2,1,0:T(8,128)(2,1)}, u32[]{:S(2)}) copy-start(bf16[4,192,512]{2,1,0:T(8,128)(2,1)} %copy-done.6) | copy-start | bytes 2359300
  141.7 2.2 %copy-start.11 = (f32[2,192,3072]{2,1,0:T(8,128)}, f32[2,192,3072]{2,1,0:T(8,128)S(1)}, u32[]{:S(2)}) copy-start(f32[2,192,3072]{2,1,0:T(8,128)S(1)} %get-tuple-element.27) | copy-start | bytes 14155780
  143.9 32.8 %collective-permute-start.20 = (f32[192,512]{1,0:T(8,128)}, f32[192,512]{1,0:T(8,128)}, u32[]{:S(2)}, u32[]{:S(2)}) collective-permute-start(f32[192,512]{1,0:T(8,128)} %get-tuple-element.26), channel_id=1, source_target_pairs={{0,4},{1,5},{2,6},{3,7},{4,0},{5,1},{6,2},{7,3},{8,12},{9,13},{10,... | collective-permute-start | bytes 1179656 | tf_op jit(solution)/shard_map/ppermute | solution.py:70
  146.1 32.4 %collective-permute-start.21 = (f32[192,512]{1,0:T(8,128)}, f32[192,512]{1,0:T(8,128)S(1)}, u32[]{:S(2)}, u32[]{:S(2)}) collective-permute-start(f32[192,512]{1,0:T(8,128)} %get-tuple-element.25), channel_id=1, source_target_pairs={{0,8},{1,9},{2,10},{3,11},{4,12},{5,13},{6,14},{7,15},{8,0},{9,1},... | collective-permute-start | bytes 1179656 | tf_op jit(solution)/shard_map/ppermute | solution.py:70
  151.1 4.0 %collective-permute-start.33 = (f32[64,64]{1,0:T(8,128)S(1)}, f32[64,64]{1,0:T(8,128)S(1)}, u32[]{:S(2)}, u32[]{:S(2)}) collective-permute-start(f32[64,64]{1,0:T(8,128)S(1)} %fusion), channel_id=1, source_target_pairs={{0,1},{1,0},{2,3},{3,2},{4,5},{5,4},{6,7},{7,6},{8,9},{9,8},{10,11... | collective-permute-start | bytes 49160 | tf_op jit(solution)/shard_map/ppermute | solution.py:70
  155.1 5.4 %collective-permute-start.34 = (f32[64,64]{1,0:T(8,128)S(1)}, f32[64,64]{1,0:T(8,128)S(1)}, u32[]{:S(2)}, u32[]{:S(2)}) collective-permute-start(f32[64,64]{1,0:T(8,128)S(1)} %add.436), channel_id=1, source_target_pairs={{0,2},{1,3},{2,0},{3,1},{4,6},{5,7},{6,4},{7,5},{8,10},{9,11},{10,... | collective-permute-start | bytes 49160 | tf_op jit(solution)/shard_map/ppermute | solution.py:70
  161.2 9.9 %collective-permute-start.35 = (f32[64,64]{1,0:T(8,128)}, f32[64,64]{1,0:T(8,128)}, u32[]{:S(2)}, u32[]{:S(2)}) collective-permute-start(f32[64,64]{1,0:T(8,128)} %add.437), channel_id=1, source_target_pairs={{0,8},{1,9},{2,10},{3,11},{4,12},{5,13},{6,14},{7,15},{8,0},{9,1},... | collective-permute-start | bytes 49160 | tf_op jit(solution)/shard_map/ppermute | solution.py:70
  161.2 2.3 %copy-start.1 = (bf16[4,192,3072]{2,1,0:T(8,128)(2,1)S(1)}, bf16[4,192,3072]{2,1,0:T(8,128)(2,1)}, u32[]{:S(2)}) copy-start(bf16[4,192,3072]{2,1,0:T(8,128)(2,1)} %copy-done) | copy-start | bytes 14155780
  163.6 9.8 %copy-start.14 = (f32[192,512]{1,0:T(8,128)S(1)}, f32[192,512]{1,0:T(8,128)}, u32[]{:S(2)}) copy-start(f32[192,512]{1,0:T(8,128)} %get-tuple-element.24) | copy-start | bytes 1179652
  173.2 11.0 %collective-permute-start.36 = (f32[8,128]{1,0:T(8,128)S(1)}, f32[8,128]{1,0:T(8,128)S(1)}, u32[]{:S(2)}, u32[]{:S(2)}) collective-permute-start(f32[8,128]{1,0:T(8,128)S(1)} %broadcast_in_dim.46), channel_id=1, source_target_pairs={{0,16},{1,17},{2,18},{3,19},{4,20},{5,21},{6,22},{7,23},{8,24},{9,... | collective-permute-start | bytes 12296 | tf_op jit(solution)/shard_map/ppermute | solution.py:70
  173.3 9.2 %collective-permute-start.22 = (f32[192,512]{1,0:T(8,128)S(1)}, f32[192,512]{1,0:T(8,128)S(1)}, u32[]{:S(2)}, u32[]{:S(2)}) collective-permute-start(f32[192,512]{1,0:T(8,128)S(1)} %copy-done.14), channel_id=1, source_target_pairs={{0,12},{1,13},{2,14},{3,15},{4,8},{5,9},{6,10},{7,11},{8,4},{9,5},... | collective-permute-start | bytes 1179656 | tf_op jit(solution)/shard_map/ppermute | solution.py:70
  184.1 16.5 %collective-permute-start.30 = (f32[192,512]{1,0:T(8,128)S(1)}, f32[192,512]{1,0:T(8,128)S(1)}, u32[]{:S(2)}, u32[]{:S(2)}) collective-permute-start(f32[192,512]{1,0:T(8,128)S(1)} %get-tuple-element.22), channel_id=1, source_target_pairs={{0,4},{1,5},{2,6},{3,7},{4,0},{5,1},{6,2},{7,3},{8,12},{9,13},{10,... | collective-permute-start | bytes 1179656 | tf_op jit(solution)/shard_map/ppermute | solution.py:70
  184.9 6.6 %collective-permute-start.37 = (f32[8,128]{1,0:T(8,128)S(1)}, f32[8,128]{1,0:T(8,128)S(1)}, u32[]{:S(2)}, u32[]{:S(2)}) collective-permute-start(f32[8,128]{1,0:T(8,128)S(1)} %broadcast_add_fusion), channel_id=1, source_target_pairs={{0,32},{1,33},{2,34},{3,35},{4,36},{5,37},{6,38},{7,39},{8,40},{9,... | collective-permute-start | bytes 12296 | tf_op jit(solution)/shard_map/ppermute | solution.py:70
  186.9 14.5 %collective-permute-start.31 = (f32[192,512]{1,0:T(8,128)S(1)}, f32[192,512]{1,0:T(8,128)S(1)}, u32[]{:S(2)}, u32[]{:S(2)}) collective-permute-start(f32[192,512]{1,0:T(8,128)S(1)} %get-tuple-element.21), channel_id=1, source_target_pairs={{0,8},{1,9},{2,10},{3,11},{4,12},{5,13},{6,14},{7,15},{8,0},{9,1},... | collective-permute-start | bytes 1179656 | tf_op jit(solution)/shard_map/ppermute | solution.py:70
  192.1 5.2 %collective-permute-start.38 = (f32[8,128]{1,0:T(8,128)S(1)}, f32[8,128]{1,0:T(8,128)S(1)}, u32[]{:S(2)}, u32[]{:S(2)}) collective-permute-start(f32[8,128]{1,0:T(8,128)S(1)} %fusion.23), channel_id=1, source_target_pairs={{0,64},{1,65},{2,66},{3,67},{4,68},{5,69},{6,70},{7,71},{8,72},{9,... | collective-permute-start | bytes 12296 | tf_op jit(solution)/shard_map/ppermute | solution.py:70
  200.1 9.0 %collective-permute-start.32 = (f32[192,512]{1,0:T(8,128)S(1)}, f32[192,512]{1,0:T(8,128)S(1)}, u32[]{:S(2)}, u32[]{:S(2)}) collective-permute-start(f32[192,512]{1,0:T(8,128)S(1)} %get-tuple-element.20), channel_id=1, source_target_pairs={{0,12},{1,13},{2,14},{3,15},{4,8},{5,9},{6,10},{7,11},{8,4},{9,5},... | collective-permute-start | bytes 1179656 | tf_op jit(solution)/shard_map/ppermute | solution.py:70

commit v2 on v1

v2 whole, which is shorter than its diff:
```python
import jax
import jax.numpy as jnp
from jax import lax
from jax.experimental import pallas as pl
from jax.experimental.pallas import tpu as pltpu
from jax.sharding import PartitionSpec as P

SIDE = 4
CHUNKS = 2


def product(offsets, left, pieces, widths):
    rows, depth = left.shape[1:]
    full = pieces[0].shape[2]
    where = [(i, p) for i, piece in enumerate(pieces) for p in range(piece.shape[0])]

    def kernel(off, l, *rest):
        refs, outs = rest[:len(pieces)], rest[len(pieces):-2]
        scratch, sems = rest[-2:]
        copies = []
        for n, (i, p) in enumerate(where):
            at = pl.multiple_of(off[n], 64)
            copies.append(pltpu.make_async_copy(refs[i].at[p], scratch.at[pl.ds(at, rows)], sems.at[n]))
        for copy in copies:
            copy.start()
        for copy in copies:
            copy.wait()
        lhs = l[...].reshape(SIDE * rows, depth)
        start = 0
        for k, width in enumerate(widths):
            got = jnp.dot(lhs, scratch[:, start:start + width], preferred_element_type=jnp.float32)
            for p in range(SIDE):
                outs[k * SIDE + p][...] = got[p * rows:(p + 1) * rows]
            start += width

    anywhere = pl.BlockSpec(memory_space=pl.ANY)
    inside = pl.BlockSpec(memory_space=pltpu.VMEM)
    return pl.pallas_call(
        kernel,
        in_specs=[pl.BlockSpec(memory_space=pltpu.SMEM), inside] + [anywhere] * len(pieces),
        out_specs=[inside] * (SIDE * len(widths)),
        out_shape=[jax.ShapeDtypeStruct((rows, width), jnp.float32) for width in widths for _ in range(SIDE)],
        scratch_shapes=[pltpu.VMEM((depth, full), jnp.bfloat16), pltpu.SemaphoreType.DMA((len(where),))],
        compiler_params=pltpu.CompilerParams(vmem_limit_bytes=32 << 20),
    )(offsets, left, *pieces)


def place(spots, blocks, shape, into=None):
    rows, width = blocks[0].shape
    n = len(blocks)

    def kernel(at, *rest):
        out, sems = rest[-2:]
        copies = []
        for k in range(n):
            start = pl.multiple_of(at[n + k], 128)
            copies.append(pltpu.make_async_copy(rest[k], out.at[at[k], :, pl.ds(start, width)], sems.at[k]))
        for copy in copies:
            copy.start()
        for copy in copies:
            copy.wait()

    anywhere = pl.BlockSpec(memory_space=pl.ANY)
    inside = pl.BlockSpec(memory_space=pltpu.VMEM)
    given = list(blocks) + ([] if into is None else [into])
    return pl.pallas_call(
        kernel,
        in_specs=[pl.BlockSpec(memory_space=pltpu.SMEM)] + [inside] * n + [anywhere] * (len(given) - n),
        out_specs=anywhere,
        out_shape=jax.ShapeDtypeStruct(shape, jnp.float32),
        scratch_shapes=[pltpu.SemaphoreType.DMA((n,))],
        input_output_aliases={} if into is None else {n + 1: 0},
        compiler_params=pltpu.CompilerParams(vmem_limit_bytes=8 << 20),
    )(spots, *given)


def solution(mesh):
    n_row, n_col = mesh.shape["row"], mesh.shape["col"]

    def pairs(move):
        found = []
        for row in range(n_row):
            for col in range(n_col):
                cx, cy = col // SIDE, col % SIDE
                g, h = (cy, cx) if row % 2 else (cx, cy)
                to, g, h = move(row, g, h)
                cx, cy = (h, g) if row % 2 else (g, h)
                if to != row:
                    cx, cy = col // SIDE, col % SIDE
                found.append((row * n_col + col, to * n_col + cx * SIDE + cy))
        return found

    along_g = {p: pairs(lambda row, g, h, p=p: (row, g ^ p, h)) for p in (1, 2, 3)}
    along_h = {p: pairs(lambda row, g, h, p=p: (row, g, h ^ p)) for p in (1, 2)}
    up = pairs(lambda row, g, h: (row, g, (h + 1) % SIDE))
    down = pairs(lambda row, g, h: (row, g, (h - 1) % SIDE))
    across = {p: pairs(lambda row, g, h, p=p: (row ^ p, g, h)) for p in (1, 2, 4)}

    def send(value, table, name):
        with jax.named_scope(name):
            return lax.ppermute(value, ("row", "col"), table)

    def after(value, *others):
        return lax.optimization_barrier((value, *others))[0]

    def body(left_edge, right_edge, projector, sector_size):
        count, rows, depth = left_edge.shape
        kept = projector.shape[2]
        half = depth // 2
        width = half // CHUNKS
        odd = lax.axis_index("row") % 2
        col = lax.axis_index("col")
        cx, cy = col // SIDE, col % SIDE
        g = jnp.where(odd == 1, cy, cx)
        h = jnp.where(odd == 1, cx, cy)
        owner = lambda gg, hh: jnp.where(odd == 1, hh * SIDE + gg, gg * SIDE + hh)

        states = jnp.arange(depth, dtype=jnp.int32)
        live = (states[None, :] < sector_size[:, None]).astype(jnp.bfloat16)
        masked = projector * live[:, :, None]

        seen = jnp.einsum("skj,sjq->skq", right_edge, masked, preferred_element_type=jnp.float32)
        top = lax.reduce_precision(seen, exponent_bits=8, mantissa_bits=7)
        shadow = jnp.concatenate([top, seen - top], axis=2).astype(jnp.bfloat16)

        sector = g // 2
        mine = lax.dynamic_index_in_dim(left_edge, sector, 0, keepdims=False)
        other = lax.dynamic_index_in_dim(left_edge, 1 - sector, 0, keepdims=False)

        def part(p):
            to = g ^ p
            got = lax.dynamic_slice(right_edge, (to // 2, 0, (to % 2) * half), (1, rows, half))[0]
            return jnp.concatenate([lax.dynamic_index_in_dim(shadow, to // 2, 0, keepdims=False), got], axis=1)

        gs = [g ^ p for p in range(SIDE)]
        hs = [h, (h - 1) % SIDE, (h + 1) % SIDE, (h + 2) % SIDE]
        offsets = jnp.stack([owner(gg, hh) * rows for hh in hs for gg in gs]).astype(jnp.int32)

        left = [mine] + [send(mine if p == 1 else other, along_g[p], f"left{p}") for p in (1, 2, 3)]
        blocks = [part(0)] + [send(part(p), along_g[p], f"right{p}") for p in (1, 2, 3)]

        extra = 2 * kept

        def cut(c):
            first = extra + c * width if c else 0
            return jnp.stack([block[:, first:extra + (c + 1) * width] for block in blocks])

        def spots(c):
            return jnp.stack([gg // 2 for gg in gs] + [(gg % 2) * half + c * width for gg in gs]).astype(jnp.int32)

        own0 = after(cut(0), left[1], left[3])
        below0, above0 = send(own0, up, "up0"), send(own0, down, "down0")
        beyond0 = send(after(below0, left[2]), up, "forward0")
        own1 = after(cut(1), below0, above0)
        below1, above1 = send(own1, up, "up1"), send(own1, down, "down1")
        left = jnp.stack(left)
        out = product(offsets, left, (own0, below0, above0, beyond0), (extra, width))
        inner, out0 = out[:SIDE], out[SIDE:]
        beyond1 = send(above1, down, "forward1")
        out0 = [out0[0]] + [send(out0[p], along_g[p], f"back0{p}") for p in (1, 2, 3)]
        beyond1 = after(beyond1, *out0[1:])
        out1 = product(offsets, left, (own1, below1, above1, beyond1), (width,))
        enlarged = place(spots(0), out0, (count, rows, depth))
        out1 = [out1[0]] + [send(out1[p], along_g[p], f"back1{p}") for p in (1, 2, 3)]
        enlarged = place(spots(1), out1, (count, rows, depth), enlarged)

        inner = [got[:, :kept] + got[:, kept:] for got in inner]
        ours = lax.dynamic_index_in_dim(masked, sector, 0, keepdims=False)
        terms = []
        for p in range(SIDE):
            chosen = lax.dynamic_slice_in_dim(ours, owner(g ^ p, h) * rows, rows, 0).astype(jnp.float32)
            terms.append(jnp.einsum("ip,iq->pq", chosen, inner[p], precision=lax.Precision.HIGHEST))
        corner = (terms[0] + terms[1]) + (terms[2] + terms[3])
        for p in (1, 2):
            corner = corner + send(corner, along_h[p], f"corner{p}")
        beside = send(corner, along_g[2], "beside")
        corner = jnp.where(sector == 0, jnp.stack([corner, beside]), jnp.stack([beside, corner]))
        total = jnp.broadcast_to(jnp.sum(corner * corner), (8, 128))
        for p in (1, 2, 4):
            total = total + send(total, across[p], f"total{p}")
        entries = n_row * count * kept * kept
        return enlarged, corner * lax.rsqrt(total[0, 0] / entries + 1e-06)

    placed = (P("row", "col", None), P("row", "col", None), P("row", None, None), P("row"))
    return jax.shard_map(
        body,
        mesh=mesh,
        in_specs=placed,
        out_specs=(P("row", "col", None), P("row", None, None)),
        check_vma=False,
    )
```

time: 211 us -> 172 us (0.82)
  starting transfers between devices: 66.6 us -> 42.6 us
  local copies, waits for them, and re-layouts: 28.8 us -> 14 us
  Pallas kernels: 23.6 us -> 20.1 us
    ppermute x39 -> x24, starting transfers between devices: 66.6 us -> 42.6 us  [send(): return lax.ppermute(value, ('row', 'col'), table)]
    pallas_call x3 -> x2, Pallas kernels: 23.6 us -> 15.5 us  [product(): pl.pallas_call(kernel, in_specs=[pl.BlockSpec(memory_space=pltpu.SMEM), i...]
    slice x6 -> x0, local copies, waits for them, and re-layouts: 7.35 us -> none  [the longest x3 3.68 us: body(): high = send(above[2:], down)]
    dynamic_update_slice x9 -> x0, local copies, waits for them, and re-layouts: 5.74 us -> none  [body(): lax.dynamic_update_slice(enlarged, block[None], ((g ^ p) // 2, 0, start))]
    another operation x1 -> x10, local copies, waits for them, and re-layouts: 0.09 us -> 5.46 us  [the longest x7 5.2 us: cut(): jnp.stack([block[:, first:extra + (c + 1) * width] for block in blocks])]
    pallas_call x0 -> x2, Pallas kernels: none -> 4.67 us  [place(): pl.pallas_call(kernel, in_specs=[pl.BlockSpec(memory_space=pltpu.SMEM)] +...]
    unnamed x36 -> x24, local copies, waits for them, and re-layouts: 6.33 us -> 2.97 us
    concatenate x3, other arithmetic: 0.08 us -> 2.76 us  [part(): jnp.concatenate([lax.dynamic_index_in_dim(shadow, to // 2, 0, keepdims=Fa...]
  transfers between devices with their start and end apart: 39 -> 24, of which waited for: 15 -> 13; matrix products, arithmetic and copies ran while one was open for 16% -> 13% of each run, Pallas kernels for 11% -> 10%
where the time goes in v2:
time: 172 us
  waiting for transfers between devices  75.3 us (44%)
  starting transfers between devices  42.6 us (25%)
  Pallas kernels  20.1 us (12%)
  local copies, waits for them, and re-layouts  14 us (8%)
  other arithmetic  10.4 us (6%)
  matrix products  7.18 us (4%)
  between operations  2.08 us (1%)
    ppermute x24, waiting for transfers between devices, send(): return lax.ppermute(value, ('row', 'col'), table)  75.3 us
    ppermute x24, starting transfers between devices, send(): return lax.ppermute(value, ('row', 'col'), table)  42.6 us
    pallas_call x2, Pallas kernels, product(): pl.pallas_call(kernel, in_specs=[pl.BlockSpec(memory_space=pltpu.SMEM), i...  15.5 us
    another operation x7, local copies, waits for them, and re-layouts, cut(): jnp.stack([block[:, first:extra + (c + 1) * width] for block in blocks])  5.2 us
    pallas_call x2, Pallas kernels, place(): pl.pallas_call(kernel, in_specs=[pl.BlockSpec(memory_space=pltpu.SMEM)] +...  4.67 us
    dot_general x4, matrix products, body(): jnp.einsum('ip,iq->pq', chosen, inner[p], precision=lax.Precision.HIGHEST)  4.32 us
  transfers between devices with their start and end apart: 24, of which 13 were waited for; matrix products, arithmetic and copies ran while one was open for 13% of the time, Pallas kernels for 10%

profile of v2, /device:TPU:0, one launch (start us, length us, event | category | flops | bytes accessed | tf_op | source)
XLA Modules:
  0.0 171.7 jit_solution(14481134284454084795)
XLA Ops:
  0.8 0.7 compare_convert_fusion
  1.6 1.2 broadcast_multiply_fusion
  2.8 2.9 %fusion.2 = (bf16[2,192,64]{1,2,0:T(8,128)(2,1)S(1)}, bf16[2,192,64]{1,2,0:T(8,128)(2,1)S(1)}) fusion(bf16[2,3072,64]{1,2,0:T(8,128)(2,1)S(1)} %broadcast_multiply_fusion, bf16[2,192,3072]{2,1,0:T(8,128)(2,1)} %param.5), kind=kOutput, calls=%fused_computation.35 | convolution fusion | flops 151093248 | bytes 3244032 | tf_op jit(solution)/shard_map/skj,sjq->skq/dot_general | solution.py:122
  5.9 1.2 dynamic-slice_bitcast_fusion.4
  7.1 1.0 pad_maximum_fusion.5
  8.0 2.8 %collective-permute-start.5 = (bf16[192,1664]{1,0:T(8,128)(2,1)}, bf16[192,1664]{1,0:T(8,128)(2,1)S(1)}, u32[]{:S(2)}, u32[]{:S(2)}) collective-permute-start(bf16[192,1664]{1,0:T(8,128)(2,1)} %pad_maximum_fusion.5), channel_id=1, source_target_pairs={{0,12},{1,13},{2,14},{3,15},{4,8},{5,9},{6,10},{7,11},{8,4},{9,5},... | collective-permute-start | bytes 1916936 | tf_op jit(solution)/shard_map/right3/ppermute | solution.py:101
  11.0 0.9 pad_maximum_fusion.4
  11.9 0.8 collective-permute-start.4
  12.7 2.9 %constant_dynamic-slice_fusion = (bf16[1,192,3072]{2,1,0:T(8,128)(2,1)S(1)}, bf16[192,3072]{1,0:T(8,128)(2,1)}) fusion(bf16[2,192,3072]{2,1,0:T(8,128)(2,1)} %param.4, s32[]{:T(128)S(6)} %select_n.240, s32[]{:T(128)S(6)} %select_n.241), kind=kLoop, calls=%fused_computation.70 | loop fusion | bytes 4718600 | tf_op jit(solution)/shard_map/jit(dynamic_index_in_dim)/dynamic_slice | solution.py:127
  15.5 0.5 collective-permute-start
  16.0 2.8 %collective-permute-start.2 = (bf16[192,3072]{1,0:T(8,128)(2,1)}, bf16[192,3072]{1,0:T(8,128)(2,1)}, u32[]{:S(2)}, u32[]{:S(2)}) collective-permute-start(bf16[192,3072]{1,0:T(8,128)(2,1)} %get-tuple-element.39), channel_id=1, source_target_pairs={{0,12},{1,13},{2,14},{3,15},{4,8},{5,9},{6,10},{7,11},{8,4},{9,5},... | collective-permute-start | bytes 3538952 | tf_op jit(solution)/shard_map/left3/ppermute | solution.py:101
  19.0 0.9 pad_maximum_fusion.3
  19.9 0.2 collective-permute-start.3
  20.2 6.5 %collective-permute-done.5 = bf16[192,1664]{1,0:T(8,128)(2,1)S(1)} collective-permute-done((bf16[192,1664]{1,0:T(8,128)(2,1)}, bf16[192,1664]{1,0:T(8,128)(2,1)S(1)}, u32[]{:S(2)}, u32[]{:S(2)}) %collective-permute-start.5) | collective-permute-done | bytes 639008 | tf_op jit(solution)/shard_map/right3/ppermute | solution.py:101
  26.8 1.2 slice_bitcast_fusion.1
  28.0 13.4 %collective-permute-done.3 = bf16[192,1664]{1,0:T(8,128)(2,1)} collective-permute-done((bf16[192,1664]{1,0:T(8,128)(2,1)}, bf16[192,1664]{1,0:T(8,128)(2,1)}, u32[]{:S(2)}, u32[]{:S(2)}) %collective-permute-start.3) | collective-permute-done | bytes 639008 | tf_op jit(solution)/shard_map/right1/ppermute | solution.py:101
  41.4 1.0 slice_bitcast_fusion.2
  42.6 1.7 %collective-permute-start.6 = (bf16[4,192,896]{2,1,0:T(8,128)(2,1)S(1)}, bf16[4,192,896]{2,1,0:T(8,128)(2,1)}, u32[]{:S(2)}, u32[]{:S(2)}) collective-permute-start(bf16[4,192,896]{2,1,0:T(8,128)(2,1)S(1)} %pad_maximum_fusion.1.rest_0_), channel_id=1, source_target_pairs={{0,1},{1,2},{2,3},{3,0},{4,5},{5,6},{6,7},{7,4},{8,9},{9,10},{10,1... | collective-permute-start | bytes 4128776 | tf_op jit(solution)/shard_map/up0/ppermute | solution.py:101
  44.4 3.0 %collective-permute-start.1 = (bf16[192,3072]{1,0:T(8,128)(2,1)}, bf16[192,3072]{1,0:T(8,128)(2,1)}, u32[]{:S(2)}, u32[]{:S(2)}) collective-permute-start(bf16[192,3072]{1,0:T(8,128)(2,1)} %get-tuple-element.39), channel_id=1, source_target_pairs={{0,8},{1,9},{2,10},{3,11},{4,12},{5,13},{6,14},{7,15},{8,0},{9,1},... | collective-permute-start | bytes 3538952 | tf_op jit(solution)/shard_map/left2/ppermute | solution.py:101
  47.4 1.7 collective-permute-start.7
  49.1 1.0 slice_bitcast_fusion.3
  50.0 1.0 slice_bitcast_fusion.4
  51.0 23.0 %collective-permute-done.1 = bf16[192,3072]{1,0:T(8,128)(2,1)} collective-permute-done((bf16[192,3072]{1,0:T(8,128)(2,1)}, bf16[192,3072]{1,0:T(8,128)(2,1)}, u32[]{:S(2)}, u32[]{:S(2)}) %collective-permute-start.1) | collective-permute-done | bytes 1179680 | tf_op jit(solution)/shard_map/left2/ppermute | solution.py:101
  74.0 0.7 collective-permute-done.6.rest_1_
  74.7 0.7 collective-permute-start.11
  75.4 1.0 slice_bitcast_fusion.5
  76.6 1.1 copy-done
  77.6 2.6 %collective-permute-start.9 = (bf16[4,192,768]{2,1,0:T(8,128)(2,1)S(1)}, bf16[4,192,768]{2,1,0:T(8,128)(2,1)}, u32[]{:S(2)}, u32[]{:S(2)}) collective-permute-start(bf16[4,192,768]{2,1,0:T(8,128)(2,1)S(1)} %pad_maximum_fusion.2.rest_0_), channel_id=1, source_target_pairs={{0,3},{1,0},{2,1},{3,2},{4,7},{5,4},{6,5},{7,6},{8,11},{9,8},{10,9... | collective-permute-start | bytes 3538952 | tf_op jit(solution)/shard_map/down1/ppermute | solution.py:101
  80.3 2.7 %pad_maximum_fusion.l = bf16[4,192,3072]{2,1,0:T(8,128)(2,1)S(1)} fusion(bf16[1,192,3072]{2,1,0:T(8,128)(2,1)} %bitcast.28, bf16[1,192,3072]{2,1,0:T(8,128)(2,1)} %bitcast.27, bf16[1,192,3072]{2,1,0:T(8,128)(2,1)} %bitcast.25, bf16[1,192,3072]{2,1,0:T(8,128)(2,1)} %copy-done.7), kind=kLoop, calls=%fused_computation | loop fusion | flops 7077888 | bytes 9437184 | tf_op jit(solution)/shard_map/stack | solution.py:156
  83.1 10.8 %collective-permute-done.9.rest_2_ = bf16[4,192,768]{2,1,0:T(8,128)(2,1)} collective-permute-done((bf16[4,192,768]{2,1,0:T(8,128)(2,1)S(1)}, bf16[4,192,768]{2,1,0:T(8,128)(2,1)}, u32[]{:S(2)}, u32[]{:S(2)}) %collective-permute-start.9) | collective-permute-done | bytes 1179680 | tf_op jit(solution)/shard_map/down1/ppermute | solution.py:101
  94.0 3.8 %collective-permute-start.10 = (bf16[4,192,768]{2,1,0:T(8,128)(2,1)}, bf16[4,192,768]{2,1,0:T(8,128)(2,1)S(1)}, u32[]{:S(2)}, u32[]{:S(2)}) collective-permute-start(bf16[4,192,768]{2,1,0:T(8,128)(2,1)} %collective-permute-done.9.rest_2_), channel_id=1, source_target_pairs={{0,3},{1,0},{2,1},{3,2},{4,7},{5,4},{6,5},{7,6},{8,11},{9,8},{10,9... | collective-permute-start | bytes 3538952 | tf_op jit(solution)/shard_map/forward1/ppermute | solution.py:101
  97.7 8.1 %shard_map.59 = (f32[192,128]{1,0:T(8,128)S(1)}, f32[192,128]{1,0:T(8,128)S(1)}, f32[192,128]{1,0:T(8,128)S(1)}, f32[192,128]{1,0:T(8,128)S(1)}, f32[192,768]{1,...) custom-call(s32[16]{0:T(128)S(1)} %stack.179.off, ...), custom_call_target="tpu_custom_call" | custom-call | tf_op jit(solution)/shard_map/pallas_call | solution.py:38
  105.9 1.1 fusion.10
  106.9 1.1 fusion.3
  108.0 1.1 convolution_add_fusion.1
  109.1 1.1 fusion
  110.3 4.0 %collective-permute-done.18 = f32[64,64]{1,0:T(8,128)S(1)} collective-permute-done((f32[64,64]{1,0:T(8,128)S(1)}, f32[64,64]{1,0:T(8,128)S(1)}, u32[]{:S(2)}, u32[]{:S(2)}) %collective-permute-start.18) | collective-permute-done | bytes 16416 | tf_op jit(solution)/shard_map/corner1/ppermute | solution.py:101
  114.4 2.1 %collective-permute-start.12 = (f32[192,768]{1,0:T(8,128)S(1)}, f32[192,768]{1,0:T(8,128)S(1)}, u32[]{:S(2)}, u32[]{:S(2)}) collective-permute-start(f32[192,768]{1,0:T(8,128)S(1)} %get-tuple-element.21), channel_id=1, source_target_pairs={{0,4},{1,5},{2,6},{3,7},{4,0},{5,1},{6,2},{7,3},{8,12},{9,13},{10,... | collective-permute-start | bytes 1769480 | tf_op jit(solution)/shard_map/back01/ppermute | solution.py:101
  116.5 2.9 %collective-permute-start.13 = (f32[192,768]{1,0:T(8,128)S(1)}, f32[192,768]{1,0:T(8,128)S(1)}, u32[]{:S(2)}, u32[]{:S(2)}) collective-permute-start(f32[192,768]{1,0:T(8,128)S(1)} %get-tuple-element.22), channel_id=1, source_target_pairs={{0,8},{1,9},{2,10},{3,11},{4,12},{5,13},{6,14},{7,15},{8,0},{9,1},... | collective-permute-start | bytes 1769480 | tf_op jit(solution)/shard_map/back02/ppermute | solution.py:101
  119.4 0.8 collective-permute-done.19
  120.2 3.3 %collective-permute-start.14 = (f32[192,768]{1,0:T(8,128)S(1)}, f32[192,768]{1,0:T(8,128)S(1)}, u32[]{:S(2)}, u32[]{:S(2)}) collective-permute-start(f32[192,768]{1,0:T(8,128)S(1)} %get-tuple-element.23), channel_id=1, source_target_pairs={{0,12},{1,13},{2,14},{3,15},{4,8},{5,9},{6,10},{7,11},{8,4},{9,5},... | collective-permute-start | bytes 1769480 | tf_op jit(solution)/shard_map/back03/ppermute | solution.py:101
  123.5 1.0 collective-permute-done.12.rest_1_
  124.5 2.7 %collective-permute-start.20 = (f32[64,64]{1,0:T(8,128)S(1)}, f32[64,64]{1,0:T(8,128)S(1)}, u32[]{:S(2)}, u32[]{:S(2)}) collective-permute-start(f32[64,64]{1,0:T(8,128)S(1)} %add.333), channel_id=1, source_target_pairs={{0,8},{1,9},{2,10},{3,11},{4,12},{5,13},{6,14},{7,15},{8,0},{9,1},... | collective-permute-start | bytes 49160 | tf_op jit(solution)/shard_map/beside/ppermute | solution.py:101
  127.2 6.4 %collective-permute-done.13.rest_2_ = f32[192,768]{1,0:T(8,128)S(1)} collective-permute-done((f32[192,768]{1,0:T(8,128)S(1)}, f32[192,768]{1,0:T(8,128)S(1)}, u32[]{:S(2)}, u32[]{:S(2)}) %collective-permute-start.13) | collective-permute-done | bytes 589856 | tf_op jit(solution)/shard_map/back02/ppermute | solution.py:101
  133.7 4.4 %collective-permute-done.14.rest_3_ = f32[192,768]{1,0:T(8,128)S(1)} collective-permute-done((f32[192,768]{1,0:T(8,128)S(1)}, f32[192,768]{1,0:T(8,128)S(1)}, u32[]{:S(2)}, u32[]{:S(2)}) %collective-permute-start.14) | collective-permute-done | bytes 589856 | tf_op jit(solution)/shard_map/back03/ppermute | solution.py:101
  138.0 7.4 %shard_map.60 = (f32[192,768]{1,0:T(8,128)S(1)}, f32[192,768]{1,0:T(8,128)}, f32[192,768]{1,0:T(8,128)}, f32[192,768]{1,0:T(8,128)}) custom-call(s32[16]{0:T(128)S(1)} %stack.179.off, bf16[4,192,3072]{2,1,0:T(8,128)(2,1)S(1)} %pad_maximum_fusion.l, bf16[4,192,768]{2,1,0:T(8,128)(2,1)S(1)} %pad_maximum_fusion.2.rest_0_, ...), custom_call_target="tpu_custom_call" | custom-call | tf_op jit(solution)/shard_map/pallas_call | solution.py:38
  145.4 0.8 copy-done.4
  146.2 0.6 collective-permute-start.15
  146.8 3.0 %collective-permute-start.16 = (f32[192,768]{1,0:T(8,128)}, f32[192,768]{1,0:T(8,128)}, u32[]{:S(2)}, u32[]{:S(2)}) collective-permute-start(f32[192,768]{1,0:T(8,128)} %get-tuple-element.27), channel_id=1, source_target_pairs={{0,8},{1,9},{2,10},{3,11},{4,12},{5,13},{6,14},{7,15},{8,0},{9,1},... | collective-permute-start | bytes 1769480 | tf_op jit(solution)/shard_map/back12/ppermute | solution.py:101
  149.8 1.1 collective-permute-start.17
  150.9 0.6 multiply_reduce_fusion
  151.5 0.6 broadcast_in_dim.2
  152.3 1.2 collective-permute-done.21
  153.4 0.6 broadcast_add_fusion
  154.0 2.0 %collective-permute-start.22 = (f32[8,128]{1,0:T(8,128)S(1)}, f32[8,128]{1,0:T(8,128)S(1)}, u32[]{:S(2)}, u32[]{:S(2)}) collective-permute-start(f32[8,128]{1,0:T(8,128)S(1)} %broadcast_add_fusion), channel_id=1, source_target_pairs={{0,32},{1,33},{2,34},{3,35},{4,36},{5,37},{6,38},{7,39},{8,40},{9,... | collective-permute-start | bytes 12296 | tf_op jit(solution)/shard_map/total2/ppermute | solution.py:101
  156.0 1.7 collective-permute-done.22
  157.7 0.6 fusion.36
  158.4 4.0 %collective-permute-start.23 = (f32[8,128]{1,0:T(8,128)S(1)}, f32[8,128]{1,0:T(8,128)S(1)}, u32[]{:S(2)}, u32[]{:S(2)}) collective-permute-start(f32[8,128]{1,0:T(8,128)S(1)} %fusion.36), channel_id=1, source_target_pairs={{0,64},{1,65},{2,66},{3,67},{4,68},{5,69},{6,70},{7,71},{8,72},{9,... | collective-permute-start | bytes 12296 | tf_op jit(solution)/shard_map/total4/ppermute | solution.py:101
  162.5 1.4 collective-permute-done.23
  163.9 0.5 slice.67
  165.1 0.6 fusion.21
  165.8 1.1 copy-done.3
  166.8 2.0 %shard_map.61.rest_4_ = f32[2,192,3072]{2,1,0:T(8,128)} custom-call(s32[8]{0:T(128)S(1)} %stack.198.at, f32[192,768]{1,0:T(8,128)S(1)} %get-tuple-element.29.rest_0_, f32[192,768]{1,0:T(8,128)S(1)} %collective-permute-done.12.rest_1_, f32[192,768]{1,0:T(8,128)S(1)} %collective-permute-done.13.rest_2_, f32[192,768]{1,0:T(8,128)S(1)} %copy-done.3), custom_call_target="tpu_custom_call" | custom-call | tf_op jit(solution)/shard_map/pallas_call | solution.py:66
  168.8 2.7 %shard_map.62 = f32[2,192,3072]{2,1,0:T(8,128)} custom-call(s32[8]{0:T(128)S(1)} %stack.162.at, f32[192,768]{1,0:T(8,128)S(1)} %copy-done.5, f32[192,768]{1,0:T(8,128)S(1)} %collective-permute-done.15.rest_1_, f32[192,768]{1,0:T(8,128)} %collective-permute-done.16.rest_2_, ...), custom_call_target="tpu_custom_call", output_to_operand_aliasing={{}: (5, {})} | custom-call | tf_op jit(solution)/shard_map/pallas_call | solution.py:66
  (52 shorter events, 1.5 us)
Async XLA Ops:
  2.8 2.9 %copy-start.8 = (bf16[2,3072,64]{1,2,0:T(8,128)(2,1)}, bf16[2,3072,64]{1,2,0:T(8,128)(2,1)S(1)}, u32[]{:S(2)}) copy-start(bf16[2,3072,64]{1,2,0:T(8,128)(2,1)S(1)} %broadcast_multiply_fusion) | copy-start | bytes 2359300
  2.8 3.1 %copy-start.6 = (bf16[2,192,3072]{2,1,0:T(8,128)(2,1)S(1)}, bf16[2,192,3072]{2,1,0:T(8,128)(2,1)}, u32[]{:S(2)}) copy-start(bf16[2,192,3072]{2,1,0:T(8,128)(2,1)} %param.5) | copy-start | bytes 7077892
  7.1 3.9 %copy-start.10 = (bf16[192,1536]{1,0:T(8,128)(2,1)S(1)}, bf16[192,1536]{1,0:T(8,128)(2,1)}, u32[]{:S(2)}) copy-start(bf16[192,1536]{1,0:T(8,128)(2,1)} %get-tuple-element.37) | copy-start | bytes 1769476
  8.0 18.7 %collective-permute-start.5 = (bf16[192,1664]{1,0:T(8,128)(2,1)}, bf16[192,1664]{1,0:T(8,128)(2,1)S(1)}, u32[]{:S(2)}, u32[]{:S(2)}) collective-permute-start(bf16[192,1664]{1,0:T(8,128)(2,1)} %pad_maximum_fusion.5), channel_id=1, source_target_pairs={{0,12},{1,13},{2,14},{3,15},{4,8},{5,9},{6,10},{7,11},{8,4},{9,5},... | collective-permute-start | bytes 1916936 | tf_op jit(solution)/shard_map/right3/ppermute | solution.py:101
  11.9 14.9 %collective-permute-start.4 = (bf16[192,1664]{1,0:T(8,128)(2,1)}, bf16[192,1664]{1,0:T(8,128)(2,1)}, u32[]{:S(2)}, u32[]{:S(2)}) collective-permute-start(bf16[192,1664]{1,0:T(8,128)(2,1)} %pad_maximum_fusion.4), channel_id=1, source_target_pairs={{0,8},{1,9},{2,10},{3,11},{4,12},{5,13},{6,14},{7,15},{8,0},{9,1},... | collective-permute-start | bytes 1916936 | tf_op jit(solution)/shard_map/right2/ppermute | solution.py:101
  12.7 6.3 %copy-start.9 = (bf16[192,1536]{1,0:T(8,128)(2,1)S(1)}, bf16[192,1536]{1,0:T(8,128)(2,1)}, u32[]{:S(2)}) copy-start(bf16[192,1536]{1,0:T(8,128)(2,1)} %get-tuple-element.35) | copy-start | bytes 1769476
  15.5 11.2 %copy-start.7 = (bf16[1,192,3072]{2,1,0:T(8,128)(2,1)}, bf16[1,192,3072]{2,1,0:T(8,128)(2,1)S(1)}, u32[]{:S(2)}) copy-start(bf16[1,192,3072]{2,1,0:T(8,128)(2,1)S(1)} %get-tuple-element.38) | copy-start | bytes 3538948
  15.5 27.1 %collective-permute-start = (bf16[192,3072]{1,0:T(8,128)(2,1)S(1)}, bf16[192,3072]{1,0:T(8,128)(2,1)}, u32[]{:S(2)}, u32[]{:S(2)}) collective-permute-start(bf16[192,3072]{1,0:T(8,128)(2,1)S(1)} %bitcast.81), channel_id=1, source_target_pairs={{0,4},{1,5},{2,6},{3,7},{4,0},{5,1},{6,2},{7,3},{8,12},{9,13},{10,... | collective-permute-start | bytes 3538952 | tf_op jit(solution)/shard_map/left1/ppermute | solution.py:101
  16.0 26.6 %collective-permute-start.2 = (bf16[192,3072]{1,0:T(8,128)(2,1)}, bf16[192,3072]{1,0:T(8,128)(2,1)}, u32[]{:S(2)}, u32[]{:S(2)}) collective-permute-start(bf16[192,3072]{1,0:T(8,128)(2,1)} %get-tuple-element.39), channel_id=1, source_target_pairs={{0,12},{1,13},{2,14},{3,15},{4,8},{5,9},{6,10},{7,11},{8,4},{9,5},... | collective-permute-start | bytes 3538952 | tf_op jit(solution)/shard_map/left3/ppermute | solution.py:101
  19.9 21.5 %collective-permute-start.3 = (bf16[192,1664]{1,0:T(8,128)(2,1)}, bf16[192,1664]{1,0:T(8,128)(2,1)}, u32[]{:S(2)}, u32[]{:S(2)}) collective-permute-start(bf16[192,1664]{1,0:T(8,128)(2,1)} %pad_maximum_fusion.3), channel_id=1, source_target_pairs={{0,4},{1,5},{2,6},{3,7},{4,0},{5,1},{6,2},{7,3},{8,12},{9,13},{10,... | collective-permute-start | bytes 1916936 | tf_op jit(solution)/shard_map/right1/ppermute | solution.py:101
  26.7 14.7 %copy-start.11 = (bf16[192,1664]{1,0:T(8,128)(2,1)}, bf16[192,1664]{1,0:T(8,128)(2,1)S(1)}, u32[]{:S(2)}) copy-start(bf16[192,1664]{1,0:T(8,128)(2,1)S(1)} %collective-permute-done.5) | copy-start | bytes 1916932
  42.6 32.1 %collective-permute-start.6 = (bf16[4,192,896]{2,1,0:T(8,128)(2,1)S(1)}, bf16[4,192,896]{2,1,0:T(8,128)(2,1)}, u32[]{:S(2)}, u32[]{:S(2)}) collective-permute-start(bf16[4,192,896]{2,1,0:T(8,128)(2,1)S(1)} %pad_maximum_fusion.1.rest_0_), channel_id=1, source_target_pairs={{0,1},{1,2},{2,3},{3,0},{4,5},{5,6},{6,7},{7,4},{8,9},{9,10},{10,1... | collective-permute-start | bytes 4128776 | tf_op jit(solution)/shard_map/up0/ppermute | solution.py:101
  44.4 29.7 %collective-permute-start.1 = (bf16[192,3072]{1,0:T(8,128)(2,1)}, bf16[192,3072]{1,0:T(8,128)(2,1)}, u32[]{:S(2)}, u32[]{:S(2)}) collective-permute-start(bf16[192,3072]{1,0:T(8,128)(2,1)} %get-tuple-element.39), channel_id=1, source_target_pairs={{0,8},{1,9},{2,10},{3,11},{4,12},{5,13},{6,14},{7,15},{8,0},{9,1},... | collective-permute-start | bytes 3538952 | tf_op jit(solution)/shard_map/left2/ppermute | solution.py:101
  47.4 29.2 %collective-permute-start.7 = (bf16[4,192,896]{2,1,0:T(8,128)(2,1)S(1)}, bf16[4,192,896]{2,1,0:T(8,128)(2,1)S(1)}, u32[]{:S(2)}, u32[]{:S(2)}) collective-permute-start(bf16[4,192,896]{2,1,0:T(8,128)(2,1)S(1)} %pad_maximum_fusion.1.rest_0_), channel_id=1, source_target_pairs={{0,3},{1,0},{2,1},{3,2},{4,7},{5,4},{6,5},{7,6},{8,11},{9,8},{10,9... | collective-permute-start | bytes 4128776 | tf_op jit(solution)/shard_map/down0/ppermute | solution.py:101
  74.7 23.0 %collective-permute-start.11 = (bf16[4,192,896]{2,1,0:T(8,128)(2,1)}, bf16[4,192,896]{2,1,0:T(8,128)(2,1)}, u32[]{:S(2)}, u32[]{:S(2)}) collective-permute-start(bf16[4,192,896]{2,1,0:T(8,128)(2,1)} %collective-permute-done.6.rest_1_), channel_id=1, source_target_pairs={{0,1},{1,2},{2,3},{3,0},{4,5},{5,6},{6,7},{7,4},{8,9},{9,10},{10,1... | collective-permute-start | bytes 4128776 | tf_op jit(solution)/shard_map/forward0/ppermute | solution.py:101
  76.6 1.1 copy-start
  77.6 16.3 %collective-permute-start.9 = (bf16[4,192,768]{2,1,0:T(8,128)(2,1)S(1)}, bf16[4,192,768]{2,1,0:T(8,128)(2,1)}, u32[]{:S(2)}, u32[]{:S(2)}) collective-permute-start(bf16[4,192,768]{2,1,0:T(8,128)(2,1)S(1)} %pad_maximum_fusion.2.rest_0_), channel_id=1, source_target_pairs={{0,3},{1,0},{2,1},{3,2},{4,7},{5,4},{6,5},{7,6},{8,11},{9,8},{10,9... | collective-permute-start | bytes 3538952 | tf_op jit(solution)/shard_map/down1/ppermute | solution.py:101
  80.3 17.4 %copy-start.1 = (bf16[4,192,896]{2,1,0:T(8,128)(2,1)S(1)}, bf16[4,192,896]{2,1,0:T(8,128)(2,1)}, u32[]{:S(2)}) copy-start(bf16[4,192,896]{2,1,0:T(8,128)(2,1)} %copy-done) | copy-start | bytes 4128772
  83.1 55.0 %collective-permute-start.8 = (bf16[4,192,768]{2,1,0:T(8,128)(2,1)S(1)}, bf16[4,192,768]{2,1,0:T(8,128)(2,1)S(1)}, u32[]{:S(2)}, u32[]{:S(2)}) collective-permute-start(bf16[4,192,768]{2,1,0:T(8,128)(2,1)S(1)} %pad_maximum_fusion.2.rest_0_), channel_id=1, source_target_pairs={{0,1},{1,2},{2,3},{3,0},{4,5},{5,6},{6,7},{7,4},{8,9},{9,10},{10,1... | collective-permute-start | bytes 3538952 | tf_op jit(solution)/shard_map/up1/ppermute | solution.py:101
  94.0 44.1 %collective-permute-start.10 = (bf16[4,192,768]{2,1,0:T(8,128)(2,1)}, bf16[4,192,768]{2,1,0:T(8,128)(2,1)S(1)}, u32[]{:S(2)}, u32[]{:S(2)}) collective-permute-start(bf16[4,192,768]{2,1,0:T(8,128)(2,1)} %collective-permute-done.9.rest_2_), channel_id=1, source_target_pairs={{0,3},{1,0},{2,1},{3,2},{4,7},{5,4},{6,5},{7,6},{8,11},{9,8},{10,9... | collective-permute-start | bytes 3538952 | tf_op jit(solution)/shard_map/forward1/ppermute | solution.py:101
  110.2 4.1 %collective-permute-start.18 = (f32[64,64]{1,0:T(8,128)S(1)}, f32[64,64]{1,0:T(8,128)S(1)}, u32[]{:S(2)}, u32[]{:S(2)}) collective-permute-start(f32[64,64]{1,0:T(8,128)S(1)} %fusion), channel_id=1, source_target_pairs={{0,1},{1,0},{2,3},{3,2},{4,5},{5,4},{6,7},{7,6},{8,9},{9,8},{10,11... | collective-permute-start | bytes 49160 | tf_op jit(solution)/shard_map/corner1/ppermute | solution.py:101
  114.3 5.8 %collective-permute-start.19 = (f32[64,64]{1,0:T(8,128)S(1)}, f32[64,64]{1,0:T(8,128)S(1)}, u32[]{:S(2)}, u32[]{:S(2)}) collective-permute-start(f32[64,64]{1,0:T(8,128)S(1)} %add.332), channel_id=1, source_target_pairs={{0,2},{1,3},{2,0},{3,1},{4,6},{5,7},{6,4},{7,5},{8,10},{9,11},{10,... | collective-permute-start | bytes 49160 | tf_op jit(solution)/shard_map/corner2/ppermute | solution.py:101
  114.4 10.1 %collective-permute-start.12 = (f32[192,768]{1,0:T(8,128)S(1)}, f32[192,768]{1,0:T(8,128)S(1)}, u32[]{:S(2)}, u32[]{:S(2)}) collective-permute-start(f32[192,768]{1,0:T(8,128)S(1)} %get-tuple-element.21), channel_id=1, source_target_pairs={{0,4},{1,5},{2,6},{3,7},{4,0},{5,1},{6,2},{7,3},{8,12},{9,13},{10,... | collective-permute-start | bytes 1769480 | tf_op jit(solution)/shard_map/back01/ppermute | solution.py:101
  116.5 17.2 %collective-permute-start.13 = (f32[192,768]{1,0:T(8,128)S(1)}, f32[192,768]{1,0:T(8,128)S(1)}, u32[]{:S(2)}, u32[]{:S(2)}) collective-permute-start(f32[192,768]{1,0:T(8,128)S(1)} %get-tuple-element.22), channel_id=1, source_target_pairs={{0,8},{1,9},{2,10},{3,11},{4,12},{5,13},{6,14},{7,15},{8,0},{9,1},... | collective-permute-start | bytes 1769480 | tf_op jit(solution)/shard_map/back02/ppermute | solution.py:101
  120.2 17.8 %collective-permute-start.14 = (f32[192,768]{1,0:T(8,128)S(1)}, f32[192,768]{1,0:T(8,128)S(1)}, u32[]{:S(2)}, u32[]{:S(2)}) collective-permute-start(f32[192,768]{1,0:T(8,128)S(1)} %get-tuple-element.23), channel_id=1, source_target_pairs={{0,12},{1,13},{2,14},{3,15},{4,8},{5,9},{6,10},{7,11},{8,4},{9,5},... | collective-permute-start | bytes 1769480 | tf_op jit(solution)/shard_map/back03/ppermute | solution.py:101
  124.5 26.4 %collective-permute-start.20 = (f32[64,64]{1,0:T(8,128)S(1)}, f32[64,64]{1,0:T(8,128)S(1)}, u32[]{:S(2)}, u32[]{:S(2)}) collective-permute-start(f32[64,64]{1,0:T(8,128)S(1)} %add.333), channel_id=1, source_target_pairs={{0,8},{1,9},{2,10},{3,11},{4,12},{5,13},{6,14},{7,15},{8,0},{9,1},... | collective-permute-start | bytes 49160 | tf_op jit(solution)/shard_map/beside/ppermute | solution.py:101
  138.0 7.4 %copy-start.2 = (f32[192,768]{1,0:T(8,128)}, f32[192,768]{1,0:T(8,128)S(1)}, u32[]{:S(2)}) copy-start(f32[192,768]{1,0:T(8,128)S(1)} %collective-permute-done.14.rest_3_) | copy-start | bytes 1769476
  145.4 0.8 copy-start.4
  146.2 22.6 %collective-permute-start.15 = (f32[192,768]{1,0:T(8,128)}, f32[192,768]{1,0:T(8,128)S(1)}, u32[]{:S(2)}, u32[]{:S(2)}) collective-permute-start(f32[192,768]{1,0:T(8,128)} %get-tuple-element.26), channel_id=1, source_target_pairs={{0,4},{1,5},{2,6},{3,7},{4,0},{5,1},{6,2},{7,3},{8,12},{9,13},{10,... | collective-permute-start | bytes 1769480 | tf_op jit(solution)/shard_map/back11/ppermute | solution.py:101
  146.8 22.0 %collective-permute-start.16 = (f32[192,768]{1,0:T(8,128)}, f32[192,768]{1,0:T(8,128)}, u32[]{:S(2)}, u32[]{:S(2)}) collective-permute-start(f32[192,768]{1,0:T(8,128)} %get-tuple-element.27), channel_id=1, source_target_pairs={{0,8},{1,9},{2,10},{3,11},{4,12},{5,13},{6,14},{7,15},{8,0},{9,1},... | collective-permute-start | bytes 1769480 | tf_op jit(solution)/shard_map/back12/ppermute | solution.py:101
  149.8 19.0 %collective-permute-start.17 = (f32[192,768]{1,0:T(8,128)}, f32[192,768]{1,0:T(8,128)}, u32[]{:S(2)}, u32[]{:S(2)}) collective-permute-start(f32[192,768]{1,0:T(8,128)} %get-tuple-element.28), channel_id=1, source_target_pairs={{0,12},{1,13},{2,14},{3,15},{4,8},{5,9},{6,10},{7,11},{8,4},{9,5},... | collective-permute-start | bytes 1769480 | tf_op jit(solution)/shard_map/back13/ppermute | solution.py:101
  152.2 1.2 collective-permute-start.21
  154.0 3.7 %collective-permute-start.22 = (f32[8,128]{1,0:T(8,128)S(1)}, f32[8,128]{1,0:T(8,128)S(1)}, u32[]{:S(2)}, u32[]{:S(2)}) collective-permute-start(f32[8,128]{1,0:T(8,128)S(1)} %broadcast_add_fusion), channel_id=1, source_target_pairs={{0,32},{1,33},{2,34},{3,35},{4,36},{5,37},{6,38},{7,39},{8,40},{9,... | collective-permute-start | bytes 12296 | tf_op jit(solution)/shard_map/total2/ppermute | solution.py:101
  158.4 5.5 %collective-permute-start.23 = (f32[8,128]{1,0:T(8,128)S(1)}, f32[8,128]{1,0:T(8,128)S(1)}, u32[]{:S(2)}, u32[]{:S(2)}) collective-permute-start(f32[8,128]{1,0:T(8,128)S(1)} %fusion.36), channel_id=1, source_target_pairs={{0,64},{1,65},{2,66},{3,67},{4,68},{5,69},{6,70},{7,71},{8,72},{9,... | collective-permute-start | bytes 12296 | tf_op jit(solution)/shard_map/total4/ppermute | solution.py:101
  165.8 1.1 copy-start.3
  166.8 2.0 %copy-start.5 = (f32[192,768]{1,0:T(8,128)S(1)}, f32[192,768]{1,0:T(8,128)}, u32[]{:S(2)}) copy-start(f32[192,768]{1,0:T(8,128)} %copy-done.4) | copy-start | bytes 1769476

commit v3 on v2

v3 whole, which is shorter than its diff:
```python
import jax
import jax.numpy as jnp
from jax import lax
from jax.experimental import pallas as pl
from jax.experimental.pallas import tpu as pltpu
from jax.sharding import PartitionSpec as P

SIDE = 4


def start_gather(refs, where, off, scratch, sems, rows, at, sides):
    copies = []
    for k, (first, last) in enumerate(sides):
        column = []
        for n, (i, p) in enumerate(where):
            into = scratch.at[pl.ds(pl.multiple_of(off[n], 64), rows), first:last]
            source = refs[i].at[p, :, at[i] + first:at[i] + last]
            column.append(pltpu.make_async_copy(source, into, sems.at[k, n]))
        copies.append(column)
    for column in copies:
        for copy in column:
            copy.start()
    return copies


def product(offsets, lefts, pieces, at, width):
    rows, depth = lefts[0].shape
    middle = width // 256 * 128
    sides = ((0, middle), (middle, width))
    where = [(i, p) for i, piece in enumerate(pieces) for p in range(piece.shape[0])]
    n_left = len(lefts)

    def kernel(off, *rest):
        ls, refs, outs = rest[:n_left], rest[n_left:n_left + len(pieces)], rest[n_left + len(pieces):-4]
        lhs, scratch, left_sems, sems = rest[-4:]
        loads = [pltpu.make_async_copy(ls[p], lhs.at[pl.ds(p * rows, rows)], left_sems.at[p]) for p in range(n_left)]
        for copy in loads:
            copy.start()
        copies = start_gather(refs, where, off, scratch, sems, rows, at, sides)
        for copy in loads:
            copy.wait()
        for column, (first, last) in zip(copies, sides):
            for copy in column:
                copy.wait()
            got = jnp.dot(lhs[...], scratch[:, first:last], preferred_element_type=jnp.float32)
            for p in range(n_left):
                outs[p][:, first:last] = got[p * rows:(p + 1) * rows]

    outside = pl.BlockSpec(memory_space=pltpu.HBM)
    inside = pl.BlockSpec(memory_space=pltpu.VMEM)
    return pl.pallas_call(
        kernel,
        in_specs=[pl.BlockSpec(memory_space=pltpu.SMEM)] + [outside] * (n_left + len(pieces)),
        out_specs=[inside] * n_left,
        out_shape=[jax.ShapeDtypeStruct((rows, width), jnp.float32)] * n_left,
        scratch_shapes=[
            pltpu.VMEM((n_left * rows, depth), jnp.bfloat16),
            pltpu.VMEM((depth, width), jnp.bfloat16),
            pltpu.SemaphoreType.DMA((n_left,)),
            pltpu.SemaphoreType.DMA((2, len(where))),
        ],
        cost_estimate=pl.CostEstimate(
            flops=2 * n_left * rows * depth * width,
            bytes_accessed=2 * depth * (n_left * rows + width) + 4 * n_left * rows * width,
            transcendentals=0,
        ),
        compiler_params=pltpu.CompilerParams(vmem_limit_bytes=56 << 20),
    )(offsets, *lefts, *pieces)


def share(offsets, lefts, chosen, pieces, extra):
    rows, depth = lefts[0].shape
    kept = extra // 2
    n_left = len(lefts)
    where = [(i, p) for i, piece in enumerate(pieces) for p in range(piece.shape[0])]

    def kernel(off, pick, *rest):
        ls, refs = rest[:n_left], rest[n_left:n_left + len(pieces)]
        out, lhs, scratch, left_sems, sems = rest[-5:]
        loads = [pltpu.make_async_copy(ls[p], lhs.at[pl.ds(p * rows, rows)], left_sems.at[p]) for p in range(n_left)]
        for copy in loads:
            copy.start()
        copies = start_gather(refs, where, off, scratch, sems, rows, [0] * len(pieces), ((0, extra),))
        for copy in loads + copies[0]:
            copy.wait()
        got = jnp.dot(lhs[...], scratch[...], preferred_element_type=jnp.float32)
        inner = got[:, :kept] + got[:, kept:]
        terms = []
        for p in range(n_left):
            left_over, term = inner[p * rows:(p + 1) * rows], None
            for _ in range(3):
                digit = left_over.astype(jnp.bfloat16)
                left_over = left_over - digit.astype(jnp.float32)
                part = jnp.dot(pick[p], digit, preferred_element_type=jnp.float32)
                term = part if term is None else term + part
            terms.append(term)
        out[...] = (terms[0] + terms[1]) + (terms[2] + terms[3])

    outside = pl.BlockSpec(memory_space=pltpu.HBM)
    inside = pl.BlockSpec(memory_space=pltpu.VMEM)
    return pl.pallas_call(
        kernel,
        in_specs=[pl.BlockSpec(memory_space=pltpu.SMEM), inside] + [outside] * (n_left + len(pieces)),
        out_specs=inside,
        out_shape=jax.ShapeDtypeStruct((kept, kept), jnp.float32),
        scratch_shapes=[
            pltpu.VMEM((n_left * rows, depth), jnp.bfloat16),
            pltpu.VMEM((depth, extra), jnp.bfloat16),
            pltpu.SemaphoreType.DMA((n_left,)),
            pltpu.SemaphoreType.DMA((1, len(where))),
        ],
        cost_estimate=pl.CostEstimate(
            flops=2 * n_left * rows * depth * extra,
            bytes_accessed=2 * depth * (n_left * rows + extra),
            transcendentals=0,
        ),
        compiler_params=pltpu.CompilerParams(vmem_limit_bytes=56 << 20),
    )(offsets, chosen, *lefts, *pieces)


def place(spots, blocks, shape, into=None):
    rows, width = blocks[0].shape
    n = len(blocks)

    def kernel(at, *rest):
        out, sems = rest[-2:]
        copies = []
        for k in range(n):
            start = pl.multiple_of(at[n + k], 128)
            copies.append(pltpu.make_async_copy(rest[k], out.at[at[k], :, pl.ds(start, width)], sems.at[k]))
        for copy in copies:
            copy.start()
        for copy in copies:
            copy.wait()

    anywhere = pl.BlockSpec(memory_space=pl.ANY)
    inside = pl.BlockSpec(memory_space=pltpu.VMEM)
    given = list(blocks) + ([] if into is None else [into])
    return pl.pallas_call(
        kernel,
        in_specs=[pl.BlockSpec(memory_space=pltpu.SMEM)] + [inside] * n + [anywhere] * (len(given) - n),
        out_specs=anywhere,
        out_shape=jax.ShapeDtypeStruct(shape, jnp.float32),
        scratch_shapes=[pltpu.SemaphoreType.DMA((n,))],
        input_output_aliases={} if into is None else {n + 1: 0},
        compiler_params=pltpu.CompilerParams(vmem_limit_bytes=8 << 20),
    )(spots, *given)


def solution(mesh):
    n_row, n_col = mesh.shape["row"], mesh.shape["col"]

    def pairs(move):
        found = []
        for row in range(n_row):
            for col in range(n_col):
                cx, cy = col // SIDE, col % SIDE
                g, h = (cy, cx) if row % 2 else (cx, cy)
                to, g, h = move(row, g, h)
                cx, cy = (h, g) if row % 2 else (g, h)
                if to != row:
                    cx, cy = col // SIDE, col % SIDE
                found.append((row * n_col + col, to * n_col + cx * SIDE + cy))
        return found

    along_g = {p: pairs(lambda row, g, h, p=p: (row, g ^ p, h)) for p in (1, 2, 3)}
    along_h = {p: pairs(lambda row, g, h, p=p: (row, g, h ^ p)) for p in (1, 2)}
    up = pairs(lambda row, g, h: (row, g, (h + 1) % SIDE))
    down = pairs(lambda row, g, h: (row, g, (h - 1) % SIDE))
    across_h = pairs(lambda row, g, h: (row, g, (h + 2) % SIDE))
    across = {p: pairs(lambda row, g, h, p=p: (row ^ p, g, h)) for p in (1, 2, 4)}

    def send(value, table, name):
        with jax.named_scope(name):
            return lax.ppermute(value, ("row", "col"), table)

    def after(value, *others):
        return lax.optimization_barrier((value, *others))[0]

    def body(left_edge, right_edge, projector, sector_size):
        count, rows, depth = left_edge.shape
        kept = projector.shape[2]
        half = depth // 2
        width = half // 2
        odd = lax.axis_index("row") % 2
        col = lax.axis_index("col")
        cx, cy = col // SIDE, col % SIDE
        g = jnp.where(odd == 1, cy, cx)
        h = jnp.where(odd == 1, cx, cy)
        owner = lambda gg, hh: jnp.where(odd == 1, hh * SIDE + gg, gg * SIDE + hh)

        states = jnp.arange(depth, dtype=jnp.int32)
        live = (states[None, :] < sector_size[:, None]).astype(jnp.bfloat16)
        masked = projector * live[:, :, None]

        sector = g // 2
        mine = lax.dynamic_index_in_dim(left_edge, sector, 0, keepdims=False)
        other = lax.dynamic_index_in_dim(left_edge, 1 - sector, 0, keepdims=False)

        right_edge = after(right_edge, mine, other)
        seen = jnp.einsum("skj,sjq->skq", right_edge, masked, preferred_element_type=jnp.float32)
        top = lax.reduce_precision(seen, exponent_bits=8, mantissa_bits=7)
        shadow = jnp.concatenate([top, seen - top], axis=2).astype(jnp.bfloat16)

        def part(p):
            to = g ^ p
            got = lax.dynamic_slice(right_edge, (to // 2, 0, (to % 2) * half), (1, rows, half))[0]
            return jnp.concatenate([lax.dynamic_index_in_dim(shadow, to // 2, 0, keepdims=False), got], axis=1)

        gs = [g ^ p for p in range(SIDE)]
        hs = [h, (h - 1) % SIDE, (h + 1) % SIDE, (h + 2) % SIDE]
        offsets = jnp.stack([owner(gg, hh) * rows for hh in hs for gg in gs]).astype(jnp.int32)

        left = [mine] + [send(mine if p == 1 else other, along_g[p], f"left{p}") for p in (1, 2, 3)]
        blocks = [part(0)] + [send(part(p), along_g[p], f"right{p}") for p in (1, 2, 3)]

        extra = 2 * kept

        def cut(c):
            first = extra + width if c else 0
            return jnp.stack([block[:, first:extra + (c + 1) * width] for block in blocks])

        def put(c, out, into):
            first = c * width
            spots = jnp.stack([gg // 2 for gg in gs] + [(gg % 2) * half + first for gg in gs]).astype(jnp.int32)
            return place(spots, out, (count, rows, depth), into)

        def back(c, out):
            return [out[0]] + [send(out[p], along_g[p], f"back{c}{p}") for p in (1, 2, 3)]

        ours = lax.dynamic_index_in_dim(masked, sector, 0, keepdims=False)
        chosen = jnp.stack([lax.dynamic_slice_in_dim(ours, owner(gg, h) * rows, rows, 0).T for gg in gs])

        shade = jnp.stack([block[:, :extra] for block in blocks])
        own0 = after(cut(0), left[1], left[3])
        far = send(shade, across_h, "shade")
        below0, above0 = send(own0, up, "up0"), send(own0, down, "down0")
        below0, above0, far, left[2] = lax.optimization_barrier((below0, above0, far, left[2]))
        own1 = cut(1)
        beyond0 = send(below0, up, "forward0")
        above1 = send(after(own1, above0), down, "down1")
        corner = share(offsets, left, chosen, (own0, below0, above0, far), extra)
        corner = corner + send(corner, along_h[1], "corner1")
        beyond0, above1, corner = lax.optimization_barrier((beyond0, above1, corner))
        below1 = send(after(own1, beyond0), up, "up1")
        beyond1 = send(above1, down, "forward1")
        corner = corner + send(corner, along_h[2], "corner2")
        skips = (extra,) * 4
        out0 = product(offsets, left, (own0, below0, above0, beyond0), skips, width)
        out0, corner = lax.optimization_barrier((out0, corner))
        out0 = back(0, out0)
        beside = send(corner, along_g[2], "beside")
        out1 = product(offsets, left, (own1, below1, above1, beyond1), (0,) * 4, width)
        out1, out0, beside = lax.optimization_barrier((out1, out0, beside))
        out1 = back(1, out1)
        enlarged = put(1, out1, put(0, out0, None))
        corner = jnp.where(sector == 0, jnp.stack([corner, beside]), jnp.stack([beside, corner]))
        total = jnp.broadcast_to(jnp.sum(corner * corner), (8, 128))
        for p in (1, 2, 4):
            total = total + send(total, across[p], f"total{p}")
        entries = n_row * count * kept * kept
        return enlarged, corner * lax.rsqrt(total[0, 0] / entries + 1e-06)

    placed = (P("row", "col", None), P("row", "col", None), P("row", None, None), P("row"))
    return jax.shard_map(
        body,
        mesh=mesh,
        in_specs=placed,
        out_specs=(P("row", "col", None), P("row", None, None)),
        check_vma=False,
    )
```

time: 172 us -> 151 us (0.88)
  waiting for transfers between devices: 75.3 us -> 52.4 us
  Pallas kernels: 20.1 us -> 33.5 us
  matrix products: 7.18 us -> 1.58 us
  local copies, waits for them, and re-layouts: 14 us -> 10.9 us
  starting transfers between devices: 42.6 us -> 40.7 us
    ppermute x24 -> x25, waiting for transfers between devices: 75.3 us -> 52.4 us  [send(): return lax.ppermute(value, ('row', 'col'), table)]
    pallas_call x2 -> x3, Pallas kernels: 15.5 us -> 29 us  [the longest x2 22.7 us: product(): pl.pallas_call(kernel, in_specs=[pl.BlockSpec(memory_space=pltpu.SMEM)] +...]
    another operation x7, local copies, waits for them, and re-layouts: 5.2 us -> 0.17 us  [cut(): jnp.stack([block[:, first:extra + (c + 1) * width] for block in blocks])]
    dot_general x4 -> x0, matrix products: 4.32 us -> none  [body(): jnp.einsum('ip,iq->pq', chosen, inner[p], precision=lax.Precision.HIGHEST)]
    dynamic_slice x5 -> x0, local copies, waits for them, and re-layouts: 3.27 us -> none  [the longest x1 2.85 us: body(): mine = lax.dynamic_index_in_dim(left_edge, sector, 0, keepdims=False)]
    squeeze x0 -> x1, local copies, waits for them, and re-layouts: none -> 2.96 us  [body(): other = lax.dynamic_index_in_dim(left_edge, 1 - sector, 0, keepdims=False)]
    concatenate x3, other arithmetic: 2.76 us -> 0.16 us  [part(): jnp.concatenate([lax.dynamic_index_in_dim(shadow, to // 2, 0, keepdims=Fa...]
    ppermute x24 -> x25, starting transfers between devices: 42.6 us -> 40.7 us  [send(): return lax.ppermute(value, ('row', 'col'), table)]
  transfers between devices with their start and end apart: 24 -> 25, of which waited for: 13 -> 11; matrix products, arithmetic and copies ran while one was open for 13% -> 12% of each run, Pallas kernels for 10% -> 21%
where the time goes in v3:
time: 151 us; the launch traced here: 150 us
  waiting for transfers between devices  52.4 us (35%)
  starting transfers between devices  40.7 us (27%)
  Pallas kernels  33.5 us (22%)
  local copies, waits for them, and re-layouts  10.9 us (7%)
  other arithmetic  9.28 us (6%)
  between operations  1.98 us (1%)
  matrix products  1.58 us (1%)
    ppermute x25, waiting for transfers between devices, send(): return lax.ppermute(value, ('row', 'col'), table)  52.4 us
    ppermute x25, starting transfers between devices, send(): return lax.ppermute(value, ('row', 'col'), table)  40.7 us
    pallas_call x2, Pallas kernels, product(): pl.pallas_call(kernel, in_specs=[pl.BlockSpec(memory_space=pltpu.SMEM)] +...  22.7 us
    pallas_call x1, Pallas kernels, share(): pl.pallas_call(kernel, in_specs=[pl.BlockSpec(memory_space=pltpu.SMEM), i...  6.3 us
    pallas_call x2, Pallas kernels, place(): pl.pallas_call(kernel, in_specs=[pl.BlockSpec(memory_space=pltpu.SMEM)] +...  4.49 us
  transfers between devices with their start and end apart: 25, of which 11 were waited for; matrix products, arithmetic and copies ran while one was open for 12% of the time, Pallas kernels for 21%

profile of v3, /device:TPU:0, one launch (start us, length us, event | category | flops | bytes accessed | tf_op | source)
XLA Modules:
  0.0 150.3 jit_solution(9133832809232348746)
XLA Ops:
  0.7 3.0 %dynamic-slice_bitcast_fusion = (bf16[192,3072]{1,0:T(8,128)(2,1)}, bf16[192,3072]{1,0:T(8,128)(2,1)S(1)}) fusion(bf16[2,192,3072]{2,1,0:T(8,128)(2,1)} %param.4, s32[]{:T(128)S(6)} %select_n.241, s32[]{:T(128)S(6)} %select_n.240), kind=kLoop, calls=%fused_computation.2 | loop fusion | bytes 4718600 | tf_op jit(solution)/shard_map/jit(dynamic_index_in_dim)/squeeze | solution.py:198
  3.7 2.8 %collective-permute-start.4 = (bf16[192,3072]{1,0:T(8,128)(2,1)}, bf16[192,3072]{1,0:T(8,128)(2,1)}, u32[]{:S(2)}, u32[]{:S(2)}) collective-permute-start(bf16[192,3072]{1,0:T(8,128)(2,1)} %get-tuple-element.72), channel_id=1, source_target_pairs={{0,12},{1,13},{2,14},{3,15},{4,8},{5,9},{6,10},{7,11},{8,4},{9,5},... | collective-permute-start | bytes 3538952 | tf_op jit(solution)/shard_map/left3/ppermute | solution.py:175
  6.5 0.2 collective-permute-start
  6.8 0.1 compare_convert_fusion
  6.8 1.2 broadcast_multiply_fusion
  8.1 1.6 %fusion.9 = (f32[2,192,64]{1,2,0:T(8,128)}, f32[2,192,64]{1,2,0:T(8,128)}) fusion(bf16[2,192,3072]{2,1,0:T(8,128)(2,1)S(1)} %copy-done.2, bf16[2,3072,64]{1,2,0:T(8,128)(2,1)S(1)} %broadcast_multiply_fusion), kind=kOutput, calls=%fused_computation.51 | convolution fusion | flops 151019520 | bytes 3342336 | tf_op jit(solution)/shard_map/skj,sjq->skq/dot_general | solution.py:201
  9.6 1.7 %copy.9 = f32[2,192,64]{2,1,0:T(8,128)} copy(f32[2,192,64]{1,2,0:T(8,128)} %get-tuple-element.84) | data formatting | bytes 196608 | tf_op jit(solution)/shard_map/reduce_precision | solution.py:202
  11.3 1.7 %copy.10 = f32[2,192,64]{2,1,0:T(8,128)} copy(f32[2,192,64]{1,2,0:T(8,128)} %get-tuple-element.85) | data formatting | bytes 196608 | tf_op jit(solution)/shard_map/skj,sjq->skq/dot_general | solution.py:201
  13.0 1.1 subtract_convert_fusion
  14.2 0.1 fusion.3
  14.3 0.2 dynamic-slice_bitcast_fusion.5
  14.5 0.1 pad_maximum_fusion.2
  14.6 1.9 %collective-permute-start.1 = (bf16[192,1664]{1,0:T(8,128)(2,1)S(1)}, bf16[192,1664]{1,0:T(8,128)(2,1)S(1)}, u32[]{:S(2)}, u32[]{:S(2)}) collective-permute-start(bf16[192,1664]{1,0:T(8,128)(2,1)S(1)} %pad_maximum_fusion.2), channel_id=1, source_target_pairs={{0,4},{1,5},{2,6},{3,7},{4,0},{5,1},{6,2},{7,3},{8,12},{9,13},{10,... | collective-permute-start | bytes 1916936 | tf_op jit(solution)/shard_map/right1/ppermute | solution.py:175
  16.5 0.1 pad_maximum_fusion.3
  16.5 0.9 collective-permute-start.2
  17.5 2.2 %collective-permute-start.3 = (bf16[192,1664]{1,0:T(8,128)(2,1)S(1)}, bf16[192,1664]{1,0:T(8,128)(2,1)S(1)}, u32[]{:S(2)}, u32[]{:S(2)}) collective-permute-start(bf16[192,1664]{1,0:T(8,128)(2,1)S(1)} %pad_maximum_fusion.4), channel_id=1, source_target_pairs={{0,12},{1,13},{2,14},{3,15},{4,8},{5,9},{6,10},{7,11},{8,4},{9,5},... | collective-permute-start | bytes 1916936 | tf_op jit(solution)/shard_map/right3/ppermute | solution.py:175
  19.7 9.9 %collective-permute-done.1 = bf16[192,1664]{1,0:T(8,128)(2,1)S(1)} collective-permute-done((bf16[192,1664]{1,0:T(8,128)(2,1)S(1)}, bf16[192,1664]{1,0:T(8,128)(2,1)S(1)}, u32[]{:S(2)}, u32[]{:S(2)}) %collective-permute-start.1) | collective-permute-done | bytes 639008 | tf_op jit(solution)/shard_map/right1/ppermute | solution.py:175
  29.6 0.8 collective-permute-start.8
  30.4 5.8 %collective-permute-done.2 = bf16[192,1664]{1,0:T(8,128)(2,1)S(1)} collective-permute-done((bf16[192,1664]{1,0:T(8,128)(2,1)S(1)}, bf16[192,1664]{1,0:T(8,128)(2,1)S(1)}, u32[]{:S(2)}, u32[]{:S(2)}) %collective-permute-start.2) | collective-permute-done | bytes 639008 | tf_op jit(solution)/shard_map/right2/ppermute | solution.py:175
  36.3 0.2 pad_maximum_fusion.rest_4_
  36.6 3.2 %collective-permute-start.6 = (bf16[4,192,896]{2,1,0:T(8,128)(2,1)S(1)}, bf16[4,192,896]{2,1,0:T(8,128)(2,1)S(1)}, u32[]{:S(2)}, u32[]{:S(2)}) collective-permute-start(bf16[4,192,896]{2,1,0:T(8,128)(2,1)S(1)} %pad_maximum_fusion.rest_4_), channel_id=1, source_target_pairs={{0,3},{1,0},{2,1},{3,2},{4,7},{5,4},{6,5},{7,6},{8,11},{9,8},{10,9... | collective-permute-start | bytes 4128776 | tf_op jit(solution)/shard_map/down0/ppermute | solution.py:175
  39.9 2.3 %collective-permute-start.7 = (bf16[4,192,128]{2,1,0:T(8,128)(2,1)S(1)}, bf16[4,192,128]{2,1,0:T(8,128)(2,1)S(1)}, u32[]{:S(2)}, u32[]{:S(2)}) collective-permute-start(bf16[4,192,128]{2,1,0:T(8,128)(2,1)S(1)} %pad_maximum_fusion.6), channel_id=1, source_target_pairs={{0,2},{1,3},{2,0},{3,1},{4,6},{5,7},{6,4},{7,5},{8,10},{9,11},{10,... | collective-permute-start | bytes 589832 | tf_op jit(solution)/shard_map/shade/ppermute | solution.py:175
  42.2 22.4 %collective-permute-done.7.rest_7_ = bf16[4,192,128]{2,1,0:T(8,128)(2,1)S(1)} collective-permute-done((bf16[4,192,128]{2,1,0:T(8,128)(2,1)S(1)}, bf16[4,192,128]{2,1,0:T(8,128)(2,1)S(1)}, u32[]{:S(2)}, u32[]{:S(2)}) %collective-permute-start.7) | collective-permute-done | bytes 196640 | tf_op jit(solution)/shard_map/shade/ppermute | solution.py:175
  64.6 0.5 collective-permute-done.5.rest_5_
  65.1 1.4 pad_maximum_fusion.1.rest_4_
  66.5 3.2 %collective-permute-start.10 = (bf16[4,192,768]{2,1,0:T(8,128)(2,1)}, bf16[4,192,768]{2,1,0:T(8,128)(2,1)S(1)}, u32[]{:S(2)}, u32[]{:S(2)}) collective-permute-start(bf16[4,192,768]{2,1,0:T(8,128)(2,1)} %pad_maximum_fusion.1.rest_4_), channel_id=1, source_target_pairs={{0,3},{1,0},{2,1},{3,2},{4,7},{5,4},{6,5},{7,6},{8,11},{9,8},{10,9... | collective-permute-start | bytes 3538952 | tf_op jit(solution)/shard_map/down1/ppermute | solution.py:175
  69.7 0.7 stack.194.off
  70.4 1.0 dynamic-slice_bitcast_fusion.9
  71.4 0.7 pad_maximum_fusion.7.pick
  72.1 6.3 %shard_map.59 = f32[64,64]{1,0:T(8,128)} custom-call(s32[16]{0:T(128)} %stack.194.off, bf16[4,64,192]{2,1,0:T(8,128)(2,1)} %pad_maximum_fusion.7.pick, bf16[192,3072]{1,0:T(8,128)(2,1)} %copy-done.4, bf16[192,3072]{1,0:T(8,128)(2,1)} %collective-permute-done.rest_1_, bf16[192,3072]{1,0:T(8,128)(2,1)} %copy-done.7, ...), custom_call_target="tpu_custom_call" | custom-call | flops 603979776 | bytes 5505024 | tf_op jit(solution)/shard_map/pallas_call | solution.py:101
  78.4 0.1 collective-permute-start.11
  78.5 4.8 %collective-permute-done.11 = f32[64,64]{1,0:T(8,128)S(1)} collective-permute-done((f32[64,64]{1,0:T(8,128)}, f32[64,64]{1,0:T(8,128)S(1)}, u32[]{:S(2)}, u32[]{:S(2)}) %collective-permute-start.11) | collective-permute-done | bytes 16416 | tf_op jit(solution)/shard_map/corner1/ppermute | solution.py:175
  83.3 0.8 add.304
  84.1 0.7 collective-permute-done.9.rest_7_
  84.8 0.6 collective-permute-start.12
  85.4 2.6 %collective-permute-start.13 = (bf16[4,192,768]{2,1,0:T(8,128)(2,1)S(1)}, bf16[4,192,768]{2,1,0:T(8,128)(2,1)S(1)}, u32[]{:S(2)}, u32[]{:S(2)}) collective-permute-start(bf16[4,192,768]{2,1,0:T(8,128)(2,1)S(1)} %collective-permute-done.10.rest_6_), channel_id=1, source_target_pairs={{0,3},{1,0},{2,1},{3,2},{4,7},{5,4},{6,5},{7,6},{8,11},{9,8},{10,9... | collective-permute-start | bytes 3538952 | tf_op jit(solution)/shard_map/forward1/ppermute | solution.py:175
  88.0 2.6 %collective-permute-start.14 = (f32[64,64]{1,0:T(8,128)S(1)}, f32[64,64]{1,0:T(8,128)S(1)}, u32[]{:S(2)}, u32[]{:S(2)}) collective-permute-start(f32[64,64]{1,0:T(8,128)S(1)} %add.304), channel_id=1, source_target_pairs={{0,2},{1,3},{2,0},{3,1},{4,6},{5,7},{6,4},{7,5},{8,10},{9,11},{10,... | collective-permute-start | bytes 49160 | tf_op jit(solution)/shard_map/corner2/ppermute | solution.py:175
  90.6 11.4 %shard_map.61 = (f32[192,768]{1,0:T(8,128)}, f32[192,768]{1,0:T(8,128)}, f32[192,768]{1,0:T(8,128)}, f32[192,768]{1,0:T(8,128)}) custom-call(s32[16]{0:T(128)} %stack.194.off, bf16[192,3072]{1,0:T(8,128)(2,1)} %copy-done.4, bf16[192,3072]{1,0:T(8,128)(2,1)} %collective-permute-done.rest_1_, bf16[192,3072]{1,0:T(8,128)(2,1)} %copy-done.7, ...), custom_call_target="tpu_custom_call" | custom-call | flops 3623878656 | bytes 11796480 | tf_op jit(solution)/shard_map/pallas_call | solution.py:51
  102.1 2.1 %collective-permute-done.14 = f32[64,64]{1,0:T(8,128)S(1)} collective-permute-done((f32[64,64]{1,0:T(8,128)S(1)}, f32[64,64]{1,0:T(8,128)S(1)}, u32[]{:S(2)}, u32[]{:S(2)}) %collective-permute-start.14) | collective-permute-done | bytes 16416 | tf_op jit(solution)/shard_map/corner2/ppermute | solution.py:175
  104.2 1.5 %collective-permute-start.15 = (f32[192,768]{1,0:T(8,128)}, f32[192,768]{1,0:T(8,128)S(1)}, u32[]{:S(2)}, u32[]{:S(2)}) collective-permute-start(f32[192,768]{1,0:T(8,128)} %get-tuple-element.55), channel_id=1, source_target_pairs={{0,4},{1,5},{2,6},{3,7},{4,0},{5,1},{6,2},{7,3},{8,12},{9,13},{10,... | collective-permute-start | bytes 1769480 | tf_op jit(solution)/shard_map/back01/ppermute | solution.py:175
  105.7 2.7 %collective-permute-start.16 = (f32[192,768]{1,0:T(8,128)}, f32[192,768]{1,0:T(8,128)S(1)}, u32[]{:S(2)}, u32[]{:S(2)}) collective-permute-start(f32[192,768]{1,0:T(8,128)} %get-tuple-element.56), channel_id=1, source_target_pairs={{0,8},{1,9},{2,10},{3,11},{4,12},{5,13},{6,14},{7,15},{8,0},{9,1},... | collective-permute-start | bytes 1769480 | tf_op jit(solution)/shard_map/back02/ppermute | solution.py:175
  108.4 0.5 collective-permute-start.17
  109.0 1.8 %collective-permute-start.18 = (f32[64,64]{1,0:T(8,128)S(1)}, f32[64,64]{1,0:T(8,128)S(1)}, u32[]{:S(2)}, u32[]{:S(2)}) collective-permute-start(f32[64,64]{1,0:T(8,128)S(1)} %add.305), channel_id=1, source_target_pairs={{0,8},{1,9},{2,10},{3,11},{4,12},{5,13},{6,14},{7,15},{8,0},{9,1},... | collective-permute-start | bytes 49160 | tf_op jit(solution)/shard_map/beside/ppermute | solution.py:175
  110.7 1.0 copy-done.17
  111.8 11.3 %shard_map.60 = (f32[192,768]{1,0:T(8,128)}, f32[192,768]{1,0:T(8,128)}, f32[192,768]{1,0:T(8,128)}, f32[192,768]{1,0:T(8,128)}) custom-call(s32[16]{0:T(128)} %stack.194.off, bf16[192,3072]{1,0:T(8,128)(2,1)} %copy-done.4, bf16[192,3072]{1,0:T(8,128)(2,1)} %collective-permute-done.rest_1_, bf16[192,3072]{1,0:T(8,128)(2,1)} %copy-done.7, ...), custom_call_target="tpu_custom_call" | custom-call | flops 3623878656 | bytes 11796480 | tf_op jit(solution)/shard_map/pallas_call | solution.py:51
  123.1 0.2 collective-permute-done.18
  123.3 3.1 %collective-permute-done.17.rest_3_ = f32[192,768]{1,0:T(8,128)S(1)} collective-permute-done((f32[192,768]{1,0:T(8,128)}, f32[192,768]{1,0:T(8,128)S(1)}, u32[]{:S(2)}, u32[]{:S(2)}) %collective-permute-start.17) | collective-permute-done | bytes 589856 | tf_op jit(solution)/shard_map/back03/ppermute | solution.py:175
  126.4 2.0 %collective-permute-start.20 = (f32[192,768]{1,0:T(8,128)}, f32[192,768]{1,0:T(8,128)S(1)}, u32[]{:S(2)}, u32[]{:S(2)}) collective-permute-start(f32[192,768]{1,0:T(8,128)} %get-tuple-element.61), channel_id=1, source_target_pairs={{0,8},{1,9},{2,10},{3,11},{4,12},{5,13},{6,14},{7,15},{8,0},{9,1},... | collective-permute-start | bytes 1769480 | tf_op jit(solution)/shard_map/back12/ppermute | solution.py:175
  128.4 2.7 %collective-permute-start.21 = (f32[192,768]{1,0:T(8,128)}, f32[192,768]{1,0:T(8,128)}, u32[]{:S(2)}, u32[]{:S(2)}) collective-permute-start(f32[192,768]{1,0:T(8,128)} %get-tuple-element.62), channel_id=1, source_target_pairs={{0,12},{1,13},{2,14},{3,15},{4,8},{5,9},{6,10},{7,11},{8,4},{9,5},... | collective-permute-start | bytes 1769480 | tf_op jit(solution)/shard_map/back13/ppermute | solution.py:175
  131.1 1.5 multiply_reduce_fusion
  132.6 0.6 broadcast_in_dim.2
  133.3 0.1 collective-permute-start.22
  133.3 1.2 collective-permute-done.22
  134.5 0.6 broadcast_add_fusion
  135.2 2.0 %collective-permute-start.23 = (f32[8,128]{1,0:T(8,128)S(1)}, f32[8,128]{1,0:T(8,128)S(1)}, u32[]{:S(2)}, u32[]{:S(2)}) collective-permute-start(f32[8,128]{1,0:T(8,128)S(1)} %broadcast_add_fusion), channel_id=1, source_target_pairs={{0,32},{1,33},{2,34},{3,35},{4,36},{5,37},{6,38},{7,39},{8,40},{9,... | collective-permute-start | bytes 12296 | tf_op jit(solution)/shard_map/total2/ppermute | solution.py:175
  137.2 1.7 %collective-permute-done.23 = f32[8,128]{1,0:T(8,128)S(1)} collective-permute-done((f32[8,128]{1,0:T(8,128)S(1)}, f32[8,128]{1,0:T(8,128)S(1)}, u32[]{:S(2)}, u32[]{:S(2)}) %collective-permute-start.23) | collective-permute-done | bytes 4128 | tf_op jit(solution)/shard_map/total2/ppermute | solution.py:175
  138.8 0.6 fusion.12
  139.5 4.0 %collective-permute-start.24 = (f32[8,128]{1,0:T(8,128)S(1)}, f32[8,128]{1,0:T(8,128)S(1)}, u32[]{:S(2)}, u32[]{:S(2)}) collective-permute-start(f32[8,128]{1,0:T(8,128)S(1)} %fusion.12), channel_id=1, source_target_pairs={{0,64},{1,65},{2,66},{3,67},{4,68},{5,69},{6,70},{7,71},{8,72},{9,... | collective-permute-start | bytes 12296 | tf_op jit(solution)/shard_map/total4/ppermute | solution.py:175
  143.5 0.1 stack.218.at
  143.5 0.1 stack.177.at
  143.7 2.0 %shard_map.62.rest_4_ = f32[2,192,3072]{2,1,0:T(8,128)} custom-call(s32[8]{0:T(128)S(1)} %stack.218.at, f32[192,768]{1,0:T(8,128)S(1)} %copy-done.1, f32[192,768]{1,0:T(8,128)S(1)} %collective-permute-done.15.rest_1_, f32[192,768]{1,0:T(8,128)S(1)} %collective-permute-done.16.rest_2_, f32[192,768]{1,0:T(8,128)S(1)} %collective-permute-done.17.rest_3_), custom_call_target="tpu_custom_call" | custom-call | tf_op jit(solution)/shard_map/pallas_call | solution.py:139
  145.7 0.6 slice.47
  147.0 0.6 fusion.8
  147.6 2.5 %shard_map.63 = f32[2,192,3072]{2,1,0:T(8,128)} custom-call(s32[8]{0:T(128)S(1)} %stack.177.at, f32[192,768]{1,0:T(8,128)S(1)} %copy-done, f32[192,768]{1,0:T(8,128)S(1)} %collective-permute-done.19.rest_1_, f32[192,768]{1,0:T(8,128)S(1)} %collective-permute-done.20.rest_2_, ...), custom_call_target="tpu_custom_call", output_to_operand_aliasing={{}: (5, {})} | custom-call | tf_op jit(solution)/shard_map/pallas_call | solution.py:139
  (67 shorter events, 0.4 us)
Async XLA Ops:
  0.7 6.1 %copy-start.13 = (s32[2]{0:T(128)S(1)}, s32[2]{0:T(128)}, u32[]{:S(2)}) copy-start(s32[2]{0:T(128)} %param.7) | copy-start | bytes 28
  0.7 7.3 %copy-start.2 = (bf16[2,192,3072]{2,1,0:T(8,128)(2,1)S(1)}, bf16[2,192,3072]{2,1,0:T(8,128)(2,1)}, u32[]{:S(2)}) copy-start(bf16[2,192,3072]{2,1,0:T(8,128)(2,1)} %param.5) | copy-start | bytes 7077892
  3.7 6.0 %copy-start.4 = (bf16[192,3072]{1,0:T(8,128)(2,1)}, bf16[192,3072]{1,0:T(8,128)(2,1)S(1)}, u32[]{:S(2)}) copy-start(bf16[192,3072]{1,0:T(8,128)(2,1)S(1)} %get-tuple-element.73.rest_0_) | copy-start | bytes 3538948
  3.7 32.9 %collective-permute-start.4 = (bf16[192,3072]{1,0:T(8,128)(2,1)}, bf16[192,3072]{1,0:T(8,128)(2,1)}, u32[]{:S(2)}, u32[]{:S(2)}) collective-permute-start(bf16[192,3072]{1,0:T(8,128)(2,1)} %get-tuple-element.72), channel_id=1, source_target_pairs={{0,12},{1,13},{2,14},{3,15},{4,8},{5,9},{6,10},{7,11},{8,4},{9,5},... | collective-permute-start | bytes 3538952 | tf_op jit(solution)/shard_map/left3/ppermute | solution.py:175
  6.5 30.0 %collective-permute-start = (bf16[192,3072]{1,0:T(8,128)(2,1)S(1)}, bf16[192,3072]{1,0:T(8,128)(2,1)}, u32[]{:S(2)}, u32[]{:S(2)}) collective-permute-start(bf16[192,3072]{1,0:T(8,128)(2,1)S(1)} %get-tuple-element.73.rest_0_), channel_id=1, source_target_pairs={{0,4},{1,5},{2,6},{3,7},{4,0},{5,1},{6,2},{7,3},{8,12},{9,13},{10,... | collective-permute-start | bytes 3538952 | tf_op jit(solution)/shard_map/left1/ppermute | solution.py:175
  8.0 1.6 %copy-start.5 = (bf16[2,3072,64]{1,2,0:T(8,128)(2,1)}, bf16[2,3072,64]{1,2,0:T(8,128)(2,1)S(1)}, u32[]{:S(2)}) copy-start(bf16[2,3072,64]{1,2,0:T(8,128)(2,1)S(1)} %broadcast_multiply_fusion) | copy-start | bytes 2359300
  14.6 15.0 %collective-permute-start.1 = (bf16[192,1664]{1,0:T(8,128)(2,1)S(1)}, bf16[192,1664]{1,0:T(8,128)(2,1)S(1)}, u32[]{:S(2)}, u32[]{:S(2)}) collective-permute-start(bf16[192,1664]{1,0:T(8,128)(2,1)S(1)} %pad_maximum_fusion.2), channel_id=1, source_target_pairs={{0,4},{1,5},{2,6},{3,7},{4,0},{5,1},{6,2},{7,3},{8,12},{9,13},{10,... | collective-permute-start | bytes 1916936 | tf_op jit(solution)/shard_map/right1/ppermute | solution.py:175
  16.5 19.7 %collective-permute-start.2 = (bf16[192,1664]{1,0:T(8,128)(2,1)S(1)}, bf16[192,1664]{1,0:T(8,128)(2,1)S(1)}, u32[]{:S(2)}, u32[]{:S(2)}) collective-permute-start(bf16[192,1664]{1,0:T(8,128)(2,1)S(1)} %pad_maximum_fusion.3), channel_id=1, source_target_pairs={{0,8},{1,9},{2,10},{3,11},{4,12},{5,13},{6,14},{7,15},{8,0},{9,1},... | collective-permute-start | bytes 1916936 | tf_op jit(solution)/shard_map/right2/ppermute | solution.py:175
  17.5 18.8 %collective-permute-start.3 = (bf16[192,1664]{1,0:T(8,128)(2,1)S(1)}, bf16[192,1664]{1,0:T(8,128)(2,1)S(1)}, u32[]{:S(2)}, u32[]{:S(2)}) collective-permute-start(bf16[192,1664]{1,0:T(8,128)(2,1)S(1)} %pad_maximum_fusion.4), channel_id=1, source_target_pairs={{0,12},{1,13},{2,14},{3,15},{4,8},{5,9},{6,10},{7,11},{8,4},{9,5},... | collective-permute-start | bytes 1916936 | tf_op jit(solution)/shard_map/right3/ppermute | solution.py:175
  29.6 35.0 %collective-permute-start.8 = (bf16[192,3072]{1,0:T(8,128)(2,1)}, bf16[192,3072]{1,0:T(8,128)(2,1)S(1)}, u32[]{:S(2)}, u32[]{:S(2)}) collective-permute-start(bf16[192,3072]{1,0:T(8,128)(2,1)} %get-tuple-element.72), channel_id=1, source_target_pairs={{0,8},{1,9},{2,10},{3,11},{4,12},{5,13},{6,14},{7,15},{8,0},{9,1},... | collective-permute-start | bytes 3538952 | tf_op jit(solution)/shard_map/left2/ppermute | solution.py:175
  36.5 28.5 %copy-start.3 = (bf16[4,192,896]{2,1,0:T(8,128)(2,1)}, bf16[4,192,896]{2,1,0:T(8,128)(2,1)S(1)}, u32[]{:S(2)}) copy-start(bf16[4,192,896]{2,1,0:T(8,128)(2,1)S(1)} %pad_maximum_fusion.rest_4_) | copy-start | bytes 4128772
  36.6 28.0 %collective-permute-start.6 = (bf16[4,192,896]{2,1,0:T(8,128)(2,1)S(1)}, bf16[4,192,896]{2,1,0:T(8,128)(2,1)S(1)}, u32[]{:S(2)}, u32[]{:S(2)}) collective-permute-start(bf16[4,192,896]{2,1,0:T(8,128)(2,1)S(1)} %pad_maximum_fusion.rest_4_), channel_id=1, source_target_pairs={{0,3},{1,0},{2,1},{3,2},{4,7},{5,4},{6,5},{7,6},{8,11},{9,8},{10,9... | collective-permute-start | bytes 4128776 | tf_op jit(solution)/shard_map/down0/ppermute | solution.py:175
  39.7 25.3 %collective-permute-start.5 = (bf16[4,192,896]{2,1,0:T(8,128)(2,1)S(1)}, bf16[4,192,896]{2,1,0:T(8,128)(2,1)}, u32[]{:S(2)}, u32[]{:S(2)}) collective-permute-start(bf16[4,192,896]{2,1,0:T(8,128)(2,1)S(1)} %pad_maximum_fusion.rest_4_), channel_id=1, source_target_pairs={{0,1},{1,2},{2,3},{3,0},{4,5},{5,6},{6,7},{7,4},{8,9},{9,10},{10,1... | collective-permute-start | bytes 4128776 | tf_op jit(solution)/shard_map/up0/ppermute | solution.py:175
  39.9 24.7 %collective-permute-start.7 = (bf16[4,192,128]{2,1,0:T(8,128)(2,1)S(1)}, bf16[4,192,128]{2,1,0:T(8,128)(2,1)S(1)}, u32[]{:S(2)}, u32[]{:S(2)}) collective-permute-start(bf16[4,192,128]{2,1,0:T(8,128)(2,1)S(1)} %pad_maximum_fusion.6), channel_id=1, source_target_pairs={{0,2},{1,3},{2,0},{3,1},{4,6},{5,7},{6,4},{7,5},{8,10},{9,11},{10,... | collective-permute-start | bytes 589832 | tf_op jit(solution)/shard_map/shade/ppermute | solution.py:175
  64.6 1.9 %copy-start.10 = (bf16[4,192,128]{2,1,0:T(8,128)(2,1)}, bf16[4,192,128]{2,1,0:T(8,128)(2,1)S(1)}, u32[]{:S(2)}) copy-start(bf16[4,192,128]{2,1,0:T(8,128)(2,1)S(1)} %collective-permute-done.7.rest_7_) | copy-start | bytes 589828
  64.6 1.9 %copy-start.7 = (bf16[192,3072]{1,0:T(8,128)(2,1)}, bf16[192,3072]{1,0:T(8,128)(2,1)S(1)}, u32[]{:S(2)}) copy-start(bf16[192,3072]{1,0:T(8,128)(2,1)S(1)} %collective-permute-done.8.rest_2_) | copy-start | bytes 3538948
  64.6 1.9 %copy-start.6 = (bf16[4,192,896]{2,1,0:T(8,128)(2,1)}, bf16[4,192,896]{2,1,0:T(8,128)(2,1)S(1)}, u32[]{:S(2)}) copy-start(bf16[4,192,896]{2,1,0:T(8,128)(2,1)S(1)} %collective-permute-done.6.rest_6_) | copy-start | bytes 4128772
  65.1 19.7 %collective-permute-start.9 = (bf16[4,192,896]{2,1,0:T(8,128)(2,1)}, bf16[4,192,896]{2,1,0:T(8,128)(2,1)S(1)}, u32[]{:S(2)}, u32[]{:S(2)}) collective-permute-start(bf16[4,192,896]{2,1,0:T(8,128)(2,1)} %collective-permute-done.5.rest_5_), channel_id=1, source_target_pairs={{0,1},{1,2},{2,3},{3,0},{4,5},{5,6},{6,7},{7,4},{8,9},{9,10},{10,1... | collective-permute-start | bytes 4128776 | tf_op jit(solution)/shard_map/forward0/ppermute | solution.py:175
  66.5 17.6 %collective-permute-start.10 = (bf16[4,192,768]{2,1,0:T(8,128)(2,1)}, bf16[4,192,768]{2,1,0:T(8,128)(2,1)S(1)}, u32[]{:S(2)}, u32[]{:S(2)}) collective-permute-start(bf16[4,192,768]{2,1,0:T(8,128)(2,1)} %pad_maximum_fusion.1.rest_4_), channel_id=1, source_target_pairs={{0,3},{1,0},{2,1},{3,2},{4,7},{5,4},{6,5},{7,6},{8,11},{9,8},{10,9... | collective-permute-start | bytes 3538952 | tf_op jit(solution)/shard_map/down1/ppermute | solution.py:175
  78.4 4.9 %collective-permute-start.11 = (f32[64,64]{1,0:T(8,128)}, f32[64,64]{1,0:T(8,128)S(1)}, u32[]{:S(2)}, u32[]{:S(2)}) collective-permute-start(f32[64,64]{1,0:T(8,128)} %shard_map.59), channel_id=1, source_target_pairs={{0,1},{1,0},{2,3},{3,2},{4,5},{5,4},{6,7},{7,6},{8,9},{9,8},{10,11... | collective-permute-start | bytes 49160 | tf_op jit(solution)/shard_map/corner1/ppermute | solution.py:175
  84.1 18.0 %copy-start.15 = (bf16[4,192,768]{2,1,0:T(8,128)(2,1)}, bf16[4,192,768]{2,1,0:T(8,128)(2,1)S(1)}, u32[]{:S(2)}) copy-start(bf16[4,192,768]{2,1,0:T(8,128)(2,1)S(1)} %collective-permute-done.10.rest_6_) | copy-start | bytes 3538948
  84.8 5.8 %copy-start.14 = (bf16[4,192,896]{2,1,0:T(8,128)(2,1)}, bf16[4,192,896]{2,1,0:T(8,128)(2,1)S(1)}, u32[]{:S(2)}) copy-start(bf16[4,192,896]{2,1,0:T(8,128)(2,1)S(1)} %collective-permute-done.9.rest_7_) | copy-start | bytes 4128772
  84.8 24.2 %collective-permute-start.12 = (bf16[4,192,768]{2,1,0:T(8,128)(2,1)}, bf16[4,192,768]{2,1,0:T(8,128)(2,1)S(1)}, u32[]{:S(2)}, u32[]{:S(2)}) collective-permute-start(bf16[4,192,768]{2,1,0:T(8,128)(2,1)} %pad_maximum_fusion.1.rest_4_), channel_id=1, source_target_pairs={{0,1},{1,2},{2,3},{3,0},{4,5},{5,6},{6,7},{7,4},{8,9},{9,10},{10,1... | collective-permute-start | bytes 3538952 | tf_op jit(solution)/shard_map/up1/ppermute | solution.py:175
  85.4 25.3 %collective-permute-start.13 = (bf16[4,192,768]{2,1,0:T(8,128)(2,1)S(1)}, bf16[4,192,768]{2,1,0:T(8,128)(2,1)S(1)}, u32[]{:S(2)}, u32[]{:S(2)}) collective-permute-start(bf16[4,192,768]{2,1,0:T(8,128)(2,1)S(1)} %collective-permute-done.10.rest_6_), channel_id=1, source_target_pairs={{0,3},{1,0},{2,1},{3,2},{4,7},{5,4},{6,5},{7,6},{8,11},{9,8},{10,9... | collective-permute-start | bytes 3538952 | tf_op jit(solution)/shard_map/forward1/ppermute | solution.py:175
  88.0 16.1 %collective-permute-start.14 = (f32[64,64]{1,0:T(8,128)S(1)}, f32[64,64]{1,0:T(8,128)S(1)}, u32[]{:S(2)}, u32[]{:S(2)}) collective-permute-start(f32[64,64]{1,0:T(8,128)S(1)} %add.304), channel_id=1, source_target_pairs={{0,2},{1,3},{2,0},{3,1},{4,6},{5,7},{6,4},{7,5},{8,10},{9,11},{10,... | collective-permute-start | bytes 49160 | tf_op jit(solution)/shard_map/corner2/ppermute | solution.py:175
  104.2 18.9 %copy-start.8 = (f32[64,64]{1,0:T(8,128)}, f32[64,64]{1,0:T(8,128)S(1)}, u32[]{:S(2)}) copy-start(f32[64,64]{1,0:T(8,128)S(1)} %add.305) | copy-start | bytes 49156
  104.2 39.5 %copy-start.1 = (f32[192,768]{1,0:T(8,128)S(1)}, f32[192,768]{1,0:T(8,128)}, u32[]{:S(2)}) copy-start(f32[192,768]{1,0:T(8,128)} %get-tuple-element.63.rest_0_) | copy-start | bytes 1769476
  104.2 19.1 %collective-permute-start.15 = (f32[192,768]{1,0:T(8,128)}, f32[192,768]{1,0:T(8,128)S(1)}, u32[]{:S(2)}, u32[]{:S(2)}) collective-permute-start(f32[192,768]{1,0:T(8,128)} %get-tuple-element.55), channel_id=1, source_target_pairs={{0,4},{1,5},{2,6},{3,7},{4,0},{5,1},{6,2},{7,3},{8,12},{9,13},{10,... | collective-permute-start | bytes 1769480 | tf_op jit(solution)/shard_map/back01/ppermute | solution.py:175
  105.7 17.6 %collective-permute-start.16 = (f32[192,768]{1,0:T(8,128)}, f32[192,768]{1,0:T(8,128)S(1)}, u32[]{:S(2)}, u32[]{:S(2)}) collective-permute-start(f32[192,768]{1,0:T(8,128)} %get-tuple-element.56), channel_id=1, source_target_pairs={{0,8},{1,9},{2,10},{3,11},{4,12},{5,13},{6,14},{7,15},{8,0},{9,1},... | collective-permute-start | bytes 1769480 | tf_op jit(solution)/shard_map/back02/ppermute | solution.py:175
  108.4 18.0 %collective-permute-start.17 = (f32[192,768]{1,0:T(8,128)}, f32[192,768]{1,0:T(8,128)S(1)}, u32[]{:S(2)}, u32[]{:S(2)}) collective-permute-start(f32[192,768]{1,0:T(8,128)} %get-tuple-element.57), channel_id=1, source_target_pairs={{0,12},{1,13},{2,14},{3,15},{4,8},{5,9},{6,10},{7,11},{8,4},{9,5},... | collective-permute-start | bytes 1769480 | tf_op jit(solution)/shard_map/back03/ppermute | solution.py:175
  109.0 1.8 %copy-start.16 = (bf16[4,192,768]{2,1,0:T(8,128)(2,1)}, bf16[4,192,768]{2,1,0:T(8,128)(2,1)S(1)}, u32[]{:S(2)}) copy-start(bf16[4,192,768]{2,1,0:T(8,128)(2,1)S(1)} %collective-permute-done.12.rest_5_) | copy-start | bytes 3538948
  109.0 14.3 %collective-permute-start.18 = (f32[64,64]{1,0:T(8,128)S(1)}, f32[64,64]{1,0:T(8,128)S(1)}, u32[]{:S(2)}, u32[]{:S(2)}) collective-permute-start(f32[64,64]{1,0:T(8,128)S(1)} %add.305), channel_id=1, source_target_pairs={{0,8},{1,9},{2,10},{3,11},{4,12},{5,13},{6,14},{7,15},{8,0},{9,1},... | collective-permute-start | bytes 49160 | tf_op jit(solution)/shard_map/beside/ppermute | solution.py:175
  110.7 1.0 copy-start.17
  123.3 3.1 %copy-start.11 = (f32[64,64]{1,0:T(8,128)}, f32[64,64]{1,0:T(8,128)S(1)}, u32[]{:S(2)}) copy-start(f32[64,64]{1,0:T(8,128)S(1)} %collective-permute-done.18) | copy-start | bytes 49156
  126.4 21.2 %collective-permute-start.19 = (f32[192,768]{1,0:T(8,128)}, f32[192,768]{1,0:T(8,128)S(1)}, u32[]{:S(2)}, u32[]{:S(2)}) collective-permute-start(f32[192,768]{1,0:T(8,128)} %get-tuple-element.60), channel_id=1, source_target_pairs={{0,4},{1,5},{2,6},{3,7},{4,0},{5,1},{6,2},{7,3},{8,12},{9,13},{10,... | collective-permute-start | bytes 1769480 | tf_op jit(solution)/shard_map/back11/ppermute | solution.py:175
  126.4 21.2 %collective-permute-start.20 = (f32[192,768]{1,0:T(8,128)}, f32[192,768]{1,0:T(8,128)S(1)}, u32[]{:S(2)}, u32[]{:S(2)}) collective-permute-start(f32[192,768]{1,0:T(8,128)} %get-tuple-element.61), channel_id=1, source_target_pairs={{0,8},{1,9},{2,10},{3,11},{4,12},{5,13},{6,14},{7,15},{8,0},{9,1},... | collective-permute-start | bytes 1769480 | tf_op jit(solution)/shard_map/back12/ppermute | solution.py:175
  128.4 19.2 %collective-permute-start.21 = (f32[192,768]{1,0:T(8,128)}, f32[192,768]{1,0:T(8,128)}, u32[]{:S(2)}, u32[]{:S(2)}) collective-permute-start(f32[192,768]{1,0:T(8,128)} %get-tuple-element.62), channel_id=1, source_target_pairs={{0,12},{1,13},{2,14},{3,15},{4,8},{5,9},{6,10},{7,11},{8,4},{9,5},... | collective-permute-start | bytes 1769480 | tf_op jit(solution)/shard_map/back13/ppermute | solution.py:175
  133.3 1.2 collective-permute-start.22
  135.2 3.7 %collective-permute-start.23 = (f32[8,128]{1,0:T(8,128)S(1)}, f32[8,128]{1,0:T(8,128)S(1)}, u32[]{:S(2)}, u32[]{:S(2)}) collective-permute-start(f32[8,128]{1,0:T(8,128)S(1)} %broadcast_add_fusion), channel_id=1, source_target_pairs={{0,32},{1,33},{2,34},{3,35},{4,36},{5,37},{6,38},{7,39},{8,40},{9,... | collective-permute-start | bytes 12296 | tf_op jit(solution)/shard_map/total2/ppermute | solution.py:175
  139.5 6.1 %collective-permute-start.24 = (f32[8,128]{1,0:T(8,128)S(1)}, f32[8,128]{1,0:T(8,128)S(1)}, u32[]{:S(2)}, u32[]{:S(2)}) collective-permute-start(f32[8,128]{1,0:T(8,128)S(1)} %fusion.12), channel_id=1, source_target_pairs={{0,64},{1,65},{2,66},{3,67},{4,68},{5,69},{6,70},{7,71},{8,72},{9,... | collective-permute-start | bytes 12296 | tf_op jit(solution)/shard_map/total4/ppermute | solution.py:175
  143.6 3.3 %copy-start.9 = (f32[64,64]{1,0:T(8,128)S(1)}, f32[64,64]{1,0:T(8,128)}, u32[]{:S(2)}) copy-start(f32[64,64]{1,0:T(8,128)} %copy-done.8) | copy-start | bytes 49156
  143.6 3.3 %copy-start.12 = (f32[64,64]{1,0:T(8,128)S(1)}, f32[64,64]{1,0:T(8,128)}, u32[]{:S(2)}) copy-start(f32[64,64]{1,0:T(8,128)} %copy-done.11) | copy-start | bytes 49156
  143.6 4.0 %copy-start = (f32[192,768]{1,0:T(8,128)S(1)}, f32[192,768]{1,0:T(8,128)}, u32[]{:S(2)}) copy-start(f32[192,768]{1,0:T(8,128)} %get-tuple-element.59.rest_0_) | copy-start | bytes 1769476

commit v4 on v3

--- a/solution.py
+++ b/solution.py
@@ -25,8 +25,7 @@
 
 def product(offsets, lefts, pieces, at, width):
     rows, depth = lefts[0].shape
-    middle = width // 256 * 128
-    sides = ((0, middle), (middle, width))
+    sides = ((0, width),)
     where = [(i, p) for i, piece in enumerate(pieces) for p in range(piece.shape[0])]
     n_left = len(lefts)
 
@@ -57,7 +56,7 @@
             pltpu.VMEM((n_left * rows, depth), jnp.bfloat16),
             pltpu.VMEM((depth, width), jnp.bfloat16),
             pltpu.SemaphoreType.DMA((n_left,)),
-            pltpu.SemaphoreType.DMA((2, len(where))),
+            pltpu.SemaphoreType.DMA((1, len(where))),
         ],
         cost_estimate=pl.CostEstimate(
             flops=2 * n_left * rows * depth * width,
@@ -168,6 +167,7 @@
     up = pairs(lambda row, g, h: (row, g, (h + 1) % SIDE))
     down = pairs(lambda row, g, h: (row, g, (h - 1) % SIDE))
     across_h = pairs(lambda row, g, h: (row, g, (h + 2) % SIDE))
+    diagonal = pairs(lambda row, g, h: (row, g ^ 2, h ^ 2))
     across = {p: pairs(lambda row, g, h, p=p: (row ^ p, g, h)) for p in (1, 2, 4)}
 
     def send(value, table, name):
@@ -226,7 +226,8 @@
             return place(spots, out, (count, rows, depth), into)
 
         def back(c, out):
-            return [out[0]] + [send(out[p], along_g[p], f"back{c}{p}") for p in (1, 2, 3)]
+            sent = {p: send(out[p], along_g[p], f"back{c}{p}") for p in (2, 1, 3)}
+            return [out[0], sent[1], sent[2], sent[3]]
 
         ours = lax.dynamic_index_in_dim(masked, sector, 0, keepdims=False)
         chosen = jnp.stack([lax.dynamic_slice_in_dim(ours, owner(gg, h) * rows, rows, 0).T for gg in gs])
@@ -244,19 +245,21 @@
         beyond0, above1, corner = lax.optimization_barrier((beyond0, above1, corner))
         below1 = send(after(own1, beyond0), up, "up1")
         beyond1 = send(above1, down, "forward1")
-        corner = corner + send(corner, along_h[2], "corner2")
+        around = [corner] + [send(corner, table, "around") for table in (along_h[2], along_g[2], diagonal)]
         skips = (extra,) * 4
         out0 = product(offsets, left, (own0, below0, above0, beyond0), skips, width)
-        out0, corner = lax.optimization_barrier((out0, corner))
+        out0, around = lax.optimization_barrier((out0, around))
         out0 = back(0, out0)
-        beside = send(corner, along_g[2], "beside")
+        corner, beside = around[0] + around[1], around[2] + around[3]
+        corner = jnp.where(sector == 0, jnp.stack([corner, beside]), jnp.stack([beside, corner]))
+        total = after(jnp.broadcast_to(jnp.sum(corner * corner), (8, 128)), below1, beyond1)
+        total = total + send(total, across[1], "total1")
         out1 = product(offsets, left, (own1, below1, above1, beyond1), (0,) * 4, width)
-        out1, out0, beside = lax.optimization_barrier((out1, out0, beside))
+        first, total = lax.optimization_barrier((out1[0], total))
+        out1 = [first] + [after(out1[p], out0[p], total) for p in (1, 2, 3)]
         out1 = back(1, out1)
         enlarged = put(1, out1, put(0, out0, None))
-        corner = jnp.where(sector == 0, jnp.stack([corner, beside]), jnp.stack([beside, corner]))
-        total = jnp.broadcast_to(jnp.sum(corner * corner), (8, 128))
-        for p in (1, 2, 4):
+        for p in (2, 4):
             total = total + send(total, across[p], f"total{p}")
         entries = n_row * count * kept * kept
         return enlarged, corner * lax.rsqrt(total[0, 0] / entries + 1e-06)

time: 151 us -> 149 us (0.987)
  Pallas kernels: 33.5 us -> 30 us
  waiting for transfers between devices: 52.4 us -> 55.5 us
  other arithmetic: 9.28 us -> 7.13 us
  starting transfers between devices: 40.7 us -> 42.5 us
    pallas_call x2, Pallas kernels: 22.7 us -> 19.2 us  [product(): pl.pallas_call(kernel, in_specs=[pl.BlockSpec(memory_space=pltpu.SMEM)] +...]
    ppermute x25 -> x26, waiting for transfers between devices: 52.4 us -> 55.5 us  [send(): return lax.ppermute(value, ('row', 'col'), table)]
    ppermute x25 -> x26, starting transfers between devices: 40.7 us -> 42.5 us  [send(): return lax.ppermute(value, ('row', 'col'), table)]
  transfers between devices with their start and end apart: 25 -> 26, of which waited for: 11 -> 12; matrix products, arithmetic and copies ran while one was open for 12% -> 10% of each run, Pallas kernels for 21% -> 19%
where the time goes in v4:
time: 149 us; the launch traced here: 148 us
  waiting for transfers between devices  55.5 us (37%)
  starting transfers between devices  42.5 us (29%)
  Pallas kernels  30 us (20%)
  local copies, waits for them, and re-layouts  9.77 us (7%)
  other arithmetic  7.13 us (5%)
  between operations  1.89 us (1%)
  matrix products  1.58 us (1%)
    ppermute x26, waiting for transfers between devices, send(): return lax.ppermute(value, ('row', 'col'), table)  55.5 us
    ppermute x26, starting transfers between devices, send(): return lax.ppermute(value, ('row', 'col'), table)  42.5 us
    pallas_call x2, Pallas kernels, product(): pl.pallas_call(kernel, in_specs=[pl.BlockSpec(memory_space=pltpu.SMEM)] +...  19.2 us
    pallas_call x1, Pallas kernels, share(): pl.pallas_call(kernel, in_specs=[pl.BlockSpec(memory_space=pltpu.SMEM), i...  6.31 us
    pallas_call x2, Pallas kernels, place(): pl.pallas_call(kernel, in_specs=[pl.BlockSpec(memory_space=pltpu.SMEM)] +...  4.49 us
  transfers between devices with their start and end apart: 26, of which 12 were waited for; matrix products, arithmetic and copies ran while one was open for 10% of the time, Pallas kernels for 19%

profile of v4, /device:TPU:0, one launch (start us, length us, event | category | flops | bytes accessed | tf_op | source)
XLA Modules:
  0.0 148.3 jit_solution(12900729637589259327)
XLA Ops:
  0.7 3.0 %dynamic-slice_bitcast_fusion = (bf16[192,3072]{1,0:T(8,128)(2,1)}, bf16[192,3072]{1,0:T(8,128)(2,1)S(1)}) fusion(bf16[2,192,3072]{2,1,0:T(8,128)(2,1)} %param.4, s32[]{:T(128)S(6)} %select_n.241, s32[]{:T(128)S(6)} %select_n.240), kind=kLoop, calls=%fused_computation.2 | loop fusion | bytes 4718600 | tf_op jit(solution)/shard_map/jit(dynamic_index_in_dim)/squeeze | solution.py:198
  3.7 2.8 %collective-permute-start.4 = (bf16[192,3072]{1,0:T(8,128)(2,1)}, bf16[192,3072]{1,0:T(8,128)(2,1)}, u32[]{:S(2)}, u32[]{:S(2)}) collective-permute-start(bf16[192,3072]{1,0:T(8,128)(2,1)} %get-tuple-element.72), channel_id=1, source_target_pairs={{0,12},{1,13},{2,14},{3,15},{4,8},{5,9},{6,10},{7,11},{8,4},{9,5},... | collective-permute-start | bytes 3538952 | tf_op jit(solution)/shard_map/left3/ppermute | solution.py:175
  6.5 0.2 collective-permute-start
  6.8 0.1 compare_convert_fusion
  6.8 1.2 broadcast_multiply_fusion
  8.1 1.6 %fusion.9 = (f32[2,192,64]{1,2,0:T(8,128)}, f32[2,192,64]{1,2,0:T(8,128)}) fusion(bf16[2,192,3072]{2,1,0:T(8,128)(2,1)S(1)} %copy-done.2, bf16[2,3072,64]{1,2,0:T(8,128)(2,1)S(1)} %broadcast_multiply_fusion), kind=kOutput, calls=%fused_computation.52 | convolution fusion | flops 151019520 | bytes 3342336 | tf_op jit(solution)/shard_map/skj,sjq->skq/dot_general | solution.py:201
  9.6 1.7 %copy.9 = f32[2,192,64]{2,1,0:T(8,128)} copy(f32[2,192,64]{1,2,0:T(8,128)} %get-tuple-element.84) | data formatting | bytes 196608 | tf_op jit(solution)/shard_map/reduce_precision | solution.py:202
  11.3 1.7 %copy.10 = f32[2,192,64]{2,1,0:T(8,128)} copy(f32[2,192,64]{1,2,0:T(8,128)} %get-tuple-element.85) | data formatting | bytes 196608 | tf_op jit(solution)/shard_map/skj,sjq->skq/dot_general | solution.py:201
  13.0 1.1 subtract_convert_fusion
  14.2 0.1 fusion.3
  14.3 0.2 dynamic-slice_bitcast_fusion.5
  14.5 0.1 pad_maximum_fusion.2
  14.6 1.9 %collective-permute-start.1 = (bf16[192,1664]{1,0:T(8,128)(2,1)S(1)}, bf16[192,1664]{1,0:T(8,128)(2,1)S(1)}, u32[]{:S(2)}, u32[]{:S(2)}) collective-permute-start(bf16[192,1664]{1,0:T(8,128)(2,1)S(1)} %pad_maximum_fusion.2), channel_id=1, source_target_pairs={{0,4},{1,5},{2,6},{3,7},{4,0},{5,1},{6,2},{7,3},{8,12},{9,13},{10,... | collective-permute-start | bytes 1916936 | tf_op jit(solution)/shard_map/right1/ppermute | solution.py:175
  16.5 0.1 pad_maximum_fusion.3
  16.5 0.9 collective-permute-start.2
  17.5 2.2 %collective-permute-start.3 = (bf16[192,1664]{1,0:T(8,128)(2,1)S(1)}, bf16[192,1664]{1,0:T(8,128)(2,1)S(1)}, u32[]{:S(2)}, u32[]{:S(2)}) collective-permute-start(bf16[192,1664]{1,0:T(8,128)(2,1)S(1)} %pad_maximum_fusion.4), channel_id=1, source_target_pairs={{0,12},{1,13},{2,14},{3,15},{4,8},{5,9},{6,10},{7,11},{8,4},{9,5},... | collective-permute-start | bytes 1916936 | tf_op jit(solution)/shard_map/right3/ppermute | solution.py:175
  19.7 9.9 %collective-permute-done.1 = bf16[192,1664]{1,0:T(8,128)(2,1)S(1)} collective-permute-done((bf16[192,1664]{1,0:T(8,128)(2,1)S(1)}, bf16[192,1664]{1,0:T(8,128)(2,1)S(1)}, u32[]{:S(2)}, u32[]{:S(2)}) %collective-permute-start.1) | collective-permute-done | bytes 639008 | tf_op jit(solution)/shard_map/right1/ppermute | solution.py:175
  29.6 0.8 collective-permute-start.8
  30.4 5.8 %collective-permute-done.2 = bf16[192,1664]{1,0:T(8,128)(2,1)S(1)} collective-permute-done((bf16[192,1664]{1,0:T(8,128)(2,1)S(1)}, bf16[192,1664]{1,0:T(8,128)(2,1)S(1)}, u32[]{:S(2)}, u32[]{:S(2)}) %collective-permute-start.2) | collective-permute-done | bytes 639008 | tf_op jit(solution)/shard_map/right2/ppermute | solution.py:175
  36.3 0.2 pad_maximum_fusion.rest_4_
  36.6 3.2 %collective-permute-start.6 = (bf16[4,192,896]{2,1,0:T(8,128)(2,1)S(1)}, bf16[4,192,896]{2,1,0:T(8,128)(2,1)S(1)}, u32[]{:S(2)}, u32[]{:S(2)}) collective-permute-start(bf16[4,192,896]{2,1,0:T(8,128)(2,1)S(1)} %pad_maximum_fusion.rest_4_), channel_id=1, source_target_pairs={{0,3},{1,0},{2,1},{3,2},{4,7},{5,4},{6,5},{7,6},{8,11},{9,8},{10,9... | collective-permute-start | bytes 4128776 | tf_op jit(solution)/shard_map/down0/ppermute | solution.py:175
  39.9 2.3 %collective-permute-start.7 = (bf16[4,192,128]{2,1,0:T(8,128)(2,1)S(1)}, bf16[4,192,128]{2,1,0:T(8,128)(2,1)S(1)}, u32[]{:S(2)}, u32[]{:S(2)}) collective-permute-start(bf16[4,192,128]{2,1,0:T(8,128)(2,1)S(1)} %pad_maximum_fusion.6), channel_id=1, source_target_pairs={{0,2},{1,3},{2,0},{3,1},{4,6},{5,7},{6,4},{7,5},{8,10},{9,11},{10,... | collective-permute-start | bytes 589832 | tf_op jit(solution)/shard_map/shade/ppermute | solution.py:175
  42.2 22.4 %collective-permute-done.7.rest_7_ = bf16[4,192,128]{2,1,0:T(8,128)(2,1)S(1)} collective-permute-done((bf16[4,192,128]{2,1,0:T(8,128)(2,1)S(1)}, bf16[4,192,128]{2,1,0:T(8,128)(2,1)S(1)}, u32[]{:S(2)}, u32[]{:S(2)}) %collective-permute-start.7) | collective-permute-done | bytes 196640 | tf_op jit(solution)/shard_map/shade/ppermute | solution.py:175
  64.6 0.5 collective-permute-done.5.rest_5_
  65.1 1.4 pad_maximum_fusion.1.rest_4_
  66.5 3.2 %collective-permute-start.10 = (bf16[4,192,768]{2,1,0:T(8,128)(2,1)}, bf16[4,192,768]{2,1,0:T(8,128)(2,1)S(1)}, u32[]{:S(2)}, u32[]{:S(2)}) collective-permute-start(bf16[4,192,768]{2,1,0:T(8,128)(2,1)} %pad_maximum_fusion.1.rest_4_), channel_id=1, source_target_pairs={{0,3},{1,0},{2,1},{3,2},{4,7},{5,4},{6,5},{7,6},{8,11},{9,8},{10,9... | collective-permute-start | bytes 3538952 | tf_op jit(solution)/shard_map/down1/ppermute | solution.py:175
  69.7 0.6 stack.194.off
  70.4 1.0 dynamic-slice_bitcast_fusion.9
  71.4 0.7 pad_maximum_fusion.7.pick
  72.0 6.3 %shard_map.59 = f32[64,64]{1,0:T(8,128)} custom-call(s32[16]{0:T(128)} %stack.194.off, bf16[4,64,192]{2,1,0:T(8,128)(2,1)} %pad_maximum_fusion.7.pick, bf16[192,3072]{1,0:T(8,128)(2,1)} %copy-done.4, bf16[192,3072]{1,0:T(8,128)(2,1)} %collective-permute-done.rest_1_, bf16[192,3072]{1,0:T(8,128)(2,1)} %copy-done.7, ...), custom_call_target="tpu_custom_call" | custom-call | flops 603979776 | bytes 5505024 | tf_op jit(solution)/shard_map/pallas_call | solution.py:100
  78.4 0.1 collective-permute-start.11
  78.5 4.9 %collective-permute-done.11 = f32[64,64]{1,0:T(8,128)S(1)} collective-permute-done((f32[64,64]{1,0:T(8,128)}, f32[64,64]{1,0:T(8,128)S(1)}, u32[]{:S(2)}, u32[]{:S(2)}) %collective-permute-start.11) | collective-permute-done | bytes 16416 | tf_op jit(solution)/shard_map/corner1/ppermute | solution.py:175
  83.3 0.8 add.307
  84.1 0.7 collective-permute-done.9.rest_7_
  84.8 0.6 collective-permute-start.12
  85.4 2.6 %collective-permute-start.13 = (bf16[4,192,768]{2,1,0:T(8,128)(2,1)S(1)}, bf16[4,192,768]{2,1,0:T(8,128)(2,1)}, u32[]{:S(2)}, u32[]{:S(2)}) collective-permute-start(bf16[4,192,768]{2,1,0:T(8,128)(2,1)S(1)} %collective-permute-done.10.rest_6_), channel_id=1, source_target_pairs={{0,3},{1,0},{2,1},{3,2},{4,7},{5,4},{6,5},{7,6},{8,11},{9,8},{10,9... | collective-permute-start | bytes 3538952 | tf_op jit(solution)/shard_map/forward1/ppermute | solution.py:175
  88.0 5.0 %collective-permute-start.16 = (f32[64,64]{1,0:T(8,128)S(1)}, f32[64,64]{1,0:T(8,128)S(1)}, u32[]{:S(2)}, u32[]{:S(2)}) collective-permute-start(f32[64,64]{1,0:T(8,128)S(1)} %add.307), channel_id=1, source_target_pairs={{0,10},{1,11},{2,8},{3,9},{4,14},{5,15},{6,12},{7,13},{8,2},{9,3},... | collective-permute-start | bytes 49160 | tf_op jit(solution)/shard_map/around/ppermute | solution.py:175
  93.0 0.6 collective-permute-start.15
  93.6 0.9 collective-permute-start.14
  94.5 9.6 %shard_map.61 = (f32[192,768]{1,0:T(8,128)}, f32[192,768]{1,0:T(8,128)}, f32[192,768]{1,0:T(8,128)}, f32[192,768]{1,0:T(8,128)}) custom-call(s32[16]{0:T(128)} %stack.194.off, bf16[192,3072]{1,0:T(8,128)(2,1)} %copy-done.4, bf16[192,3072]{1,0:T(8,128)(2,1)} %collective-permute-done.rest_1_, bf16[192,3072]{1,0:T(8,128)(2,1)} %copy-done.7, ...), custom_call_target="tpu_custom_call" | custom-call | flops 3623878656 | bytes 11796480 | tf_op jit(solution)/shard_map/pallas_call | solution.py:50
  104.2 0.7 collective-permute-done.14
  104.9 3.1 %collective-permute-start.22 = (f32[192,768]{1,0:T(8,128)}, f32[192,768]{1,0:T(8,128)S(1)}, u32[]{:S(2)}, u32[]{:S(2)}) collective-permute-start(f32[192,768]{1,0:T(8,128)} %get-tuple-element.65), channel_id=1, source_target_pairs={{0,12},{1,13},{2,14},{3,15},{4,8},{5,9},{6,10},{7,11},{8,4},{9,5},... | collective-permute-start | bytes 1769480 | tf_op jit(solution)/shard_map/back03/ppermute | solution.py:175
  107.9 0.5 collective-permute-start.20
  108.4 0.6 collective-permute-start.18
  109.0 0.6 multiply_reduce_fusion
  109.6 0.6 broadcast_in_dim.2
  110.3 0.7 collective-permute-start.17
  111.0 9.6 %shard_map.60 = (f32[192,768]{1,0:T(8,128)}, f32[192,768]{1,0:T(8,128)}, f32[192,768]{1,0:T(8,128)}, f32[192,768]{1,0:T(8,128)}) custom-call(s32[16]{0:T(128)} %stack.194.off, bf16[192,3072]{1,0:T(8,128)(2,1)} %copy-done.4, bf16[192,3072]{1,0:T(8,128)(2,1)} %collective-permute-done.rest_1_, bf16[192,3072]{1,0:T(8,128)(2,1)} %copy-done.7, ...), custom_call_target="tpu_custom_call" | custom-call | flops 3623878656 | bytes 11796480 | tf_op jit(solution)/shard_map/pallas_call | solution.py:50
  120.6 1.9 %collective-permute-done.22.rest_3_ = f32[192,768]{1,0:T(8,128)S(1)} collective-permute-done((f32[192,768]{1,0:T(8,128)}, f32[192,768]{1,0:T(8,128)S(1)}, u32[]{:S(2)}, u32[]{:S(2)}) %collective-permute-start.22) | collective-permute-done | bytes 589856 | tf_op jit(solution)/shard_map/back03/ppermute | solution.py:175
  122.5 0.9 collective-permute-done.18.rest_1_
  123.4 1.4 collective-permute-start.19
  124.8 3.1 %collective-permute-start.21 = (f32[192,768]{1,0:T(8,128)}, f32[192,768]{1,0:T(8,128)S(1)}, u32[]{:S(2)}, u32[]{:S(2)}) collective-permute-start(f32[192,768]{1,0:T(8,128)} %get-tuple-element.63), channel_id=1, source_target_pairs={{0,8},{1,9},{2,10},{3,11},{4,12},{5,13},{6,14},{7,15},{8,0},{9,1},... | collective-permute-start | bytes 1769480 | tf_op jit(solution)/shard_map/back12/ppermute | solution.py:175
  127.9 0.2 collective-permute-start.23
  128.1 1.9 %collective-permute-start.24 = (f32[8,128]{1,0:T(8,128)S(1)}, f32[8,128]{1,0:T(8,128)S(1)}, u32[]{:S(2)}, u32[]{:S(2)}) collective-permute-start(f32[8,128]{1,0:T(8,128)S(1)} %add.310), channel_id=1, source_target_pairs={{0,32},{1,33},{2,34},{3,35},{4,36},{5,37},{6,38},{7,39},{8,40},{9,... | collective-permute-start | bytes 12296 | tf_op jit(solution)/shard_map/total2/ppermute | solution.py:175
  130.0 1.7 %collective-permute-done.24 = f32[8,128]{1,0:T(8,128)S(1)} collective-permute-done((f32[8,128]{1,0:T(8,128)S(1)}, f32[8,128]{1,0:T(8,128)S(1)}, u32[]{:S(2)}, u32[]{:S(2)}) %collective-permute-start.24) | collective-permute-done | bytes 4128 | tf_op jit(solution)/shard_map/total2/ppermute | solution.py:175
  131.7 3.8 %collective-permute-start.25 = (f32[8,128]{1,0:T(8,128)S(1)}, f32[8,128]{1,0:T(8,128)S(1)}, u32[]{:S(2)}, u32[]{:S(2)}) collective-permute-start(f32[8,128]{1,0:T(8,128)S(1)} %add.311), channel_id=1, source_target_pairs={{0,64},{1,65},{2,66},{3,67},{4,68},{5,69},{6,70},{7,71},{8,72},{9,... | collective-permute-start | bytes 12296 | tf_op jit(solution)/shard_map/total4/ppermute | solution.py:175
  135.5 0.1 stack.222.at
  135.6 0.1 stack.177.at
  135.7 2.0 %shard_map.62.rest_4_ = f32[2,192,3072]{2,1,0:T(8,128)} custom-call(s32[8]{0:T(128)S(1)} %stack.222.at, f32[192,768]{1,0:T(8,128)S(1)} %copy-done, f32[192,768]{1,0:T(8,128)S(1)} %collective-permute-done.18.rest_1_, f32[192,768]{1,0:T(8,128)S(1)} %collective-permute-done.20.rest_2_, f32[192,768]{1,0:T(8,128)S(1)} %collective-permute-done.22.rest_3_), custom_call_target="tpu_custom_call" | custom-call | tf_op jit(solution)/shard_map/pallas_call | solution.py:138
  137.7 0.5 slice.47
  138.9 0.6 fusion.8
  139.5 2.9 %collective-permute-done.21.rest_2_ = f32[192,768]{1,0:T(8,128)S(1)} collective-permute-done((f32[192,768]{1,0:T(8,128)}, f32[192,768]{1,0:T(8,128)S(1)}, u32[]{:S(2)}, u32[]{:S(2)}) %collective-permute-start.21) | collective-permute-done | bytes 589856 | tf_op jit(solution)/shard_map/back12/ppermute | solution.py:175
  142.4 3.2 %collective-permute-done.23.rest_3_ = f32[192,768]{1,0:T(8,128)} collective-permute-done((f32[192,768]{1,0:T(8,128)}, f32[192,768]{1,0:T(8,128)}, u32[]{:S(2)}, u32[]{:S(2)}) %collective-permute-start.23) | collective-permute-done | bytes 589856 | tf_op jit(solution)/shard_map/back13/ppermute | solution.py:175
  145.7 2.5 %shard_map.63 = f32[2,192,3072]{2,1,0:T(8,128)} custom-call(s32[8]{0:T(128)S(1)} %stack.177.at, f32[192,768]{1,0:T(8,128)S(1)} %copy-done.1, f32[192,768]{1,0:T(8,128)S(1)} %collective-permute-done.19.rest_1_, f32[192,768]{1,0:T(8,128)S(1)} %collective-permute-done.21.rest_2_, ...), custom_call_target="tpu_custom_call", output_to_operand_aliasing={{}: (5, {})} | custom-call | tf_op jit(solution)/shard_map/pallas_call | solution.py:138
  (65 shorter events, 0.4 us)
Async XLA Ops:
  0.7 6.1 %copy-start.13 = (s32[2]{0:T(128)S(1)}, s32[2]{0:T(128)}, u32[]{:S(2)}) copy-start(s32[2]{0:T(128)} %param.7) | copy-start | bytes 28
  0.7 7.3 %copy-start.2 = (bf16[2,192,3072]{2,1,0:T(8,128)(2,1)S(1)}, bf16[2,192,3072]{2,1,0:T(8,128)(2,1)}, u32[]{:S(2)}) copy-start(bf16[2,192,3072]{2,1,0:T(8,128)(2,1)} %param.5) | copy-start | bytes 7077892
  3.7 6.0 %copy-start.4 = (bf16[192,3072]{1,0:T(8,128)(2,1)}, bf16[192,3072]{1,0:T(8,128)(2,1)S(1)}, u32[]{:S(2)}) copy-start(bf16[192,3072]{1,0:T(8,128)(2,1)S(1)} %get-tuple-element.73.rest_0_) | copy-start | bytes 3538948
  3.7 32.9 %collective-permute-start.4 = (bf16[192,3072]{1,0:T(8,128)(2,1)}, bf16[192,3072]{1,0:T(8,128)(2,1)}, u32[]{:S(2)}, u32[]{:S(2)}) collective-permute-start(bf16[192,3072]{1,0:T(8,128)(2,1)} %get-tuple-element.72), channel_id=1, source_target_pairs={{0,12},{1,13},{2,14},{3,15},{4,8},{5,9},{6,10},{7,11},{8,4},{9,5},... | collective-permute-start | bytes 3538952 | tf_op jit(solution)/shard_map/left3/ppermute | solution.py:175
  6.5 30.0 %collective-permute-start = (bf16[192,3072]{1,0:T(8,128)(2,1)S(1)}, bf16[192,3072]{1,0:T(8,128)(2,1)}, u32[]{:S(2)}, u32[]{:S(2)}) collective-permute-start(bf16[192,3072]{1,0:T(8,128)(2,1)S(1)} %get-tuple-element.73.rest_0_), channel_id=1, source_target_pairs={{0,4},{1,5},{2,6},{3,7},{4,0},{5,1},{6,2},{7,3},{8,12},{9,13},{10,... | collective-permute-start | bytes 3538952 | tf_op jit(solution)/shard_map/left1/ppermute | solution.py:175
  8.0 1.6 %copy-start.5 = (bf16[2,3072,64]{1,2,0:T(8,128)(2,1)}, bf16[2,3072,64]{1,2,0:T(8,128)(2,1)S(1)}, u32[]{:S(2)}) copy-start(bf16[2,3072,64]{1,2,0:T(8,128)(2,1)S(1)} %broadcast_multiply_fusion) | copy-start | bytes 2359300
  14.6 15.0 %collective-permute-start.1 = (bf16[192,1664]{1,0:T(8,128)(2,1)S(1)}, bf16[192,1664]{1,0:T(8,128)(2,1)S(1)}, u32[]{:S(2)}, u32[]{:S(2)}) collective-permute-start(bf16[192,1664]{1,0:T(8,128)(2,1)S(1)} %pad_maximum_fusion.2), channel_id=1, source_target_pairs={{0,4},{1,5},{2,6},{3,7},{4,0},{5,1},{6,2},{7,3},{8,12},{9,13},{10,... | collective-permute-start | bytes 1916936 | tf_op jit(solution)/shard_map/right1/ppermute | solution.py:175
  16.5 19.7 %collective-permute-start.2 = (bf16[192,1664]{1,0:T(8,128)(2,1)S(1)}, bf16[192,1664]{1,0:T(8,128)(2,1)S(1)}, u32[]{:S(2)}, u32[]{:S(2)}) collective-permute-start(bf16[192,1664]{1,0:T(8,128)(2,1)S(1)} %pad_maximum_fusion.3), channel_id=1, source_target_pairs={{0,8},{1,9},{2,10},{3,11},{4,12},{5,13},{6,14},{7,15},{8,0},{9,1},... | collective-permute-start | bytes 1916936 | tf_op jit(solution)/shard_map/right2/ppermute | solution.py:175
  17.5 18.8 %collective-permute-start.3 = (bf16[192,1664]{1,0:T(8,128)(2,1)S(1)}, bf16[192,1664]{1,0:T(8,128)(2,1)S(1)}, u32[]{:S(2)}, u32[]{:S(2)}) collective-permute-start(bf16[192,1664]{1,0:T(8,128)(2,1)S(1)} %pad_maximum_fusion.4), channel_id=1, source_target_pairs={{0,12},{1,13},{2,14},{3,15},{4,8},{5,9},{6,10},{7,11},{8,4},{9,5},... | collective-permute-start | bytes 1916936 | tf_op jit(solution)/shard_map/right3/ppermute | solution.py:175
  29.6 35.0 %collective-permute-start.8 = (bf16[192,3072]{1,0:T(8,128)(2,1)}, bf16[192,3072]{1,0:T(8,128)(2,1)S(1)}, u32[]{:S(2)}, u32[]{:S(2)}) collective-permute-start(bf16[192,3072]{1,0:T(8,128)(2,1)} %get-tuple-element.72), channel_id=1, source_target_pairs={{0,8},{1,9},{2,10},{3,11},{4,12},{5,13},{6,14},{7,15},{8,0},{9,1},... | collective-permute-start | bytes 3538952 | tf_op jit(solution)/shard_map/left2/ppermute | solution.py:175
  36.5 28.5 %copy-start.3 = (bf16[4,192,896]{2,1,0:T(8,128)(2,1)}, bf16[4,192,896]{2,1,0:T(8,128)(2,1)S(1)}, u32[]{:S(2)}) copy-start(bf16[4,192,896]{2,1,0:T(8,128)(2,1)S(1)} %pad_maximum_fusion.rest_4_) | copy-start | bytes 4128772
  36.6 28.0 %collective-permute-start.6 = (bf16[4,192,896]{2,1,0:T(8,128)(2,1)S(1)}, bf16[4,192,896]{2,1,0:T(8,128)(2,1)S(1)}, u32[]{:S(2)}, u32[]{:S(2)}) collective-permute-start(bf16[4,192,896]{2,1,0:T(8,128)(2,1)S(1)} %pad_maximum_fusion.rest_4_), channel_id=1, source_target_pairs={{0,3},{1,0},{2,1},{3,2},{4,7},{5,4},{6,5},{7,6},{8,11},{9,8},{10,9... | collective-permute-start | bytes 4128776 | tf_op jit(solution)/shard_map/down0/ppermute | solution.py:175
  39.7 25.3 %collective-permute-start.5 = (bf16[4,192,896]{2,1,0:T(8,128)(2,1)S(1)}, bf16[4,192,896]{2,1,0:T(8,128)(2,1)}, u32[]{:S(2)}, u32[]{:S(2)}) collective-permute-start(bf16[4,192,896]{2,1,0:T(8,128)(2,1)S(1)} %pad_maximum_fusion.rest_4_), channel_id=1, source_target_pairs={{0,1},{1,2},{2,3},{3,0},{4,5},{5,6},{6,7},{7,4},{8,9},{9,10},{10,1... | collective-permute-start | bytes 4128776 | tf_op jit(solution)/shard_map/up0/ppermute | solution.py:175
  39.9 24.7 %collective-permute-start.7 = (bf16[4,192,128]{2,1,0:T(8,128)(2,1)S(1)}, bf16[4,192,128]{2,1,0:T(8,128)(2,1)S(1)}, u32[]{:S(2)}, u32[]{:S(2)}) collective-permute-start(bf16[4,192,128]{2,1,0:T(8,128)(2,1)S(1)} %pad_maximum_fusion.6), channel_id=1, source_target_pairs={{0,2},{1,3},{2,0},{3,1},{4,6},{5,7},{6,4},{7,5},{8,10},{9,11},{10,... | collective-permute-start | bytes 589832 | tf_op jit(solution)/shard_map/shade/ppermute | solution.py:175
  64.6 1.9 %copy-start.12 = (bf16[4,192,128]{2,1,0:T(8,128)(2,1)}, bf16[4,192,128]{2,1,0:T(8,128)(2,1)S(1)}, u32[]{:S(2)}) copy-start(bf16[4,192,128]{2,1,0:T(8,128)(2,1)S(1)} %collective-permute-done.7.rest_7_) | copy-start | bytes 589828
  64.6 1.9 %copy-start.7 = (bf16[192,3072]{1,0:T(8,128)(2,1)}, bf16[192,3072]{1,0:T(8,128)(2,1)S(1)}, u32[]{:S(2)}) copy-start(bf16[192,3072]{1,0:T(8,128)(2,1)S(1)} %collective-permute-done.8.rest_2_) | copy-start | bytes 3538948
  64.6 1.9 %copy-start.6 = (bf16[4,192,896]{2,1,0:T(8,128)(2,1)}, bf16[4,192,896]{2,1,0:T(8,128)(2,1)S(1)}, u32[]{:S(2)}) copy-start(bf16[4,192,896]{2,1,0:T(8,128)(2,1)S(1)} %collective-permute-done.6.rest_6_) | copy-start | bytes 4128772
  65.1 19.7 %collective-permute-start.9 = (bf16[4,192,896]{2,1,0:T(8,128)(2,1)}, bf16[4,192,896]{2,1,0:T(8,128)(2,1)S(1)}, u32[]{:S(2)}, u32[]{:S(2)}) collective-permute-start(bf16[4,192,896]{2,1,0:T(8,128)(2,1)} %collective-permute-done.5.rest_5_), channel_id=1, source_target_pairs={{0,1},{1,2},{2,3},{3,0},{4,5},{5,6},{6,7},{7,4},{8,9},{9,10},{10,1... | collective-permute-start | bytes 4128776 | tf_op jit(solution)/shard_map/forward0/ppermute | solution.py:175
  66.5 17.6 %collective-permute-start.10 = (bf16[4,192,768]{2,1,0:T(8,128)(2,1)}, bf16[4,192,768]{2,1,0:T(8,128)(2,1)S(1)}, u32[]{:S(2)}, u32[]{:S(2)}) collective-permute-start(bf16[4,192,768]{2,1,0:T(8,128)(2,1)} %pad_maximum_fusion.1.rest_4_), channel_id=1, source_target_pairs={{0,3},{1,0},{2,1},{3,2},{4,7},{5,4},{6,5},{7,6},{8,11},{9,8},{10,9... | collective-permute-start | bytes 3538952 | tf_op jit(solution)/shard_map/down1/ppermute | solution.py:175
  78.4 5.0 %collective-permute-start.11 = (f32[64,64]{1,0:T(8,128)}, f32[64,64]{1,0:T(8,128)S(1)}, u32[]{:S(2)}, u32[]{:S(2)}) collective-permute-start(f32[64,64]{1,0:T(8,128)} %shard_map.59), channel_id=1, source_target_pairs={{0,1},{1,0},{2,3},{3,2},{4,5},{5,4},{6,7},{7,6},{8,9},{9,8},{10,11... | collective-permute-start | bytes 49160 | tf_op jit(solution)/shard_map/corner1/ppermute | solution.py:175
  84.1 20.0 %copy-start.15 = (bf16[4,192,768]{2,1,0:T(8,128)(2,1)}, bf16[4,192,768]{2,1,0:T(8,128)(2,1)S(1)}, u32[]{:S(2)}) copy-start(bf16[4,192,768]{2,1,0:T(8,128)(2,1)S(1)} %collective-permute-done.10.rest_6_) | copy-start | bytes 3538948
  84.8 9.7 %copy-start.14 = (bf16[4,192,896]{2,1,0:T(8,128)(2,1)}, bf16[4,192,896]{2,1,0:T(8,128)(2,1)S(1)}, u32[]{:S(2)}) copy-start(bf16[4,192,896]{2,1,0:T(8,128)(2,1)S(1)} %collective-permute-done.9.rest_7_) | copy-start | bytes 4128772
  84.8 24.8 %collective-permute-start.12 = (bf16[4,192,768]{2,1,0:T(8,128)(2,1)}, bf16[4,192,768]{2,1,0:T(8,128)(2,1)}, u32[]{:S(2)}, u32[]{:S(2)}) collective-permute-start(bf16[4,192,768]{2,1,0:T(8,128)(2,1)} %pad_maximum_fusion.1.rest_4_), channel_id=1, source_target_pairs={{0,1},{1,2},{2,3},{3,0},{4,5},{5,6},{6,7},{7,4},{8,9},{9,10},{10,1... | collective-permute-start | bytes 3538952 | tf_op jit(solution)/shard_map/up1/ppermute | solution.py:175
  85.4 24.2 %collective-permute-start.13 = (bf16[4,192,768]{2,1,0:T(8,128)(2,1)S(1)}, bf16[4,192,768]{2,1,0:T(8,128)(2,1)}, u32[]{:S(2)}, u32[]{:S(2)}) collective-permute-start(bf16[4,192,768]{2,1,0:T(8,128)(2,1)S(1)} %collective-permute-done.10.rest_6_), channel_id=1, source_target_pairs={{0,3},{1,0},{2,1},{3,2},{4,7},{5,4},{6,5},{7,6},{8,11},{9,8},{10,9... | collective-permute-start | bytes 3538952 | tf_op jit(solution)/shard_map/forward1/ppermute | solution.py:175
  88.0 16.1 %collective-permute-start.16 = (f32[64,64]{1,0:T(8,128)S(1)}, f32[64,64]{1,0:T(8,128)S(1)}, u32[]{:S(2)}, u32[]{:S(2)}) collective-permute-start(f32[64,64]{1,0:T(8,128)S(1)} %add.307), channel_id=1, source_target_pairs={{0,10},{1,11},{2,8},{3,9},{4,14},{5,15},{6,12},{7,13},{8,2},{9,3},... | collective-permute-start | bytes 49160 | tf_op jit(solution)/shard_map/around/ppermute | solution.py:175
  93.0 11.1 %collective-permute-start.15 = (f32[64,64]{1,0:T(8,128)S(1)}, f32[64,64]{1,0:T(8,128)S(1)}, u32[]{:S(2)}, u32[]{:S(2)}) collective-permute-start(f32[64,64]{1,0:T(8,128)S(1)} %add.307), channel_id=1, source_target_pairs={{0,8},{1,9},{2,10},{3,11},{4,12},{5,13},{6,14},{7,15},{8,0},{9,1},... | collective-permute-start | bytes 49160 | tf_op jit(solution)/shard_map/around/ppermute | solution.py:175
  93.6 11.3 %collective-permute-start.14 = (f32[64,64]{1,0:T(8,128)S(1)}, f32[64,64]{1,0:T(8,128)S(1)}, u32[]{:S(2)}, u32[]{:S(2)}) collective-permute-start(f32[64,64]{1,0:T(8,128)S(1)} %add.307), channel_id=1, source_target_pairs={{0,2},{1,3},{2,0},{3,1},{4,6},{5,7},{6,4},{7,5},{8,10},{9,11},{10,... | collective-permute-start | bytes 49160 | tf_op jit(solution)/shard_map/around/ppermute | solution.py:175
  104.9 17.6 %collective-permute-start.22 = (f32[192,768]{1,0:T(8,128)}, f32[192,768]{1,0:T(8,128)S(1)}, u32[]{:S(2)}, u32[]{:S(2)}) collective-permute-start(f32[192,768]{1,0:T(8,128)} %get-tuple-element.65), channel_id=1, source_target_pairs={{0,12},{1,13},{2,14},{3,15},{4,8},{5,9},{6,10},{7,11},{8,4},{9,5},... | collective-permute-start | bytes 1769480 | tf_op jit(solution)/shard_map/back03/ppermute | solution.py:175
  107.9 14.6 %collective-permute-start.20 = (f32[192,768]{1,0:T(8,128)}, f32[192,768]{1,0:T(8,128)S(1)}, u32[]{:S(2)}, u32[]{:S(2)}) collective-permute-start(f32[192,768]{1,0:T(8,128)} %get-tuple-element.62), channel_id=1, source_target_pairs={{0,8},{1,9},{2,10},{3,11},{4,12},{5,13},{6,14},{7,15},{8,0},{9,1},... | collective-permute-start | bytes 1769480 | tf_op jit(solution)/shard_map/back02/ppermute | solution.py:175
  108.4 15.0 %collective-permute-start.18 = (f32[192,768]{1,0:T(8,128)}, f32[192,768]{1,0:T(8,128)S(1)}, u32[]{:S(2)}, u32[]{:S(2)}) collective-permute-start(f32[192,768]{1,0:T(8,128)} %get-tuple-element.58), channel_id=1, source_target_pairs={{0,4},{1,5},{2,6},{3,7},{4,0},{5,1},{6,2},{7,3},{8,12},{9,13},{10,... | collective-permute-start | bytes 1769480 | tf_op jit(solution)/shard_map/back01/ppermute | solution.py:175
  109.0 0.7 copy-start.8
  109.0 1.3 copy-start.10
  110.3 25.4 %copy-start = (f32[192,768]{1,0:T(8,128)S(1)}, f32[192,768]{1,0:T(8,128)}, u32[]{:S(2)}) copy-start(f32[192,768]{1,0:T(8,128)} %get-tuple-element.67.rest_0_) | copy-start | bytes 1769476
  110.3 10.3 %collective-permute-start.17 = (f32[8,128]{1,0:T(8,128)S(1)}, f32[8,128]{1,0:T(8,128)S(1)}, u32[]{:S(2)}, u32[]{:S(2)}) collective-permute-start(f32[8,128]{1,0:T(8,128)S(1)} %broadcast_in_dim.2), channel_id=1, source_target_pairs={{0,16},{1,17},{2,18},{3,19},{4,20},{5,21},{6,22},{7,23},{8,24},{9,... | collective-permute-start | bytes 12296 | tf_op jit(solution)/shard_map/total1/ppermute | solution.py:175
  123.4 16.2 %collective-permute-start.19 = (f32[192,768]{1,0:T(8,128)}, f32[192,768]{1,0:T(8,128)S(1)}, u32[]{:S(2)}, u32[]{:S(2)}) collective-permute-start(f32[192,768]{1,0:T(8,128)} %get-tuple-element.60), channel_id=1, source_target_pairs={{0,4},{1,5},{2,6},{3,7},{4,0},{5,1},{6,2},{7,3},{8,12},{9,13},{10,... | collective-permute-start | bytes 1769480 | tf_op jit(solution)/shard_map/back11/ppermute | solution.py:175
  124.8 17.6 %collective-permute-start.21 = (f32[192,768]{1,0:T(8,128)}, f32[192,768]{1,0:T(8,128)S(1)}, u32[]{:S(2)}, u32[]{:S(2)}) collective-permute-start(f32[192,768]{1,0:T(8,128)} %get-tuple-element.63), channel_id=1, source_target_pairs={{0,8},{1,9},{2,10},{3,11},{4,12},{5,13},{6,14},{7,15},{8,0},{9,1},... | collective-permute-start | bytes 1769480 | tf_op jit(solution)/shard_map/back12/ppermute | solution.py:175
  127.9 17.7 %collective-permute-start.23 = (f32[192,768]{1,0:T(8,128)}, f32[192,768]{1,0:T(8,128)}, u32[]{:S(2)}, u32[]{:S(2)}) collective-permute-start(f32[192,768]{1,0:T(8,128)} %get-tuple-element.66), channel_id=1, source_target_pairs={{0,12},{1,13},{2,14},{3,15},{4,8},{5,9},{6,10},{7,11},{8,4},{9,5},... | collective-permute-start | bytes 1769480 | tf_op jit(solution)/shard_map/back13/ppermute | solution.py:175
  128.1 3.6 %collective-permute-start.24 = (f32[8,128]{1,0:T(8,128)S(1)}, f32[8,128]{1,0:T(8,128)S(1)}, u32[]{:S(2)}, u32[]{:S(2)}) collective-permute-start(f32[8,128]{1,0:T(8,128)S(1)} %add.310), channel_id=1, source_target_pairs={{0,32},{1,33},{2,34},{3,35},{4,36},{5,37},{6,38},{7,39},{8,40},{9,... | collective-permute-start | bytes 12296 | tf_op jit(solution)/shard_map/total2/ppermute | solution.py:175
  131.7 6.0 %collective-permute-start.25 = (f32[8,128]{1,0:T(8,128)S(1)}, f32[8,128]{1,0:T(8,128)S(1)}, u32[]{:S(2)}, u32[]{:S(2)}) collective-permute-start(f32[8,128]{1,0:T(8,128)S(1)} %add.311), channel_id=1, source_target_pairs={{0,64},{1,65},{2,66},{3,67},{4,68},{5,69},{6,70},{7,71},{8,72},{9,... | collective-permute-start | bytes 12296 | tf_op jit(solution)/shard_map/total4/ppermute | solution.py:175
  135.7 3.2 %copy-start.9 = (f32[1,64,64]{2,1,0:T(8,128)S(1)}, f32[1,64,64]{2,1,0:T(8,128)}, u32[]{:S(2)}) copy-start(f32[1,64,64]{2,1,0:T(8,128)} %copy-done.8) | copy-start | bytes 49156
  135.7 3.2 %copy-start.11 = (f32[1,64,64]{2,1,0:T(8,128)S(1)}, f32[1,64,64]{2,1,0:T(8,128)}, u32[]{:S(2)}) copy-start(f32[1,64,64]{2,1,0:T(8,128)} %copy-done.10) | copy-start | bytes 49156
  135.7 9.9 %copy-start.1 = (f32[192,768]{1,0:T(8,128)S(1)}, f32[192,768]{1,0:T(8,128)}, u32[]{:S(2)}) copy-start(f32[192,768]{1,0:T(8,128)} %get-tuple-element.56.rest_0_) | copy-start | bytes 1769476

commit v5 on v4

--- a/solution.py
+++ b/solution.py
@@ -248,15 +248,16 @@
         around = [corner] + [send(corner, table, "around") for table in (along_h[2], along_g[2], diagonal)]
         skips = (extra,) * 4
         out0 = product(offsets, left, (own0, below0, above0, beyond0), skips, width)
-        out0, around = lax.optimization_barrier((out0, around))
-        out0 = back(0, out0)
+        longest = out0[2]
+        out0, around = lax.optimization_barrier(([out0[0], out0[1], out0[3]], around))
+        out0 = back(0, [out0[0], out0[1], longest, out0[2]])
         corner, beside = around[0] + around[1], around[2] + around[3]
         corner = jnp.where(sector == 0, jnp.stack([corner, beside]), jnp.stack([beside, corner]))
         total = after(jnp.broadcast_to(jnp.sum(corner * corner), (8, 128)), below1, beyond1)
         total = total + send(total, across[1], "total1")
         out1 = product(offsets, left, (own1, below1, above1, beyond1), (0,) * 4, width)
         first, total = lax.optimization_barrier((out1[0], total))
-        out1 = [first] + [after(out1[p], out0[p], total) for p in (1, 2, 3)]
+        out1 = [first, after(out1[1], *out0[1:]), after(out1[2], out0[2], total), after(out1[3], *out0[1:])]
         out1 = back(1, out1)
         enlarged = put(1, out1, put(0, out0, None))
         for p in (2, 4):

time: 149 us -> 145 us (0.973)
  waiting for transfers between devices: 55.5 us -> 50.6 us
    ppermute x26, waiting for transfers between devices: 55.5 us -> 50.6 us  [send(): return lax.ppermute(value, ('row', 'col'), table)]
  transfers between devices with their start and end apart: 26 -> 26, of which waited for: 12 -> 9; matrix products, arithmetic and copies ran while one was open for 10% -> 11% of each run, Pallas kernels for 19% -> 19%
where the time goes in v5:
time: 145 us; the launch traced here: 144 us
  waiting for transfers between devices  50.6 us (35%)
  starting transfers between devices  43.3 us (30%)
  Pallas kernels  30 us (21%)
  local copies, waits for them, and re-layouts  9.77 us (7%)
  other arithmetic  7.13 us (5%)
  between operations  1.88 us (1%)
  matrix products  1.58 us (1%)
    ppermute x26, waiting for transfers between devices, send(): return lax.ppermute(value, ('row', 'col'), table)  50.6 us
    ppermute x26, starting transfers between devices, send(): return lax.ppermute(value, ('row', 'col'), table)  43.3 us
    pallas_call x2, Pallas kernels, product(): pl.pallas_call(kernel, in_specs=[pl.BlockSpec(memory_space=pltpu.SMEM)] +...  19.2 us
    pallas_call x1, Pallas kernels, share(): pl.pallas_call(kernel, in_specs=[pl.BlockSpec(memory_space=pltpu.SMEM), i...  6.31 us
    pallas_call x2, Pallas kernels, place(): pl.pallas_call(kernel, in_specs=[pl.BlockSpec(memory_space=pltpu.SMEM)] +...  4.49 us
    squeeze x1, local copies, waits for them, and re-layouts, body(): other = lax.dynamic_index_in_dim(left_edge, 1 - sector, 0, keepdims=False)  2.96 us
  transfers between devices with their start and end apart: 26, of which 9 were waited for; matrix products, arithmetic and copies ran while one was open for 11% of the time, Pallas kernels for 19%

profile of v5, /device:TPU:0, one launch (start us, length us, event | category | flops | bytes accessed | tf_op | source)
XLA Modules:
  0.0 144.1 jit_solution(9443854314374042469)
XLA Ops:
  0.7 3.0 %dynamic-slice_bitcast_fusion = (bf16[192,3072]{1,0:T(8,128)(2,1)}, bf16[192,3072]{1,0:T(8,128)(2,1)S(1)}) fusion(bf16[2,192,3072]{2,1,0:T(8,128)(2,1)} %param.4, s32[]{:T(128)S(6)} %select_n.241, s32[]{:T(128)S(6)} %select_n.240), kind=kLoop, calls=%fused_computation.2 | loop fusion | bytes 4718600 | tf_op jit(solution)/shard_map/jit(dynamic_index_in_dim)/squeeze | solution.py:198
  3.7 2.8 %collective-permute-start.4 = (bf16[192,3072]{1,0:T(8,128)(2,1)}, bf16[192,3072]{1,0:T(8,128)(2,1)}, u32[]{:S(2)}, u32[]{:S(2)}) collective-permute-start(bf16[192,3072]{1,0:T(8,128)(2,1)} %get-tuple-element.70), channel_id=1, source_target_pairs={{0,12},{1,13},{2,14},{3,15},{4,8},{5,9},{6,10},{7,11},{8,4},{9,5},... | collective-permute-start | bytes 3538952 | tf_op jit(solution)/shard_map/left3/ppermute | solution.py:175
  6.5 0.2 collective-permute-start
  6.8 0.1 compare_convert_fusion
  6.8 1.2 broadcast_multiply_fusion
  8.1 1.6 %fusion.9 = (f32[2,192,64]{1,2,0:T(8,128)}, f32[2,192,64]{1,2,0:T(8,128)}) fusion(bf16[2,192,3072]{2,1,0:T(8,128)(2,1)S(1)} %copy-done.2, bf16[2,3072,64]{1,2,0:T(8,128)(2,1)S(1)} %broadcast_multiply_fusion), kind=kOutput, calls=%fused_computation.52 | convolution fusion | flops 151019520 | bytes 3342336 | tf_op jit(solution)/shard_map/skj,sjq->skq/dot_general | solution.py:201
  9.6 1.7 %copy.9 = f32[2,192,64]{2,1,0:T(8,128)} copy(f32[2,192,64]{1,2,0:T(8,128)} %get-tuple-element.82) | data formatting | bytes 196608 | tf_op jit(solution)/shard_map/reduce_precision | solution.py:202
  11.3 1.7 %copy.10 = f32[2,192,64]{2,1,0:T(8,128)} copy(f32[2,192,64]{1,2,0:T(8,128)} %get-tuple-element.83) | data formatting | bytes 196608 | tf_op jit(solution)/shard_map/skj,sjq->skq/dot_general | solution.py:201
  13.0 1.1 subtract_convert_fusion
  14.2 0.1 fusion.3
  14.3 0.2 dynamic-slice_bitcast_fusion.5
  14.5 0.1 pad_maximum_fusion.2
  14.6 1.9 %collective-permute-start.1 = (bf16[192,1664]{1,0:T(8,128)(2,1)S(1)}, bf16[192,1664]{1,0:T(8,128)(2,1)S(1)}, u32[]{:S(2)}, u32[]{:S(2)}) collective-permute-start(bf16[192,1664]{1,0:T(8,128)(2,1)S(1)} %pad_maximum_fusion.2), channel_id=1, source_target_pairs={{0,4},{1,5},{2,6},{3,7},{4,0},{5,1},{6,2},{7,3},{8,12},{9,13},{10,... | collective-permute-start | bytes 1916936 | tf_op jit(solution)/shard_map/right1/ppermute | solution.py:175
  16.5 0.1 pad_maximum_fusion.3
  16.5 0.9 collective-permute-start.2
  17.4 0.1 pad_maximum_fusion.4
  17.5 2.2 %collective-permute-start.3 = (bf16[192,1664]{1,0:T(8,128)(2,1)S(1)}, bf16[192,1664]{1,0:T(8,128)(2,1)S(1)}, u32[]{:S(2)}, u32[]{:S(2)}) collective-permute-start(bf16[192,1664]{1,0:T(8,128)(2,1)S(1)} %pad_maximum_fusion.4), channel_id=1, source_target_pairs={{0,12},{1,13},{2,14},{3,15},{4,8},{5,9},{6,10},{7,11},{8,4},{9,5},... | collective-permute-start | bytes 1916936 | tf_op jit(solution)/shard_map/right3/ppermute | solution.py:175
  19.7 9.9 %collective-permute-done.1 = bf16[192,1664]{1,0:T(8,128)(2,1)S(1)} collective-permute-done((bf16[192,1664]{1,0:T(8,128)(2,1)S(1)}, bf16[192,1664]{1,0:T(8,128)(2,1)S(1)}, u32[]{:S(2)}, u32[]{:S(2)}) %collective-permute-start.1) | collective-permute-done | bytes 639008 | tf_op jit(solution)/shard_map/right1/ppermute | solution.py:175
  29.6 0.8 collective-permute-start.8
  30.4 5.8 %collective-permute-done.2 = bf16[192,1664]{1,0:T(8,128)(2,1)S(1)} collective-permute-done((bf16[192,1664]{1,0:T(8,128)(2,1)S(1)}, bf16[192,1664]{1,0:T(8,128)(2,1)S(1)}, u32[]{:S(2)}, u32[]{:S(2)}) %collective-permute-start.2) | collective-permute-done | bytes 639008 | tf_op jit(solution)/shard_map/right2/ppermute | solution.py:175
  36.3 0.2 pad_maximum_fusion.rest_4_
  36.5 0.0 copy-start.3
  36.6 3.2 %collective-permute-start.6 = (bf16[4,192,896]{2,1,0:T(8,128)(2,1)S(1)}, bf16[4,192,896]{2,1,0:T(8,128)(2,1)S(1)}, u32[]{:S(2)}, u32[]{:S(2)}) collective-permute-start(bf16[4,192,896]{2,1,0:T(8,128)(2,1)S(1)} %pad_maximum_fusion.rest_4_), channel_id=1, source_target_pairs={{0,3},{1,0},{2,1},{3,2},{4,7},{5,4},{6,5},{7,6},{8,11},{9,8},{10,9... | collective-permute-start | bytes 4128776 | tf_op jit(solution)/shard_map/down0/ppermute | solution.py:175
  39.9 2.3 %collective-permute-start.7 = (bf16[4,192,128]{2,1,0:T(8,128)(2,1)S(1)}, bf16[4,192,128]{2,1,0:T(8,128)(2,1)S(1)}, u32[]{:S(2)}, u32[]{:S(2)}) collective-permute-start(bf16[4,192,128]{2,1,0:T(8,128)(2,1)S(1)} %pad_maximum_fusion.6), channel_id=1, source_target_pairs={{0,2},{1,3},{2,0},{3,1},{4,6},{5,7},{6,4},{7,5},{8,10},{9,11},{10,... | collective-permute-start | bytes 589832 | tf_op jit(solution)/shard_map/shade/ppermute | solution.py:175
  42.2 22.4 %collective-permute-done.7.rest_7_ = bf16[4,192,128]{2,1,0:T(8,128)(2,1)S(1)} collective-permute-done((bf16[4,192,128]{2,1,0:T(8,128)(2,1)S(1)}, bf16[4,192,128]{2,1,0:T(8,128)(2,1)S(1)}, u32[]{:S(2)}, u32[]{:S(2)}) %collective-permute-start.7) | collective-permute-done | bytes 196640 | tf_op jit(solution)/shard_map/shade/ppermute | solution.py:175
  64.6 0.5 collective-permute-done.5.rest_5_
  65.1 1.4 pad_maximum_fusion.1.rest_4_
  66.5 3.2 %collective-permute-start.10 = (bf16[4,192,768]{2,1,0:T(8,128)(2,1)}, bf16[4,192,768]{2,1,0:T(8,128)(2,1)S(1)}, u32[]{:S(2)}, u32[]{:S(2)}) collective-permute-start(bf16[4,192,768]{2,1,0:T(8,128)(2,1)} %pad_maximum_fusion.1.rest_4_), channel_id=1, source_target_pairs={{0,3},{1,0},{2,1},{3,2},{4,7},{5,4},{6,5},{7,6},{8,11},{9,8},{10,9... | collective-permute-start | bytes 3538952 | tf_op jit(solution)/shard_map/down1/ppermute | solution.py:175
  69.7 0.6 stack.194.off
  70.4 1.0 dynamic-slice_bitcast_fusion.9
  71.4 0.7 pad_maximum_fusion.7.pick
  72.0 6.3 %shard_map.59 = f32[64,64]{1,0:T(8,128)} custom-call(s32[16]{0:T(128)} %stack.194.off, bf16[4,64,192]{2,1,0:T(8,128)(2,1)} %pad_maximum_fusion.7.pick, bf16[192,3072]{1,0:T(8,128)(2,1)} %copy-done.4, bf16[192,3072]{1,0:T(8,128)(2,1)} %collective-permute-done.rest_1_, bf16[192,3072]{1,0:T(8,128)(2,1)} %copy-done.7, ...), custom_call_target="tpu_custom_call" | custom-call | flops 603979776 | bytes 5505024 | tf_op jit(solution)/shard_map/pallas_call | solution.py:100
  78.4 0.1 collective-permute-start.11
  78.5 4.9 %collective-permute-done.11 = f32[64,64]{1,0:T(8,128)S(1)} collective-permute-done((f32[64,64]{1,0:T(8,128)}, f32[64,64]{1,0:T(8,128)S(1)}, u32[]{:S(2)}, u32[]{:S(2)}) %collective-permute-start.11) | collective-permute-done | bytes 16416 | tf_op jit(solution)/shard_map/corner1/ppermute | solution.py:175
  83.3 0.8 add.307
  84.1 0.7 collective-permute-done.9.rest_7_
  84.8 0.6 collective-permute-start.12
  85.4 2.6 %collective-permute-start.13 = (bf16[4,192,768]{2,1,0:T(8,128)(2,1)S(1)}, bf16[4,192,768]{2,1,0:T(8,128)(2,1)}, u32[]{:S(2)}, u32[]{:S(2)}) collective-permute-start(bf16[4,192,768]{2,1,0:T(8,128)(2,1)S(1)} %collective-permute-done.10.rest_6_), channel_id=1, source_target_pairs={{0,3},{1,0},{2,1},{3,2},{4,7},{5,4},{6,5},{7,6},{8,11},{9,8},{10,9... | collective-permute-start | bytes 3538952 | tf_op jit(solution)/shard_map/forward1/ppermute | solution.py:175
  88.0 5.0 %collective-permute-start.16 = (f32[64,64]{1,0:T(8,128)S(1)}, f32[64,64]{1,0:T(8,128)S(1)}, u32[]{:S(2)}, u32[]{:S(2)}) collective-permute-start(f32[64,64]{1,0:T(8,128)S(1)} %add.307), channel_id=1, source_target_pairs={{0,10},{1,11},{2,8},{3,9},{4,14},{5,15},{6,12},{7,13},{8,2},{9,3},... | collective-permute-start | bytes 49160 | tf_op jit(solution)/shard_map/around/ppermute | solution.py:175
  93.0 0.6 collective-permute-start.15
  93.6 0.9 collective-permute-start.14
  94.5 9.6 %shard_map.61 = (f32[192,768]{1,0:T(8,128)}, f32[192,768]{1,0:T(8,128)}, f32[192,768]{1,0:T(8,128)}, f32[192,768]{1,0:T(8,128)}) custom-call(s32[16]{0:T(128)} %stack.194.off, bf16[192,3072]{1,0:T(8,128)(2,1)} %copy-done.4, bf16[192,3072]{1,0:T(8,128)(2,1)} %collective-permute-done.rest_1_, bf16[192,3072]{1,0:T(8,128)(2,1)} %copy-done.7, ...), custom_call_target="tpu_custom_call" | custom-call | flops 3623878656 | bytes 11796480 | tf_op jit(solution)/shard_map/pallas_call | solution.py:50
  104.2 3.1 %collective-permute-start.19 = (f32[192,768]{1,0:T(8,128)}, f32[192,768]{1,0:T(8,128)S(1)}, u32[]{:S(2)}, u32[]{:S(2)}) collective-permute-start(f32[192,768]{1,0:T(8,128)} %get-tuple-element.57), channel_id=1, source_target_pairs={{0,8},{1,9},{2,10},{3,11},{4,12},{5,13},{6,14},{7,15},{8,0},{9,1},... | collective-permute-start | bytes 1769480 | tf_op jit(solution)/shard_map/back02/ppermute | solution.py:175
  107.3 0.6 collective-permute-start.18
  107.9 0.9 collective-permute-start.20
  108.8 0.0 copy-start.10
  108.8 0.6 multiply_reduce_fusion
  109.4 0.6 broadcast_in_dim.2
  110.1 0.9 collective-permute-start.17
  111.0 9.6 %shard_map.60 = (f32[192,768]{1,0:T(8,128)}, f32[192,768]{1,0:T(8,128)}, f32[192,768]{1,0:T(8,128)}, f32[192,768]{1,0:T(8,128)}) custom-call(s32[16]{0:T(128)} %stack.194.off, bf16[192,3072]{1,0:T(8,128)(2,1)} %copy-done.4, bf16[192,3072]{1,0:T(8,128)(2,1)} %collective-permute-done.rest_1_, bf16[192,3072]{1,0:T(8,128)(2,1)} %copy-done.7, ...), custom_call_target="tpu_custom_call" | custom-call | flops 3623878656 | bytes 11796480 | tf_op jit(solution)/shard_map/pallas_call | solution.py:50
  120.6 1.7 %collective-permute-done.18.rest_1_ = f32[192,768]{1,0:T(8,128)S(1)} collective-permute-done((f32[192,768]{1,0:T(8,128)}, f32[192,768]{1,0:T(8,128)S(1)}, u32[]{:S(2)}, u32[]{:S(2)}) %collective-permute-start.18) | collective-permute-done | bytes 589856 | tf_op jit(solution)/shard_map/back01/ppermute | solution.py:175
  122.3 2.6 %collective-permute-start.23 = (f32[192,768]{1,0:T(8,128)}, f32[192,768]{1,0:T(8,128)S(1)}, u32[]{:S(2)}, u32[]{:S(2)}) collective-permute-start(f32[192,768]{1,0:T(8,128)} %get-tuple-element.64), channel_id=1, source_target_pairs={{0,12},{1,13},{2,14},{3,15},{4,8},{5,9},{6,10},{7,11},{8,4},{9,5},... | collective-permute-start | bytes 1769480 | tf_op jit(solution)/shard_map/back13/ppermute | solution.py:175
  124.9 0.2 collective-permute-start.21
  125.1 1.8 %collective-permute-start.22 = (f32[192,768]{1,0:T(8,128)}, f32[192,768]{1,0:T(8,128)}, u32[]{:S(2)}, u32[]{:S(2)}) collective-permute-start(f32[192,768]{1,0:T(8,128)} %get-tuple-element.62), channel_id=1, source_target_pairs={{0,8},{1,9},{2,10},{3,11},{4,12},{5,13},{6,14},{7,15},{8,0},{9,1},... | collective-permute-start | bytes 1769480 | tf_op jit(solution)/shard_map/back12/ppermute | solution.py:175
  127.0 1.9 %collective-permute-start.24 = (f32[8,128]{1,0:T(8,128)S(1)}, f32[8,128]{1,0:T(8,128)S(1)}, u32[]{:S(2)}, u32[]{:S(2)}) collective-permute-start(f32[8,128]{1,0:T(8,128)S(1)} %add.310), channel_id=1, source_target_pairs={{0,32},{1,33},{2,34},{3,35},{4,36},{5,37},{6,38},{7,39},{8,40},{9,... | collective-permute-start | bytes 12296 | tf_op jit(solution)/shard_map/total2/ppermute | solution.py:175
  128.9 1.7 %collective-permute-done.24 = f32[8,128]{1,0:T(8,128)S(1)} collective-permute-done((f32[8,128]{1,0:T(8,128)S(1)}, f32[8,128]{1,0:T(8,128)S(1)}, u32[]{:S(2)}, u32[]{:S(2)}) %collective-permute-start.24) | collective-permute-done | bytes 4128 | tf_op jit(solution)/shard_map/total2/ppermute | solution.py:175
  130.6 3.9 %collective-permute-start.25 = (f32[8,128]{1,0:T(8,128)S(1)}, f32[8,128]{1,0:T(8,128)S(1)}, u32[]{:S(2)}, u32[]{:S(2)}) collective-permute-start(f32[8,128]{1,0:T(8,128)S(1)} %add.311), channel_id=1, source_target_pairs={{0,64},{1,65},{2,66},{3,67},{4,68},{5,69},{6,70},{7,71},{8,72},{9,... | collective-permute-start | bytes 12296 | tf_op jit(solution)/shard_map/total4/ppermute | solution.py:175
  134.5 0.1 stack.222.at
  134.6 0.1 stack.177.at
  134.7 2.0 %shard_map.62.rest_4_ = f32[2,192,3072]{2,1,0:T(8,128)} custom-call(s32[8]{0:T(128)S(1)} %stack.222.at, f32[192,768]{1,0:T(8,128)S(1)} %copy-done, f32[192,768]{1,0:T(8,128)S(1)} %collective-permute-done.18.rest_1_, f32[192,768]{1,0:T(8,128)S(1)} %collective-permute-done.19.rest_2_, f32[192,768]{1,0:T(8,128)S(1)} %collective-permute-done.20.rest_3_), custom_call_target="tpu_custom_call" | custom-call | tf_op jit(solution)/shard_map/pallas_call | solution.py:138
  136.7 0.5 slice.47
  137.8 0.6 fusion.8
  138.5 3.0 %collective-permute-done.22.rest_2_ = f32[192,768]{1,0:T(8,128)} collective-permute-done((f32[192,768]{1,0:T(8,128)}, f32[192,768]{1,0:T(8,128)}, u32[]{:S(2)}, u32[]{:S(2)}) %collective-permute-start.22) | collective-permute-done | bytes 589856 | tf_op jit(solution)/shard_map/back12/ppermute | solution.py:175
  141.5 2.5 %shard_map.63 = f32[2,192,3072]{2,1,0:T(8,128)} custom-call(s32[8]{0:T(128)S(1)} %stack.177.at, f32[192,768]{1,0:T(8,128)S(1)} %copy-done.1, f32[192,768]{1,0:T(8,128)S(1)} %collective-permute-done.21.rest_1_, f32[192,768]{1,0:T(8,128)} %collective-permute-done.22.rest_2_, ...), custom_call_target="tpu_custom_call", output_to_operand_aliasing={{}: (5, {})} | custom-call | tf_op jit(solution)/shard_map/pallas_call | solution.py:138
  (65 shorter events, 0.4 us)
Async XLA Ops:
  0.7 6.1 %copy-start.13 = (s32[2]{0:T(128)S(1)}, s32[2]{0:T(128)}, u32[]{:S(2)}) copy-start(s32[2]{0:T(128)} %param.7) | copy-start | bytes 28
  0.7 7.3 %copy-start.2 = (bf16[2,192,3072]{2,1,0:T(8,128)(2,1)S(1)}, bf16[2,192,3072]{2,1,0:T(8,128)(2,1)}, u32[]{:S(2)}) copy-start(bf16[2,192,3072]{2,1,0:T(8,128)(2,1)} %param.5) | copy-start | bytes 7077892
  3.7 6.0 %copy-start.4 = (bf16[192,3072]{1,0:T(8,128)(2,1)}, bf16[192,3072]{1,0:T(8,128)(2,1)S(1)}, u32[]{:S(2)}) copy-start(bf16[192,3072]{1,0:T(8,128)(2,1)S(1)} %get-tuple-element.71.rest_0_) | copy-start | bytes 3538948
  3.7 32.9 %collective-permute-start.4 = (bf16[192,3072]{1,0:T(8,128)(2,1)}, bf16[192,3072]{1,0:T(8,128)(2,1)}, u32[]{:S(2)}, u32[]{:S(2)}) collective-permute-start(bf16[192,3072]{1,0:T(8,128)(2,1)} %get-tuple-element.70), channel_id=1, source_target_pairs={{0,12},{1,13},{2,14},{3,15},{4,8},{5,9},{6,10},{7,11},{8,4},{9,5},... | collective-permute-start | bytes 3538952 | tf_op jit(solution)/shard_map/left3/ppermute | solution.py:175
  6.5 30.0 %collective-permute-start = (bf16[192,3072]{1,0:T(8,128)(2,1)S(1)}, bf16[192,3072]{1,0:T(8,128)(2,1)}, u32[]{:S(2)}, u32[]{:S(2)}) collective-permute-start(bf16[192,3072]{1,0:T(8,128)(2,1)S(1)} %get-tuple-element.71.rest_0_), channel_id=1, source_target_pairs={{0,4},{1,5},{2,6},{3,7},{4,0},{5,1},{6,2},{7,3},{8,12},{9,13},{10,... | collective-permute-start | bytes 3538952 | tf_op jit(solution)/shard_map/left1/ppermute | solution.py:175
  8.0 1.6 %copy-start.5 = (bf16[2,3072,64]{1,2,0:T(8,128)(2,1)}, bf16[2,3072,64]{1,2,0:T(8,128)(2,1)S(1)}, u32[]{:S(2)}) copy-start(bf16[2,3072,64]{1,2,0:T(8,128)(2,1)S(1)} %broadcast_multiply_fusion) | copy-start | bytes 2359300
  14.6 15.0 %collective-permute-start.1 = (bf16[192,1664]{1,0:T(8,128)(2,1)S(1)}, bf16[192,1664]{1,0:T(8,128)(2,1)S(1)}, u32[]{:S(2)}, u32[]{:S(2)}) collective-permute-start(bf16[192,1664]{1,0:T(8,128)(2,1)S(1)} %pad_maximum_fusion.2), channel_id=1, source_target_pairs={{0,4},{1,5},{2,6},{3,7},{4,0},{5,1},{6,2},{7,3},{8,12},{9,13},{10,... | collective-permute-start | bytes 1916936 | tf_op jit(solution)/shard_map/right1/ppermute | solution.py:175
  16.5 19.7 %collective-permute-start.2 = (bf16[192,1664]{1,0:T(8,128)(2,1)S(1)}, bf16[192,1664]{1,0:T(8,128)(2,1)S(1)}, u32[]{:S(2)}, u32[]{:S(2)}) collective-permute-start(bf16[192,1664]{1,0:T(8,128)(2,1)S(1)} %pad_maximum_fusion.3), channel_id=1, source_target_pairs={{0,8},{1,9},{2,10},{3,11},{4,12},{5,13},{6,14},{7,15},{8,0},{9,1},... | collective-permute-start | bytes 1916936 | tf_op jit(solution)/shard_map/right2/ppermute | solution.py:175
  17.5 18.8 %collective-permute-start.3 = (bf16[192,1664]{1,0:T(8,128)(2,1)S(1)}, bf16[192,1664]{1,0:T(8,128)(2,1)S(1)}, u32[]{:S(2)}, u32[]{:S(2)}) collective-permute-start(bf16[192,1664]{1,0:T(8,128)(2,1)S(1)} %pad_maximum_fusion.4), channel_id=1, source_target_pairs={{0,12},{1,13},{2,14},{3,15},{4,8},{5,9},{6,10},{7,11},{8,4},{9,5},... | collective-permute-start | bytes 1916936 | tf_op jit(solution)/shard_map/right3/ppermute | solution.py:175
  29.6 35.0 %collective-permute-start.8 = (bf16[192,3072]{1,0:T(8,128)(2,1)}, bf16[192,3072]{1,0:T(8,128)(2,1)S(1)}, u32[]{:S(2)}, u32[]{:S(2)}) collective-permute-start(bf16[192,3072]{1,0:T(8,128)(2,1)} %get-tuple-element.70), channel_id=1, source_target_pairs={{0,8},{1,9},{2,10},{3,11},{4,12},{5,13},{6,14},{7,15},{8,0},{9,1},... | collective-permute-start | bytes 3538952 | tf_op jit(solution)/shard_map/left2/ppermute | solution.py:175
  36.5 28.5 %copy-start.3 = (bf16[4,192,896]{2,1,0:T(8,128)(2,1)}, bf16[4,192,896]{2,1,0:T(8,128)(2,1)S(1)}, u32[]{:S(2)}) copy-start(bf16[4,192,896]{2,1,0:T(8,128)(2,1)S(1)} %pad_maximum_fusion.rest_4_) | copy-start | bytes 4128772
  36.6 28.0 %collective-permute-start.6 = (bf16[4,192,896]{2,1,0:T(8,128)(2,1)S(1)}, bf16[4,192,896]{2,1,0:T(8,128)(2,1)S(1)}, u32[]{:S(2)}, u32[]{:S(2)}) collective-permute-start(bf16[4,192,896]{2,1,0:T(8,128)(2,1)S(1)} %pad_maximum_fusion.rest_4_), channel_id=1, source_target_pairs={{0,3},{1,0},{2,1},{3,2},{4,7},{5,4},{6,5},{7,6},{8,11},{9,8},{10,9... | collective-permute-start | bytes 4128776 | tf_op jit(solution)/shard_map/down0/ppermute | solution.py:175
  39.7 25.3 %collective-permute-start.5 = (bf16[4,192,896]{2,1,0:T(8,128)(2,1)S(1)}, bf16[4,192,896]{2,1,0:T(8,128)(2,1)}, u32[]{:S(2)}, u32[]{:S(2)}) collective-permute-start(bf16[4,192,896]{2,1,0:T(8,128)(2,1)S(1)} %pad_maximum_fusion.rest_4_), channel_id=1, source_target_pairs={{0,1},{1,2},{2,3},{3,0},{4,5},{5,6},{6,7},{7,4},{8,9},{9,10},{10,1... | collective-permute-start | bytes 4128776 | tf_op jit(solution)/shard_map/up0/ppermute | solution.py:175
  39.9 24.7 %collective-permute-start.7 = (bf16[4,192,128]{2,1,0:T(8,128)(2,1)S(1)}, bf16[4,192,128]{2,1,0:T(8,128)(2,1)S(1)}, u32[]{:S(2)}, u32[]{:S(2)}) collective-permute-start(bf16[4,192,128]{2,1,0:T(8,128)(2,1)S(1)} %pad_maximum_fusion.6), channel_id=1, source_target_pairs={{0,2},{1,3},{2,0},{3,1},{4,6},{5,7},{6,4},{7,5},{8,10},{9,11},{10,... | collective-permute-start | bytes 589832 | tf_op jit(solution)/shard_map/shade/ppermute | solution.py:175
  64.6 1.9 %copy-start.12 = (bf16[4,192,128]{2,1,0:T(8,128)(2,1)}, bf16[4,192,128]{2,1,0:T(8,128)(2,1)S(1)}, u32[]{:S(2)}) copy-start(bf16[4,192,128]{2,1,0:T(8,128)(2,1)S(1)} %collective-permute-done.7.rest_7_) | copy-start | bytes 589828
  64.6 1.9 %copy-start.7 = (bf16[192,3072]{1,0:T(8,128)(2,1)}, bf16[192,3072]{1,0:T(8,128)(2,1)S(1)}, u32[]{:S(2)}) copy-start(bf16[192,3072]{1,0:T(8,128)(2,1)S(1)} %collective-permute-done.8.rest_2_) | copy-start | bytes 3538948
  64.6 1.9 %copy-start.6 = (bf16[4,192,896]{2,1,0:T(8,128)(2,1)}, bf16[4,192,896]{2,1,0:T(8,128)(2,1)S(1)}, u32[]{:S(2)}) copy-start(bf16[4,192,896]{2,1,0:T(8,128)(2,1)S(1)} %collective-permute-done.6.rest_6_) | copy-start | bytes 4128772
  65.1 19.7 %collective-permute-start.9 = (bf16[4,192,896]{2,1,0:T(8,128)(2,1)}, bf16[4,192,896]{2,1,0:T(8,128)(2,1)S(1)}, u32[]{:S(2)}, u32[]{:S(2)}) collective-permute-start(bf16[4,192,896]{2,1,0:T(8,128)(2,1)} %collective-permute-done.5.rest_5_), channel_id=1, source_target_pairs={{0,1},{1,2},{2,3},{3,0},{4,5},{5,6},{6,7},{7,4},{8,9},{9,10},{10,1... | collective-permute-start | bytes 4128776 | tf_op jit(solution)/shard_map/forward0/ppermute | solution.py:175
  66.5 17.6 %collective-permute-start.10 = (bf16[4,192,768]{2,1,0:T(8,128)(2,1)}, bf16[4,192,768]{2,1,0:T(8,128)(2,1)S(1)}, u32[]{:S(2)}, u32[]{:S(2)}) collective-permute-start(bf16[4,192,768]{2,1,0:T(8,128)(2,1)} %pad_maximum_fusion.1.rest_4_), channel_id=1, source_target_pairs={{0,3},{1,0},{2,1},{3,2},{4,7},{5,4},{6,5},{7,6},{8,11},{9,8},{10,9... | collective-permute-start | bytes 3538952 | tf_op jit(solution)/shard_map/down1/ppermute | solution.py:175
  78.4 5.0 %collective-permute-start.11 = (f32[64,64]{1,0:T(8,128)}, f32[64,64]{1,0:T(8,128)S(1)}, u32[]{:S(2)}, u32[]{:S(2)}) collective-permute-start(f32[64,64]{1,0:T(8,128)} %shard_map.59), channel_id=1, source_target_pairs={{0,1},{1,0},{2,3},{3,2},{4,5},{5,4},{6,7},{7,6},{8,9},{9,8},{10,11... | collective-permute-start | bytes 49160 | tf_op jit(solution)/shard_map/corner1/ppermute | solution.py:175
  84.1 20.0 %copy-start.15 = (bf16[4,192,768]{2,1,0:T(8,128)(2,1)}, bf16[4,192,768]{2,1,0:T(8,128)(2,1)S(1)}, u32[]{:S(2)}) copy-start(bf16[4,192,768]{2,1,0:T(8,128)(2,1)S(1)} %collective-permute-done.10.rest_6_) | copy-start | bytes 3538948
  84.8 9.7 %copy-start.14 = (bf16[4,192,896]{2,1,0:T(8,128)(2,1)}, bf16[4,192,896]{2,1,0:T(8,128)(2,1)S(1)}, u32[]{:S(2)}) copy-start(bf16[4,192,896]{2,1,0:T(8,128)(2,1)S(1)} %collective-permute-done.9.rest_7_) | copy-start | bytes 4128772
  84.8 24.6 %collective-permute-start.12 = (bf16[4,192,768]{2,1,0:T(8,128)(2,1)}, bf16[4,192,768]{2,1,0:T(8,128)(2,1)}, u32[]{:S(2)}, u32[]{:S(2)}) collective-permute-start(bf16[4,192,768]{2,1,0:T(8,128)(2,1)} %pad_maximum_fusion.1.rest_4_), channel_id=1, source_target_pairs={{0,1},{1,2},{2,3},{3,0},{4,5},{5,6},{6,7},{7,4},{8,9},{9,10},{10,1... | collective-permute-start | bytes 3538952 | tf_op jit(solution)/shard_map/up1/ppermute | solution.py:175
  85.4 24.0 %collective-permute-start.13 = (bf16[4,192,768]{2,1,0:T(8,128)(2,1)S(1)}, bf16[4,192,768]{2,1,0:T(8,128)(2,1)}, u32[]{:S(2)}, u32[]{:S(2)}) collective-permute-start(bf16[4,192,768]{2,1,0:T(8,128)(2,1)S(1)} %collective-permute-done.10.rest_6_), channel_id=1, source_target_pairs={{0,3},{1,0},{2,1},{3,2},{4,7},{5,4},{6,5},{7,6},{8,11},{9,8},{10,9... | collective-permute-start | bytes 3538952 | tf_op jit(solution)/shard_map/forward1/ppermute | solution.py:175
  88.0 16.1 %collective-permute-start.16 = (f32[64,64]{1,0:T(8,128)S(1)}, f32[64,64]{1,0:T(8,128)S(1)}, u32[]{:S(2)}, u32[]{:S(2)}) collective-permute-start(f32[64,64]{1,0:T(8,128)S(1)} %add.307), channel_id=1, source_target_pairs={{0,10},{1,11},{2,8},{3,9},{4,14},{5,15},{6,12},{7,13},{8,2},{9,3},... | collective-permute-start | bytes 49160 | tf_op jit(solution)/shard_map/around/ppermute | solution.py:175
  93.0 14.2 %collective-permute-start.15 = (f32[64,64]{1,0:T(8,128)S(1)}, f32[64,64]{1,0:T(8,128)S(1)}, u32[]{:S(2)}, u32[]{:S(2)}) collective-permute-start(f32[64,64]{1,0:T(8,128)S(1)} %add.307), channel_id=1, source_target_pairs={{0,8},{1,9},{2,10},{3,11},{4,12},{5,13},{6,14},{7,15},{8,0},{9,1},... | collective-permute-start | bytes 49160 | tf_op jit(solution)/shard_map/around/ppermute | solution.py:175
  93.6 13.7 %collective-permute-start.14 = (f32[64,64]{1,0:T(8,128)S(1)}, f32[64,64]{1,0:T(8,128)S(1)}, u32[]{:S(2)}, u32[]{:S(2)}) collective-permute-start(f32[64,64]{1,0:T(8,128)S(1)} %add.307), channel_id=1, source_target_pairs={{0,2},{1,3},{2,0},{3,1},{4,6},{5,7},{6,4},{7,5},{8,10},{9,11},{10,... | collective-permute-start | bytes 49160 | tf_op jit(solution)/shard_map/around/ppermute | solution.py:175
  104.2 16.4 %collective-permute-start.19 = (f32[192,768]{1,0:T(8,128)}, f32[192,768]{1,0:T(8,128)S(1)}, u32[]{:S(2)}, u32[]{:S(2)}) collective-permute-start(f32[192,768]{1,0:T(8,128)} %get-tuple-element.57), channel_id=1, source_target_pairs={{0,8},{1,9},{2,10},{3,11},{4,12},{5,13},{6,14},{7,15},{8,0},{9,1},... | collective-permute-start | bytes 1769480 | tf_op jit(solution)/shard_map/back02/ppermute | solution.py:175
  107.3 15.0 %collective-permute-start.18 = (f32[192,768]{1,0:T(8,128)}, f32[192,768]{1,0:T(8,128)S(1)}, u32[]{:S(2)}, u32[]{:S(2)}) collective-permute-start(f32[192,768]{1,0:T(8,128)} %get-tuple-element.56), channel_id=1, source_target_pairs={{0,4},{1,5},{2,6},{3,7},{4,0},{5,1},{6,2},{7,3},{8,12},{9,13},{10,... | collective-permute-start | bytes 1769480 | tf_op jit(solution)/shard_map/back01/ppermute | solution.py:175
  107.9 14.4 %collective-permute-start.20 = (f32[192,768]{1,0:T(8,128)}, f32[192,768]{1,0:T(8,128)S(1)}, u32[]{:S(2)}, u32[]{:S(2)}) collective-permute-start(f32[192,768]{1,0:T(8,128)} %get-tuple-element.58), channel_id=1, source_target_pairs={{0,12},{1,13},{2,14},{3,15},{4,8},{5,9},{6,10},{7,11},{8,4},{9,5},... | collective-permute-start | bytes 1769480 | tf_op jit(solution)/shard_map/back03/ppermute | solution.py:175
  108.8 0.7 copy-start.8
  108.8 1.3 copy-start.10
  110.1 24.6 %copy-start = (f32[192,768]{1,0:T(8,128)S(1)}, f32[192,768]{1,0:T(8,128)}, u32[]{:S(2)}) copy-start(f32[192,768]{1,0:T(8,128)} %get-tuple-element.65.rest_0_) | copy-start | bytes 1769476
  110.1 15.0 %collective-permute-start.17 = (f32[8,128]{1,0:T(8,128)S(1)}, f32[8,128]{1,0:T(8,128)S(1)}, u32[]{:S(2)}, u32[]{:S(2)}) collective-permute-start(f32[8,128]{1,0:T(8,128)S(1)} %broadcast_in_dim.2), channel_id=1, source_target_pairs={{0,16},{1,17},{2,18},{3,19},{4,20},{5,21},{6,22},{7,23},{8,24},{9,... | collective-permute-start | bytes 12296 | tf_op jit(solution)/shard_map/total1/ppermute | solution.py:175
  122.3 16.2 %collective-permute-start.23 = (f32[192,768]{1,0:T(8,128)}, f32[192,768]{1,0:T(8,128)S(1)}, u32[]{:S(2)}, u32[]{:S(2)}) collective-permute-start(f32[192,768]{1,0:T(8,128)} %get-tuple-element.64), channel_id=1, source_target_pairs={{0,12},{1,13},{2,14},{3,15},{4,8},{5,9},{6,10},{7,11},{8,4},{9,5},... | collective-permute-start | bytes 1769480 | tf_op jit(solution)/shard_map/back13/ppermute | solution.py:175
  124.9 13.6 %collective-permute-start.21 = (f32[192,768]{1,0:T(8,128)}, f32[192,768]{1,0:T(8,128)S(1)}, u32[]{:S(2)}, u32[]{:S(2)}) collective-permute-start(f32[192,768]{1,0:T(8,128)} %get-tuple-element.59), channel_id=1, source_target_pairs={{0,4},{1,5},{2,6},{3,7},{4,0},{5,1},{6,2},{7,3},{8,12},{9,13},{10,... | collective-permute-start | bytes 1769480 | tf_op jit(solution)/shard_map/back11/ppermute | solution.py:175
  125.1 16.3 %collective-permute-start.22 = (f32[192,768]{1,0:T(8,128)}, f32[192,768]{1,0:T(8,128)}, u32[]{:S(2)}, u32[]{:S(2)}) collective-permute-start(f32[192,768]{1,0:T(8,128)} %get-tuple-element.62), channel_id=1, source_target_pairs={{0,8},{1,9},{2,10},{3,11},{4,12},{5,13},{6,14},{7,15},{8,0},{9,1},... | collective-permute-start | bytes 1769480 | tf_op jit(solution)/shard_map/back12/ppermute | solution.py:175
  127.0 3.6 %collective-permute-start.24 = (f32[8,128]{1,0:T(8,128)S(1)}, f32[8,128]{1,0:T(8,128)S(1)}, u32[]{:S(2)}, u32[]{:S(2)}) collective-permute-start(f32[8,128]{1,0:T(8,128)S(1)} %add.310), channel_id=1, source_target_pairs={{0,32},{1,33},{2,34},{3,35},{4,36},{5,37},{6,38},{7,39},{8,40},{9,... | collective-permute-start | bytes 12296 | tf_op jit(solution)/shard_map/total2/ppermute | solution.py:175
  130.6 6.1 %collective-permute-start.25 = (f32[8,128]{1,0:T(8,128)S(1)}, f32[8,128]{1,0:T(8,128)S(1)}, u32[]{:S(2)}, u32[]{:S(2)}) collective-permute-start(f32[8,128]{1,0:T(8,128)S(1)} %add.311), channel_id=1, source_target_pairs={{0,64},{1,65},{2,66},{3,67},{4,68},{5,69},{6,70},{7,71},{8,72},{9,... | collective-permute-start | bytes 12296 | tf_op jit(solution)/shard_map/total4/ppermute | solution.py:175
  134.7 3.2 %copy-start.9 = (f32[1,64,64]{2,1,0:T(8,128)S(1)}, f32[1,64,64]{2,1,0:T(8,128)}, u32[]{:S(2)}) copy-start(f32[1,64,64]{2,1,0:T(8,128)} %copy-done.8) | copy-start | bytes 49156
  134.7 3.2 %copy-start.11 = (f32[1,64,64]{2,1,0:T(8,128)S(1)}, f32[1,64,64]{2,1,0:T(8,128)}, u32[]{:S(2)}) copy-start(f32[1,64,64]{2,1,0:T(8,128)} %copy-done.10) | copy-start | bytes 49156
  134.7 6.8 %copy-start.1 = (f32[192,768]{1,0:T(8,128)S(1)}, f32[192,768]{1,0:T(8,128)}, u32[]{:S(2)}) copy-start(f32[192,768]{1,0:T(8,128)} %get-tuple-element.54.rest_0_) | copy-start | bytes 1769476

commit v6 on v5

--- a/solution.py
+++ b/solution.py
@@ -257,7 +257,7 @@
         total = total + send(total, across[1], "total1")
         out1 = product(offsets, left, (own1, below1, above1, beyond1), (0,) * 4, width)
         first, total = lax.optimization_barrier((out1[0], total))
-        out1 = [first, after(out1[1], *out0[1:]), after(out1[2], out0[2], total), after(out1[3], *out0[1:])]
+        out1 = [first, after(out1[1], *out0[1:]), after(out1[2], out0[2]), after(out1[3], *out0[1:])]
         out1 = back(1, out1)
         enlarged = put(1, out1, put(0, out0, None))
         for p in (2, 4):

time: 145 us -> 145 us (level)
  local copies, waits for them, and re-layouts: 9.77 us -> 12.5 us
  waiting for transfers between devices: 50.6 us -> 49 us
  starting transfers between devices: 43.3 us -> 41.7 us
    unnamed x32 -> x42, local copies, waits for them, and re-layouts: 0.07 us -> 2.74 us
    ppermute x26, starting transfers between devices: 43.3 us -> 41.7 us  [send(): return lax.ppermute(value, ('row', 'col'), table)]
    ppermute x26, waiting for transfers between devices: 50.6 us -> 49 us  [send(): return lax.ppermute(value, ('row', 'col'), table)]
where the time goes in v6:
time: 145 us
  waiting for transfers between devices  49 us (34%)
  starting transfers between devices  41.7 us (29%)
  Pallas kernels  30.1 us (21%)
  local copies, waits for them, and re-layouts  12.5 us (9%)
  other arithmetic  7.99 us (6%)
  between operations  1.98 us (1%)
  matrix products  1.58 us (1%)
    ppermute x26, waiting for transfers between devices, send(): return lax.ppermute(value, ('row', 'col'), table)  49 us
    ppermute x26, starting transfers between devices, send(): return lax.ppermute(value, ('row', 'col'), table)  41.7 us
    pallas_call x2, Pallas kernels, product(): pl.pallas_call(kernel, in_specs=[pl.BlockSpec(memory_space=pltpu.SMEM)] +...  19.3 us
    pallas_call x1, Pallas kernels, share(): pl.pallas_call(kernel, in_specs=[pl.BlockSpec(memory_space=pltpu.SMEM), i...  6.3 us
    pallas_call x2, Pallas kernels, place(): pl.pallas_call(kernel, in_specs=[pl.BlockSpec(memory_space=pltpu.SMEM)] +...  4.49 us
    squeeze x1, local copies, waits for them, and re-layouts, body(): other = lax.dynamic_index_in_dim(left_edge, 1 - sector, 0, keepdims=False)  2.95 us
  transfers between devices with their start and end apart: 26, of which 9 were waited for; matrix products, arithmetic and copies ran while one was open for 11% of the time, Pallas kernels for 19%

profile of v6, /device:TPU:0, one launch (start us, length us, event | category | flops | bytes accessed | tf_op | source)
XLA Modules:
  0.0 144.7 jit_solution(17227685531797794370)
XLA Ops:
  0.7 3.0 %dynamic-slice_bitcast_fusion = (bf16[192,3072]{1,0:T(8,128)(2,1)}, bf16[192,3072]{1,0:T(8,128)(2,1)S(1)}) fusion(bf16[2,192,3072]{2,1,0:T(8,128)(2,1)} %param.4, s32[]{:T(128)S(6)} %select_n.241, s32[]{:T(128)S(6)} %select_n.240), kind=kLoop, calls=%fused_computation.2 | loop fusion | bytes 4718600 | tf_op jit(solution)/shard_map/jit(dynamic_index_in_dim)/squeeze | solution.py:198
  3.7 2.8 %collective-permute-start.4 = (bf16[192,3072]{1,0:T(8,128)(2,1)}, bf16[192,3072]{1,0:T(8,128)(2,1)}, u32[]{:S(2)}, u32[]{:S(2)}) collective-permute-start(bf16[192,3072]{1,0:T(8,128)(2,1)} %get-tuple-element.70), channel_id=1, source_target_pairs={{0,12},{1,13},{2,14},{3,15},{4,8},{5,9},{6,10},{7,11},{8,4},{9,5},... | collective-permute-start | bytes 3538952 | tf_op jit(solution)/shard_map/left3/ppermute | solution.py:175
  6.5 0.2 collective-permute-start
  6.7 0.1 compare_convert_fusion
  6.8 1.2 broadcast_multiply_fusion
  8.0 1.6 %fusion.9 = (f32[2,192,64]{1,2,0:T(8,128)}, f32[2,192,64]{1,2,0:T(8,128)}) fusion(bf16[2,192,3072]{2,1,0:T(8,128)(2,1)S(1)} %copy-done.2, bf16[2,3072,64]{1,2,0:T(8,128)(2,1)S(1)} %broadcast_multiply_fusion), kind=kOutput, calls=%fused_computation.52 | convolution fusion | flops 151019520 | bytes 3342336 | tf_op jit(solution)/shard_map/skj,sjq->skq/dot_general | solution.py:201
  9.6 1.7 %copy.9 = f32[2,192,64]{2,1,0:T(8,128)} copy(f32[2,192,64]{1,2,0:T(8,128)} %get-tuple-element.82) | data formatting | bytes 196608 | tf_op jit(solution)/shard_map/reduce_precision | solution.py:202
  11.3 1.7 %copy.10 = f32[2,192,64]{2,1,0:T(8,128)} copy(f32[2,192,64]{1,2,0:T(8,128)} %get-tuple-element.83) | data formatting | bytes 196608 | tf_op jit(solution)/shard_map/skj,sjq->skq/dot_general | solution.py:201
  13.0 1.1 subtract_convert_fusion
  14.2 0.1 fusion.3
  14.3 0.2 dynamic-slice_bitcast_fusion.5
  14.5 0.1 pad_maximum_fusion.2
  14.6 1.9 %collective-permute-start.1 = (bf16[192,1664]{1,0:T(8,128)(2,1)S(1)}, bf16[192,1664]{1,0:T(8,128)(2,1)S(1)}, u32[]{:S(2)}, u32[]{:S(2)}) collective-permute-start(bf16[192,1664]{1,0:T(8,128)(2,1)S(1)} %pad_maximum_fusion.2), channel_id=1, source_target_pairs={{0,4},{1,5},{2,6},{3,7},{4,0},{5,1},{6,2},{7,3},{8,12},{9,13},{10,... | collective-permute-start | bytes 1916936 | tf_op jit(solution)/shard_map/right1/ppermute | solution.py:175
  16.5 0.9 collective-permute-start.2
  17.5 2.2 %collective-permute-start.3 = (bf16[192,1664]{1,0:T(8,128)(2,1)S(1)}, bf16[192,1664]{1,0:T(8,128)(2,1)S(1)}, u32[]{:S(2)}, u32[]{:S(2)}) collective-permute-start(bf16[192,1664]{1,0:T(8,128)(2,1)S(1)} %pad_maximum_fusion.4), channel_id=1, source_target_pairs={{0,12},{1,13},{2,14},{3,15},{4,8},{5,9},{6,10},{7,11},{8,4},{9,5},... | collective-permute-start | bytes 1916936 | tf_op jit(solution)/shard_map/right3/ppermute | solution.py:175
  19.7 9.9 %collective-permute-done.1 = bf16[192,1664]{1,0:T(8,128)(2,1)S(1)} collective-permute-done((bf16[192,1664]{1,0:T(8,128)(2,1)S(1)}, bf16[192,1664]{1,0:T(8,128)(2,1)S(1)}, u32[]{:S(2)}, u32[]{:S(2)}) %collective-permute-start.1) | collective-permute-done | bytes 639008 | tf_op jit(solution)/shard_map/right1/ppermute | solution.py:175
  29.6 0.8 collective-permute-start.8
  30.4 5.8 %collective-permute-done.2 = bf16[192,1664]{1,0:T(8,128)(2,1)S(1)} collective-permute-done((bf16[192,1664]{1,0:T(8,128)(2,1)S(1)}, bf16[192,1664]{1,0:T(8,128)(2,1)S(1)}, u32[]{:S(2)}, u32[]{:S(2)}) %collective-permute-start.2) | collective-permute-done | bytes 639008 | tf_op jit(solution)/shard_map/right2/ppermute | solution.py:175
  36.3 0.2 pad_maximum_fusion.rest_4_
  36.6 3.2 %collective-permute-start.6 = (bf16[4,192,896]{2,1,0:T(8,128)(2,1)S(1)}, bf16[4,192,896]{2,1,0:T(8,128)(2,1)S(1)}, u32[]{:S(2)}, u32[]{:S(2)}) collective-permute-start(bf16[4,192,896]{2,1,0:T(8,128)(2,1)S(1)} %pad_maximum_fusion.rest_4_), channel_id=1, source_target_pairs={{0,3},{1,0},{2,1},{3,2},{4,7},{5,4},{6,5},{7,6},{8,11},{9,8},{10,9... | collective-permute-start | bytes 4128776 | tf_op jit(solution)/shard_map/down0/ppermute | solution.py:175
  39.8 2.3 %collective-permute-start.7 = (bf16[4,192,128]{2,1,0:T(8,128)(2,1)S(1)}, bf16[4,192,128]{2,1,0:T(8,128)(2,1)S(1)}, u32[]{:S(2)}, u32[]{:S(2)}) collective-permute-start(bf16[4,192,128]{2,1,0:T(8,128)(2,1)S(1)} %pad_maximum_fusion.6), channel_id=1, source_target_pairs={{0,2},{1,3},{2,0},{3,1},{4,6},{5,7},{6,4},{7,5},{8,10},{9,11},{10,... | collective-permute-start | bytes 589832 | tf_op jit(solution)/shard_map/shade/ppermute | solution.py:175
  42.2 22.4 %collective-permute-done.7.rest_7_ = bf16[4,192,128]{2,1,0:T(8,128)(2,1)S(1)} collective-permute-done((bf16[4,192,128]{2,1,0:T(8,128)(2,1)S(1)}, bf16[4,192,128]{2,1,0:T(8,128)(2,1)S(1)}, u32[]{:S(2)}, u32[]{:S(2)}) %collective-permute-start.7) | collective-permute-done | bytes 196640 | tf_op jit(solution)/shard_map/shade/ppermute | solution.py:175
  64.6 0.5 collective-permute-done.5.rest_5_
  65.1 1.5 %pad_maximum_fusion.1.rest_4_ = bf16[4,192,768]{2,1,0:T(8,128)(2,1)} fusion(bf16[1,192,768]{2,1,0:T(8,128)(2,1)S(1)} %slice_bitcast_fusion.3, bf16[1,192,768]{2,1,0:T(8,128)(2,1)S(1)} %slice_bitcast_fusion.4, bf16[1,192,768]{2,1,0:T(8,128)(2,1)S(1)} %slice_bitcast_fusion.5, bf16[1,192,768]{2,1,0:T(8,128)(2,1)S(1)} %slice_bitcast_fusion.6), kind=kLoop, calls=%fused_computation.1 | loop fusion | flops 1769472 | bytes 2359296 | tf_op jit(solution)/shard_map/stack | solution.py:221
  66.6 3.2 %collective-permute-start.10 = (bf16[4,192,768]{2,1,0:T(8,128)(2,1)}, bf16[4,192,768]{2,1,0:T(8,128)(2,1)}, u32[]{:S(2)}, u32[]{:S(2)}) collective-permute-start(bf16[4,192,768]{2,1,0:T(8,128)(2,1)} %pad_maximum_fusion.1.rest_4_), channel_id=1, source_target_pairs={{0,3},{1,0},{2,1},{3,2},{4,7},{5,4},{6,5},{7,6},{8,11},{9,8},{10,9... | collective-permute-start | bytes 3538952 | tf_op jit(solution)/shard_map/down1/ppermute | solution.py:175
  69.7 0.6 stack.194.off
  70.4 1.0 dynamic-slice_bitcast_fusion.9
  71.4 0.7 pad_maximum_fusion.7.pick
  72.1 6.3 %shard_map.59 = f32[64,64]{1,0:T(8,128)} custom-call(s32[16]{0:T(128)} %stack.194.off, bf16[4,64,192]{2,1,0:T(8,128)(2,1)} %pad_maximum_fusion.7.pick, bf16[192,3072]{1,0:T(8,128)(2,1)} %copy-done.4, bf16[192,3072]{1,0:T(8,128)(2,1)} %collective-permute-done.rest_1_, bf16[192,3072]{1,0:T(8,128)(2,1)} %copy-done.7, ...), custom_call_target="tpu_custom_call" | custom-call | flops 603979776 | bytes 5505024 | tf_op jit(solution)/shard_map/pallas_call | solution.py:100
  78.4 0.1 collective-permute-start.11
  78.5 4.9 %collective-permute-done.11 = f32[64,64]{1,0:T(8,128)S(1)} collective-permute-done((f32[64,64]{1,0:T(8,128)}, f32[64,64]{1,0:T(8,128)S(1)}, u32[]{:S(2)}, u32[]{:S(2)}) %collective-permute-start.11) | collective-permute-done | bytes 16416 | tf_op jit(solution)/shard_map/corner1/ppermute | solution.py:175
  83.4 0.8 add.307
  84.2 0.6 collective-permute-done.9.rest_7_
  84.8 0.6 collective-permute-start.12
  85.4 2.6 %collective-permute-start.13 = (bf16[4,192,768]{2,1,0:T(8,128)(2,1)}, bf16[4,192,768]{2,1,0:T(8,128)(2,1)S(1)}, u32[]{:S(2)}, u32[]{:S(2)}) collective-permute-start(bf16[4,192,768]{2,1,0:T(8,128)(2,1)} %collective-permute-done.10.rest_6_), channel_id=1, source_target_pairs={{0,3},{1,0},{2,1},{3,2},{4,7},{5,4},{6,5},{7,6},{8,11},{9,8},{10,9... | collective-permute-start | bytes 3538952 | tf_op jit(solution)/shard_map/forward1/ppermute | solution.py:175
  88.0 5.0 %collective-permute-start.16 = (f32[64,64]{1,0:T(8,128)S(1)}, f32[64,64]{1,0:T(8,128)S(1)}, u32[]{:S(2)}, u32[]{:S(2)}) collective-permute-start(f32[64,64]{1,0:T(8,128)S(1)} %add.307), channel_id=1, source_target_pairs={{0,10},{1,11},{2,8},{3,9},{4,14},{5,15},{6,12},{7,13},{8,2},{9,3},... | collective-permute-start | bytes 49160 | tf_op jit(solution)/shard_map/around/ppermute | solution.py:175
  93.0 0.6 collective-permute-start.15
  93.6 0.9 collective-permute-start.14
  94.5 9.7 %shard_map.61 = (f32[192,768]{1,0:T(8,128)}, f32[192,768]{1,0:T(8,128)}, f32[192,768]{1,0:T(8,128)}, f32[192,768]{1,0:T(8,128)}) custom-call(s32[16]{0:T(128)} %stack.194.off, bf16[192,3072]{1,0:T(8,128)(2,1)} %copy-done.4, bf16[192,3072]{1,0:T(8,128)(2,1)} %collective-permute-done.rest_1_, bf16[192,3072]{1,0:T(8,128)(2,1)} %copy-done.7, ...), custom_call_target="tpu_custom_call" | custom-call | flops 3623878656 | bytes 11796480 | tf_op jit(solution)/shard_map/pallas_call | solution.py:50
  104.3 3.1 %collective-permute-start.19 = (f32[192,768]{1,0:T(8,128)}, f32[192,768]{1,0:T(8,128)S(1)}, u32[]{:S(2)}, u32[]{:S(2)}) collective-permute-start(f32[192,768]{1,0:T(8,128)} %get-tuple-element.57), channel_id=1, source_target_pairs={{0,8},{1,9},{2,10},{3,11},{4,12},{5,13},{6,14},{7,15},{8,0},{9,1},... | collective-permute-start | bytes 1769480 | tf_op jit(solution)/shard_map/back02/ppermute | solution.py:175
  107.4 0.7 collective-permute-start.18
  108.1 0.7 collective-permute-start.20
  108.8 1.0 copy-done.19
  109.8 1.1 copy-done.20
  110.8 9.6 %shard_map.60 = (f32[192,768]{1,0:T(8,128)}, f32[192,768]{1,0:T(8,128)}, f32[192,768]{1,0:T(8,128)}, f32[192,768]{1,0:T(8,128)}) custom-call(s32[16]{0:T(128)} %stack.194.off, bf16[192,3072]{1,0:T(8,128)(2,1)} %copy-done.4, bf16[192,3072]{1,0:T(8,128)(2,1)} %collective-permute-done.rest_1_, bf16[192,3072]{1,0:T(8,128)(2,1)} %copy-done.7, ...), custom_call_target="tpu_custom_call" | custom-call | flops 3623878656 | bytes 11796480 | tf_op jit(solution)/shard_map/pallas_call | solution.py:50
  120.4 2.0 %collective-permute-done.18.rest_1_ = f32[192,768]{1,0:T(8,128)S(1)} collective-permute-done((f32[192,768]{1,0:T(8,128)}, f32[192,768]{1,0:T(8,128)S(1)}, u32[]{:S(2)}, u32[]{:S(2)}) %collective-permute-start.18) | collective-permute-done | bytes 589856 | tf_op jit(solution)/shard_map/back01/ppermute | solution.py:175
  122.4 2.6 %collective-permute-start.23 = (f32[192,768]{1,0:T(8,128)}, f32[192,768]{1,0:T(8,128)S(1)}, u32[]{:S(2)}, u32[]{:S(2)}) collective-permute-start(f32[192,768]{1,0:T(8,128)} %get-tuple-element.63), channel_id=1, source_target_pairs={{0,12},{1,13},{2,14},{3,15},{4,8},{5,9},{6,10},{7,11},{8,4},{9,5},... | collective-permute-start | bytes 1769480 | tf_op jit(solution)/shard_map/back13/ppermute | solution.py:175
  125.0 0.9 collective-permute-start.22
  125.9 0.6 collective-permute-start.21
  126.5 0.8 add_bitcast_fusion
  127.3 0.6 copy-done.8
  127.9 0.6 multiply_reduce_fusion
  128.5 0.6 broadcast_in_dim.2
  129.2 0.1 collective-permute-start.17
  129.3 1.2 collective-permute-done.17
  130.4 1.9 %collective-permute-start.24 = (f32[8,128]{1,0:T(8,128)S(1)}, f32[8,128]{1,0:T(8,128)S(1)}, u32[]{:S(2)}, u32[]{:S(2)}) collective-permute-start(f32[8,128]{1,0:T(8,128)S(1)} %add.310), channel_id=1, source_target_pairs={{0,32},{1,33},{2,34},{3,35},{4,36},{5,37},{6,38},{7,39},{8,40},{9,... | collective-permute-start | bytes 12296 | tf_op jit(solution)/shard_map/total2/ppermute | solution.py:175
  132.4 1.7 %collective-permute-done.24 = f32[8,128]{1,0:T(8,128)S(1)} collective-permute-done((f32[8,128]{1,0:T(8,128)S(1)}, f32[8,128]{1,0:T(8,128)S(1)}, u32[]{:S(2)}, u32[]{:S(2)}) %collective-permute-start.24) | collective-permute-done | bytes 4128 | tf_op jit(solution)/shard_map/total2/ppermute | solution.py:175
  134.1 3.9 %collective-permute-start.25 = (f32[8,128]{1,0:T(8,128)S(1)}, f32[8,128]{1,0:T(8,128)S(1)}, u32[]{:S(2)}, u32[]{:S(2)}) collective-permute-start(f32[8,128]{1,0:T(8,128)S(1)} %add.311), channel_id=1, source_target_pairs={{0,64},{1,65},{2,66},{3,67},{4,68},{5,69},{6,70},{7,71},{8,72},{9,... | collective-permute-start | bytes 12296 | tf_op jit(solution)/shard_map/total4/ppermute | solution.py:175
  137.9 0.1 stack.222.at
  138.0 0.1 stack.177.at
  138.1 2.0 %shard_map.62.rest_4_ = f32[2,192,3072]{2,1,0:T(8,128)} custom-call(s32[8]{0:T(128)S(1)} %stack.222.at, f32[192,768]{1,0:T(8,128)S(1)} %copy-done.1, f32[192,768]{1,0:T(8,128)S(1)} %collective-permute-done.18.rest_1_, f32[192,768]{1,0:T(8,128)S(1)} %collective-permute-done.19.rest_2_, f32[192,768]{1,0:T(8,128)S(1)} %collective-permute-done.20.rest_3_), custom_call_target="tpu_custom_call" | custom-call | tf_op jit(solution)/shard_map/pallas_call | solution.py:138
  140.1 0.6 slice.47
  141.4 0.6 fusion.8
  142.1 2.5 %shard_map.63 = f32[2,192,3072]{2,1,0:T(8,128)} custom-call(s32[8]{0:T(128)S(1)} %stack.177.at, f32[192,768]{1,0:T(8,128)S(1)} %copy-done, f32[192,768]{1,0:T(8,128)} %collective-permute-done.21.rest_1_, f32[192,768]{1,0:T(8,128)S(1)} %collective-permute-done.22.rest_2_, ...), custom_call_target="tpu_custom_call", output_to_operand_aliasing={{}: (5, {})} | custom-call | tf_op jit(solution)/shard_map/pallas_call | solution.py:138
  (75 shorter events, 0.5 us)
Async XLA Ops:
  0.7 6.0 %copy-start.17 = (s32[2]{0:T(128)S(1)}, s32[2]{0:T(128)}, u32[]{:S(2)}) copy-start(s32[2]{0:T(128)} %param.7) | copy-start | bytes 28
  0.7 7.3 %copy-start.2 = (bf16[2,192,3072]{2,1,0:T(8,128)(2,1)S(1)}, bf16[2,192,3072]{2,1,0:T(8,128)(2,1)}, u32[]{:S(2)}) copy-start(bf16[2,192,3072]{2,1,0:T(8,128)(2,1)} %param.5) | copy-start | bytes 7077892
  3.7 6.0 %copy-start.4 = (bf16[192,3072]{1,0:T(8,128)(2,1)}, bf16[192,3072]{1,0:T(8,128)(2,1)S(1)}, u32[]{:S(2)}) copy-start(bf16[192,3072]{1,0:T(8,128)(2,1)S(1)} %get-tuple-element.71.rest_0_) | copy-start | bytes 3538948
  3.7 32.9 %collective-permute-start.4 = (bf16[192,3072]{1,0:T(8,128)(2,1)}, bf16[192,3072]{1,0:T(8,128)(2,1)}, u32[]{:S(2)}, u32[]{:S(2)}) collective-permute-start(bf16[192,3072]{1,0:T(8,128)(2,1)} %get-tuple-element.70), channel_id=1, source_target_pairs={{0,12},{1,13},{2,14},{3,15},{4,8},{5,9},{6,10},{7,11},{8,4},{9,5},... | collective-permute-start | bytes 3538952 | tf_op jit(solution)/shard_map/left3/ppermute | solution.py:175
  6.5 30.0 %collective-permute-start = (bf16[192,3072]{1,0:T(8,128)(2,1)S(1)}, bf16[192,3072]{1,0:T(8,128)(2,1)}, u32[]{:S(2)}, u32[]{:S(2)}) collective-permute-start(bf16[192,3072]{1,0:T(8,128)(2,1)S(1)} %get-tuple-element.71.rest_0_), channel_id=1, source_target_pairs={{0,4},{1,5},{2,6},{3,7},{4,0},{5,1},{6,2},{7,3},{8,12},{9,13},{10,... | collective-permute-start | bytes 3538952 | tf_op jit(solution)/shard_map/left1/ppermute | solution.py:175
  8.0 1.6 %copy-start.5 = (bf16[2,3072,64]{1,2,0:T(8,128)(2,1)}, bf16[2,3072,64]{1,2,0:T(8,128)(2,1)S(1)}, u32[]{:S(2)}) copy-start(bf16[2,3072,64]{1,2,0:T(8,128)(2,1)S(1)} %broadcast_multiply_fusion) | copy-start | bytes 2359300
  14.6 15.0 %collective-permute-start.1 = (bf16[192,1664]{1,0:T(8,128)(2,1)S(1)}, bf16[192,1664]{1,0:T(8,128)(2,1)S(1)}, u32[]{:S(2)}, u32[]{:S(2)}) collective-permute-start(bf16[192,1664]{1,0:T(8,128)(2,1)S(1)} %pad_maximum_fusion.2), channel_id=1, source_target_pairs={{0,4},{1,5},{2,6},{3,7},{4,0},{5,1},{6,2},{7,3},{8,12},{9,13},{10,... | collective-permute-start | bytes 1916936 | tf_op jit(solution)/shard_map/right1/ppermute | solution.py:175
  16.5 19.7 %collective-permute-start.2 = (bf16[192,1664]{1,0:T(8,128)(2,1)S(1)}, bf16[192,1664]{1,0:T(8,128)(2,1)S(1)}, u32[]{:S(2)}, u32[]{:S(2)}) collective-permute-start(bf16[192,1664]{1,0:T(8,128)(2,1)S(1)} %pad_maximum_fusion.3), channel_id=1, source_target_pairs={{0,8},{1,9},{2,10},{3,11},{4,12},{5,13},{6,14},{7,15},{8,0},{9,1},... | collective-permute-start | bytes 1916936 | tf_op jit(solution)/shard_map/right2/ppermute | solution.py:175
  17.5 18.8 %collective-permute-start.3 = (bf16[192,1664]{1,0:T(8,128)(2,1)S(1)}, bf16[192,1664]{1,0:T(8,128)(2,1)S(1)}, u32[]{:S(2)}, u32[]{:S(2)}) collective-permute-start(bf16[192,1664]{1,0:T(8,128)(2,1)S(1)} %pad_maximum_fusion.4), channel_id=1, source_target_pairs={{0,12},{1,13},{2,14},{3,15},{4,8},{5,9},{6,10},{7,11},{8,4},{9,5},... | collective-permute-start | bytes 1916936 | tf_op jit(solution)/shard_map/right3/ppermute | solution.py:175
  29.6 35.0 %collective-permute-start.8 = (bf16[192,3072]{1,0:T(8,128)(2,1)}, bf16[192,3072]{1,0:T(8,128)(2,1)S(1)}, u32[]{:S(2)}, u32[]{:S(2)}) collective-permute-start(bf16[192,3072]{1,0:T(8,128)(2,1)} %get-tuple-element.70), channel_id=1, source_target_pairs={{0,8},{1,9},{2,10},{3,11},{4,12},{5,13},{6,14},{7,15},{8,0},{9,1},... | collective-permute-start | bytes 3538952 | tf_op jit(solution)/shard_map/left2/ppermute | solution.py:175
  36.5 28.5 %copy-start.3 = (bf16[4,192,896]{2,1,0:T(8,128)(2,1)}, bf16[4,192,896]{2,1,0:T(8,128)(2,1)S(1)}, u32[]{:S(2)}) copy-start(bf16[4,192,896]{2,1,0:T(8,128)(2,1)S(1)} %pad_maximum_fusion.rest_4_) | copy-start | bytes 4128772
  36.6 28.0 %collective-permute-start.6 = (bf16[4,192,896]{2,1,0:T(8,128)(2,1)S(1)}, bf16[4,192,896]{2,1,0:T(8,128)(2,1)S(1)}, u32[]{:S(2)}, u32[]{:S(2)}) collective-permute-start(bf16[4,192,896]{2,1,0:T(8,128)(2,1)S(1)} %pad_maximum_fusion.rest_4_), channel_id=1, source_target_pairs={{0,3},{1,0},{2,1},{3,2},{4,7},{5,4},{6,5},{7,6},{8,11},{9,8},{10,9... | collective-permute-start | bytes 4128776 | tf_op jit(solution)/shard_map/down0/ppermute | solution.py:175
  39.7 25.3 %collective-permute-start.5 = (bf16[4,192,896]{2,1,0:T(8,128)(2,1)S(1)}, bf16[4,192,896]{2,1,0:T(8,128)(2,1)}, u32[]{:S(2)}, u32[]{:S(2)}) collective-permute-start(bf16[4,192,896]{2,1,0:T(8,128)(2,1)S(1)} %pad_maximum_fusion.rest_4_), channel_id=1, source_target_pairs={{0,1},{1,2},{2,3},{3,0},{4,5},{5,6},{6,7},{7,4},{8,9},{9,10},{10,1... | collective-permute-start | bytes 4128776 | tf_op jit(solution)/shard_map/up0/ppermute | solution.py:175
  39.8 24.7 %collective-permute-start.7 = (bf16[4,192,128]{2,1,0:T(8,128)(2,1)S(1)}, bf16[4,192,128]{2,1,0:T(8,128)(2,1)S(1)}, u32[]{:S(2)}, u32[]{:S(2)}) collective-permute-start(bf16[4,192,128]{2,1,0:T(8,128)(2,1)S(1)} %pad_maximum_fusion.6), channel_id=1, source_target_pairs={{0,2},{1,3},{2,0},{3,1},{4,6},{5,7},{6,4},{7,5},{8,10},{9,11},{10,... | collective-permute-start | bytes 589832 | tf_op jit(solution)/shard_map/shade/ppermute | solution.py:175
  64.6 2.0 %copy-start.12 = (bf16[4,192,128]{2,1,0:T(8,128)(2,1)}, bf16[4,192,128]{2,1,0:T(8,128)(2,1)S(1)}, u32[]{:S(2)}) copy-start(bf16[4,192,128]{2,1,0:T(8,128)(2,1)S(1)} %collective-permute-done.7.rest_7_) | copy-start | bytes 589828
  64.6 2.0 %copy-start.7 = (bf16[192,3072]{1,0:T(8,128)(2,1)}, bf16[192,3072]{1,0:T(8,128)(2,1)S(1)}, u32[]{:S(2)}) copy-start(bf16[192,3072]{1,0:T(8,128)(2,1)S(1)} %collective-permute-done.8.rest_2_) | copy-start | bytes 3538948
  64.6 2.0 %copy-start.6 = (bf16[4,192,896]{2,1,0:T(8,128)(2,1)}, bf16[4,192,896]{2,1,0:T(8,128)(2,1)S(1)}, u32[]{:S(2)}) copy-start(bf16[4,192,896]{2,1,0:T(8,128)(2,1)S(1)} %collective-permute-done.6.rest_6_) | copy-start | bytes 4128772
  65.0 19.7 %collective-permute-start.9 = (bf16[4,192,896]{2,1,0:T(8,128)(2,1)}, bf16[4,192,896]{2,1,0:T(8,128)(2,1)S(1)}, u32[]{:S(2)}, u32[]{:S(2)}) collective-permute-start(bf16[4,192,896]{2,1,0:T(8,128)(2,1)} %collective-permute-done.5.rest_5_), channel_id=1, source_target_pairs={{0,1},{1,2},{2,3},{3,0},{4,5},{5,6},{6,7},{7,4},{8,9},{9,10},{10,1... | collective-permute-start | bytes 4128776 | tf_op jit(solution)/shard_map/forward0/ppermute | solution.py:175
  66.6 17.6 %collective-permute-start.10 = (bf16[4,192,768]{2,1,0:T(8,128)(2,1)}, bf16[4,192,768]{2,1,0:T(8,128)(2,1)}, u32[]{:S(2)}, u32[]{:S(2)}) collective-permute-start(bf16[4,192,768]{2,1,0:T(8,128)(2,1)} %pad_maximum_fusion.1.rest_4_), channel_id=1, source_target_pairs={{0,3},{1,0},{2,1},{3,2},{4,7},{5,4},{6,5},{7,6},{8,11},{9,8},{10,9... | collective-permute-start | bytes 3538952 | tf_op jit(solution)/shard_map/down1/ppermute | solution.py:175
  78.4 5.0 %collective-permute-start.11 = (f32[64,64]{1,0:T(8,128)}, f32[64,64]{1,0:T(8,128)S(1)}, u32[]{:S(2)}, u32[]{:S(2)}) collective-permute-start(f32[64,64]{1,0:T(8,128)} %shard_map.59), channel_id=1, source_target_pairs={{0,1},{1,0},{2,3},{3,2},{4,5},{5,4},{6,7},{7,6},{8,9},{9,8},{10,11... | collective-permute-start | bytes 49160 | tf_op jit(solution)/shard_map/corner1/ppermute | solution.py:175
  84.2 20.1 %copy-start.13 = (f32[64,64]{1,0:T(8,128)}, f32[64,64]{1,0:T(8,128)S(1)}, u32[]{:S(2)}) copy-start(f32[64,64]{1,0:T(8,128)S(1)} %add.307) | copy-start | bytes 49156
  84.8 9.7 %copy-start.18 = (bf16[4,192,896]{2,1,0:T(8,128)(2,1)}, bf16[4,192,896]{2,1,0:T(8,128)(2,1)S(1)}, u32[]{:S(2)}) copy-start(bf16[4,192,896]{2,1,0:T(8,128)(2,1)S(1)} %collective-permute-done.9.rest_7_) | copy-start | bytes 4128772
  84.8 24.0 %collective-permute-start.12 = (bf16[4,192,768]{2,1,0:T(8,128)(2,1)}, bf16[4,192,768]{2,1,0:T(8,128)(2,1)S(1)}, u32[]{:S(2)}, u32[]{:S(2)}) collective-permute-start(bf16[4,192,768]{2,1,0:T(8,128)(2,1)} %pad_maximum_fusion.1.rest_4_), channel_id=1, source_target_pairs={{0,1},{1,2},{2,3},{3,0},{4,5},{5,6},{6,7},{7,4},{8,9},{9,10},{10,1... | collective-permute-start | bytes 3538952 | tf_op jit(solution)/shard_map/up1/ppermute | solution.py:175
  85.4 23.3 %collective-permute-start.13 = (bf16[4,192,768]{2,1,0:T(8,128)(2,1)}, bf16[4,192,768]{2,1,0:T(8,128)(2,1)S(1)}, u32[]{:S(2)}, u32[]{:S(2)}) collective-permute-start(bf16[4,192,768]{2,1,0:T(8,128)(2,1)} %collective-permute-done.10.rest_6_), channel_id=1, source_target_pairs={{0,3},{1,0},{2,1},{3,2},{4,7},{5,4},{6,5},{7,6},{8,11},{9,8},{10,9... | collective-permute-start | bytes 3538952 | tf_op jit(solution)/shard_map/forward1/ppermute | solution.py:175
  88.0 16.2 %collective-permute-start.16 = (f32[64,64]{1,0:T(8,128)S(1)}, f32[64,64]{1,0:T(8,128)S(1)}, u32[]{:S(2)}, u32[]{:S(2)}) collective-permute-start(f32[64,64]{1,0:T(8,128)S(1)} %add.307), channel_id=1, source_target_pairs={{0,10},{1,11},{2,8},{3,9},{4,14},{5,15},{6,12},{7,13},{8,2},{9,3},... | collective-permute-start | bytes 49160 | tf_op jit(solution)/shard_map/around/ppermute | solution.py:175
  93.0 14.4 %collective-permute-start.15 = (f32[64,64]{1,0:T(8,128)S(1)}, f32[64,64]{1,0:T(8,128)S(1)}, u32[]{:S(2)}, u32[]{:S(2)}) collective-permute-start(f32[64,64]{1,0:T(8,128)S(1)} %add.307), channel_id=1, source_target_pairs={{0,8},{1,9},{2,10},{3,11},{4,12},{5,13},{6,14},{7,15},{8,0},{9,1},... | collective-permute-start | bytes 49160 | tf_op jit(solution)/shard_map/around/ppermute | solution.py:175
  93.6 13.8 %collective-permute-start.14 = (f32[64,64]{1,0:T(8,128)S(1)}, f32[64,64]{1,0:T(8,128)S(1)}, u32[]{:S(2)}, u32[]{:S(2)}) collective-permute-start(f32[64,64]{1,0:T(8,128)S(1)} %add.307), channel_id=1, source_target_pairs={{0,2},{1,3},{2,0},{3,1},{4,6},{5,7},{6,4},{7,5},{8,10},{9,11},{10,... | collective-permute-start | bytes 49160 | tf_op jit(solution)/shard_map/around/ppermute | solution.py:175
  104.3 16.1 %copy-start.14 = (f32[64,64]{1,0:T(8,128)}, f32[64,64]{1,0:T(8,128)S(1)}, u32[]{:S(2)}) copy-start(f32[64,64]{1,0:T(8,128)S(1)} %collective-permute-done.16) | copy-start | bytes 49156
  104.3 16.2 %collective-permute-start.19 = (f32[192,768]{1,0:T(8,128)}, f32[192,768]{1,0:T(8,128)S(1)}, u32[]{:S(2)}, u32[]{:S(2)}) collective-permute-start(f32[192,768]{1,0:T(8,128)} %get-tuple-element.57), channel_id=1, source_target_pairs={{0,8},{1,9},{2,10},{3,11},{4,12},{5,13},{6,14},{7,15},{8,0},{9,1},... | collective-permute-start | bytes 1769480 | tf_op jit(solution)/shard_map/back02/ppermute | solution.py:175
  107.4 13.0 %copy-start.15 = (f32[64,64]{1,0:T(8,128)}, f32[64,64]{1,0:T(8,128)S(1)}, u32[]{:S(2)}) copy-start(f32[64,64]{1,0:T(8,128)S(1)} %collective-permute-done.15) | copy-start | bytes 49156
  107.4 13.0 %copy-start.16 = (f32[64,64]{1,0:T(8,128)}, f32[64,64]{1,0:T(8,128)S(1)}, u32[]{:S(2)}) copy-start(f32[64,64]{1,0:T(8,128)S(1)} %collective-permute-done.14) | copy-start | bytes 49156
  107.4 30.7 %copy-start.1 = (f32[192,768]{1,0:T(8,128)S(1)}, f32[192,768]{1,0:T(8,128)}, u32[]{:S(2)}) copy-start(f32[192,768]{1,0:T(8,128)} %get-tuple-element.64.rest_0_) | copy-start | bytes 1769476
  107.4 15.0 %collective-permute-start.18 = (f32[192,768]{1,0:T(8,128)}, f32[192,768]{1,0:T(8,128)S(1)}, u32[]{:S(2)}, u32[]{:S(2)}) collective-permute-start(f32[192,768]{1,0:T(8,128)} %get-tuple-element.56), channel_id=1, source_target_pairs={{0,4},{1,5},{2,6},{3,7},{4,0},{5,1},{6,2},{7,3},{8,12},{9,13},{10,... | collective-permute-start | bytes 1769480 | tf_op jit(solution)/shard_map/back01/ppermute | solution.py:175
  108.1 14.3 %collective-permute-start.20 = (f32[192,768]{1,0:T(8,128)}, f32[192,768]{1,0:T(8,128)S(1)}, u32[]{:S(2)}, u32[]{:S(2)}) collective-permute-start(f32[192,768]{1,0:T(8,128)} %get-tuple-element.58), channel_id=1, source_target_pairs={{0,12},{1,13},{2,14},{3,15},{4,8},{5,9},{6,10},{7,11},{8,4},{9,5},... | collective-permute-start | bytes 1769480 | tf_op jit(solution)/shard_map/back03/ppermute | solution.py:175
  108.7 1.0 copy-start.19
  109.8 1.1 copy-start.20
  122.4 19.7 %collective-permute-start.23 = (f32[192,768]{1,0:T(8,128)}, f32[192,768]{1,0:T(8,128)S(1)}, u32[]{:S(2)}, u32[]{:S(2)}) collective-permute-start(f32[192,768]{1,0:T(8,128)} %get-tuple-element.63), channel_id=1, source_target_pairs={{0,12},{1,13},{2,14},{3,15},{4,8},{5,9},{6,10},{7,11},{8,4},{9,5},... | collective-permute-start | bytes 1769480 | tf_op jit(solution)/shard_map/back13/ppermute | solution.py:175
  125.0 17.0 %collective-permute-start.22 = (f32[192,768]{1,0:T(8,128)}, f32[192,768]{1,0:T(8,128)S(1)}, u32[]{:S(2)}, u32[]{:S(2)}) collective-permute-start(f32[192,768]{1,0:T(8,128)} %get-tuple-element.61), channel_id=1, source_target_pairs={{0,8},{1,9},{2,10},{3,11},{4,12},{5,13},{6,14},{7,15},{8,0},{9,1},... | collective-permute-start | bytes 1769480 | tf_op jit(solution)/shard_map/back12/ppermute | solution.py:175
  125.9 16.2 %collective-permute-start.21 = (f32[192,768]{1,0:T(8,128)}, f32[192,768]{1,0:T(8,128)}, u32[]{:S(2)}, u32[]{:S(2)}) collective-permute-start(f32[192,768]{1,0:T(8,128)} %get-tuple-element.59), channel_id=1, source_target_pairs={{0,4},{1,5},{2,6},{3,7},{4,0},{5,1},{6,2},{7,3},{8,12},{9,13},{10,... | collective-permute-start | bytes 1769480 | tf_op jit(solution)/shard_map/back11/ppermute | solution.py:175
  127.3 0.6 copy-start.8
  127.3 1.2 copy-start.10
  129.2 1.2 collective-permute-start.17
  130.4 3.6 %collective-permute-start.24 = (f32[8,128]{1,0:T(8,128)S(1)}, f32[8,128]{1,0:T(8,128)S(1)}, u32[]{:S(2)}, u32[]{:S(2)}) collective-permute-start(f32[8,128]{1,0:T(8,128)S(1)} %add.310), channel_id=1, source_target_pairs={{0,32},{1,33},{2,34},{3,35},{4,36},{5,37},{6,38},{7,39},{8,40},{9,... | collective-permute-start | bytes 12296 | tf_op jit(solution)/shard_map/total2/ppermute | solution.py:175
  134.1 6.1 %collective-permute-start.25 = (f32[8,128]{1,0:T(8,128)S(1)}, f32[8,128]{1,0:T(8,128)S(1)}, u32[]{:S(2)}, u32[]{:S(2)}) collective-permute-start(f32[8,128]{1,0:T(8,128)S(1)} %add.311), channel_id=1, source_target_pairs={{0,64},{1,65},{2,66},{3,67},{4,68},{5,69},{6,70},{7,71},{8,72},{9,... | collective-permute-start | bytes 12296 | tf_op jit(solution)/shard_map/total4/ppermute | solution.py:175
  138.1 3.3 %copy-start.9 = (f32[1,64,64]{2,1,0:T(8,128)S(1)}, f32[1,64,64]{2,1,0:T(8,128)}, u32[]{:S(2)}) copy-start(f32[1,64,64]{2,1,0:T(8,128)} %copy-done.8) | copy-start | bytes 49156
  138.1 3.3 %copy-start.11 = (f32[1,64,64]{2,1,0:T(8,128)S(1)}, f32[1,64,64]{2,1,0:T(8,128)}, u32[]{:S(2)}) copy-start(f32[1,64,64]{2,1,0:T(8,128)} %copy-done.10) | copy-start | bytes 49156
  138.1 3.9 %copy-start = (f32[192,768]{1,0:T(8,128)S(1)}, f32[192,768]{1,0:T(8,128)}, u32[]{:S(2)}) copy-start(f32[192,768]{1,0:T(8,128)} %get-tuple-element.54.rest_0_) | copy-start | bytes 1769476
